TPU v7x, 32 devices: a whole 2x2x4 slice. The times are simulated.
32 devices in a mesh: dp: 4 (over y, x), ctx: 8 (over z, core).
Axes of the slice: x: 2, y: 2, z: 4, core: 2. Of those that a mesh axis runs over, the one named last changes fastest.
Arguments:
- signal: bfloat16 [4, 1024, 2048], P('dp', 'ctx'), may hold values from -6 to 6
- gate_input: bfloat16 [4, 1024, 2048], P('dp', 'ctx'), may hold values from -6 to 6
- cotangent: bfloat16 [4, 1024, 2048], P('dp', 'ctx'), may hold values from -6 to 6
- long_filter: float32 [128, 1024], P('ctx'), may hold values from -0.1875 to 0.1875
- short_taps: bfloat16 [128, 2048], replicated, may hold values from -0.5 to 0.5
- skip_gain: float32 [2048], P('ctx'), may hold values from -4 to 4
Outputs:
- output: bfloat16 [4, 1024, 2048], P('dp', 'ctx')
- gate_grad: bfloat16 [4, 1024, 2048], P('dp', 'ctx')
- signal_grad: bfloat16 [4, 1024, 2048], P('dp', 'ctx')
- long_grad: float32 [128, 1024], P('ctx')
- taps_grad: float32 [128, 2048], P(None, 'ctx')
- skip_grad: float32 [2048], P('ctx')
All inputs are finite; a program needn't handle non-finite values.
Results may differ from a plain program's by a relative error of at most 0.0058.
Values may be sent and summed in bfloat16 or wider, within the bound.
No kernel may reach another device: no remote copies, remote signals or barrier semaphores. Data moves between devices by JAX's collectives and lax.ppermute only.
A program may use at most 64 MiB of HBM per device.

v0:
```python
import math

import jax
import jax.numpy as jnp
from jax import lax
from jax.sharding import PartitionSpec as P

HIGH = lax.Precision.HIGHEST


def shifted(array, axis, by):
    devices = lax.axis_size(axis)
    pairs = [(i, i + by) for i in range(devices) if 0 <= i + by < devices]
    return lax.ppermute(array, axis, pairs)


def angle_table(row_count, col_count, modulus):
    row_index = lax.iota(jnp.int32, row_count)[:, None]
    col_index = lax.iota(jnp.int32, col_count)[None, :]
    phase = (row_index * col_index % modulus).astype(jnp.float32) * (2.0 * math.pi / modulus)
    return (jnp.cos(phase), jnp.sin(phase))


def rotation(cos_part, sin_part, sign):
    upper = jnp.concatenate([cos_part, sign * sin_part], axis=1)
    lower = jnp.concatenate([-sign * sin_part, cos_part], axis=1)
    return jnp.concatenate([upper, lower], axis=0)


def lead_product(table, data):
    return lax.dot_general(table, data, (((0,), (0,)), ((), ())), precision=HIGH)


def tail_product(data, table):
    return lax.dot_general(data, table, (((2,), (0,)), ((), ())), precision=HIGH)


def forward_table(half_outer, outer_size, packed):
    cos_outer, sin_outer = angle_table(half_outer, outer_size, outer_size)
    real_rows = jnp.concatenate([cos_outer, -sin_outer], axis=1)
    if not packed:
        return real_rows
    imag_rows = jnp.concatenate([sin_outer, cos_outer], axis=1)
    return jnp.stack([real_rows, imag_rows], axis=1).reshape(2 * half_outer, 2 * outer_size)


def forward_dft(data, table, outer_size, inner_size):
    section = lead_product(table, data)
    width = section.shape[1]
    section_re = section[:outer_size]
    section_im = section[outer_size:]
    cos_twist, sin_twist = angle_table(outer_size, inner_size, outer_size * inner_size)
    cos_twist = cos_twist[:, None, :]
    sin_twist = sin_twist[:, None, :]
    twist_re = section_re * cos_twist + section_im * sin_twist
    twist_im = section_im * cos_twist - section_re * sin_twist
    twisted = jnp.stack([twist_re, twist_im], axis=2).reshape(outer_size, width, 2 * inner_size)
    cos_inner, sin_inner = angle_table(inner_size, inner_size, inner_size)
    return tail_product(twisted, rotation(cos_inner, sin_inner, -1.0))


def inverse_dft(spec, table, outer_size, inner_size):
    cos_inner, sin_inner = angle_table(inner_size, inner_size, inner_size)
    section = tail_product(spec, rotation(cos_inner, sin_inner, 1.0))
    section_re = section[:, :, :inner_size]
    section_im = section[:, :, inner_size:]
    cos_twist, sin_twist = angle_table(outer_size, inner_size, outer_size * inner_size)
    cos_twist = cos_twist[:, None, :]
    sin_twist = sin_twist[:, None, :]
    twist_re = section_re * cos_twist - section_im * sin_twist
    twist_im = section_im * cos_twist + section_re * sin_twist
    joined = jnp.concatenate([twist_re, twist_im], axis=0)
    return lead_product(table, joined) * (1.0 / (outer_size * inner_size))


def mirror_index(spec):
    turned = jnp.roll(jnp.flip(spec, (0, 2)), 1, axis=0)
    first_row = jnp.roll(turned[:1], 1, axis=2)
    return jnp.concatenate([first_row, turned[1:]], axis=0)


def long_section(pairs_in, long_filter, skip_gain):
    half_outer = pairs_in.shape[0]
    chan_count = pairs_in.shape[2]
    inner_size = pairs_in.shape[3]
    outer_size = 2 * half_outer
    group_count = long_filter.shape[0]
    group_size = chan_count // group_count
    pairs = pairs_in.astype(jnp.float32)
    mixed_f = pairs[:, 0]
    grad_f = pairs[:, 1]
    packed = forward_dft(
        pairs.reshape(2 * half_outer, chan_count, inner_size),
        forward_table(half_outer, outer_size, True),
        outer_size,
        inner_size,
    )
    filter_time = jnp.transpose(long_filter.reshape(group_count, half_outer, inner_size), (1, 0, 2))
    filt = forward_dft(
        filter_time, forward_table(half_outer, outer_size, False), outer_size, inner_size
    )
    packed_re = packed[:, :, :inner_size]
    packed_im = packed[:, :, inner_size:]
    mirror_re = mirror_index(packed_re)
    mirror_im = mirror_index(packed_im)
    grouped = (outer_size, group_count, group_size, inner_size)
    sig_re = (0.5 * (packed_re + mirror_re)).reshape(grouped)
    sig_im = (0.5 * (packed_im - mirror_im)).reshape(grouped)
    grad_re = (0.5 * (packed_im + mirror_im)).reshape(grouped)
    grad_im = (0.5 * (mirror_re - packed_re)).reshape(grouped)
    filt_re = filt[:, :, None, :inner_size]
    filt_im = filt[:, :, None, inner_size:]
    joint_re = sig_re * filt_re - sig_im * filt_im - (grad_im * filt_re - grad_re * filt_im)
    joint_im = sig_re * filt_im + sig_im * filt_re + grad_re * filt_re + grad_im * filt_im
    joint = jnp.concatenate([joint_re, joint_im], axis=3).reshape(
        outer_size, chan_count, 2 * inner_size
    )
    lag_re = jnp.sum(grad_re * sig_re + grad_im * sig_im, axis=2)
    lag_im = jnp.sum(grad_im * sig_re - grad_re * sig_im, axis=2)
    lag_spec = jnp.concatenate([lag_re, lag_im], axis=2)
    cos_outer, sin_outer = angle_table(outer_size, half_outer, outer_size)
    timed = inverse_dft(joint, rotation(cos_outer, sin_outer, 1.0), outer_size, inner_size)
    lag_time = inverse_dft(
        lag_spec, jnp.concatenate([cos_outer, -sin_outer], axis=0), outer_size, inner_size
    )
    lag_part = jnp.transpose(lag_time, (1, 0, 2)).reshape(group_count, half_outer * inner_size)
    gains = skip_gain[None, :, None]
    conv_ch = (timed[:half_outer] + gains * mixed_f).astype(jnp.bfloat16)
    back_ch = (timed[half_outer:] + gains * grad_f).astype(jnp.bfloat16)
    skip_part = jnp.sum(grad_f * mixed_f, axis=(0, 2))
    return (conv_ch, back_ch, lag_part, skip_part)


def to_blocks(rows_first, rows_second, ctx_count):
    row_count, chan_total = rows_first.shape
    stacked = jnp.stack([rows_first, rows_second], axis=0)
    stacked = stacked.reshape(2, row_count, ctx_count, chan_total // ctx_count)
    return jnp.transpose(stacked, (2, 0, 3, 1))


def to_rows(blocks, which):
    picked = blocks[:, which]
    return picked.reshape(-1, picked.shape[2]).T


def taps_time(extended, kernel):
    chan_count = extended.shape[1]
    return lax.conv_general_dilated(
        extended[None],
        kernel[:, None, :],
        (1,),
        "VALID",
        dimension_numbers=("NHC", "HIO", "NHC"),
        feature_group_count=chan_count,
        preferred_element_type=jnp.float32,
    )[0]


def local(signal, gate_input, cotangent, long_filter, short_taps, skip_gain):
    series = signal[0]
    gating = gate_input[0]
    upstream = cotangent[0]
    row_count = series.shape[0]
    tap_count = short_taps.shape[0]
    ctx_count = lax.axis_size("ctx")
    seq_length = row_count * ctx_count
    grad_gate = (upstream.astype(jnp.float32) * gating.astype(jnp.float32)).astype(jnp.bfloat16)
    earlier = shifted(series[row_count - (tap_count - 1) :], "ctx", 1)
    extended = jnp.concatenate([earlier, series], axis=0)
    mixed_rows = taps_time(extended, short_taps[::-1]).astype(jnp.bfloat16)
    received = lax.all_to_all(
        to_blocks(mixed_rows, grad_gate, ctx_count), "ctx", split_axis=0, concat_axis=0, tiled=True
    )
    conv_ch, back_ch, lag_grad, skip_part = long_section(received, long_filter, skip_gain)
    returned = lax.all_to_all(
        jnp.stack([conv_ch, back_ch], axis=1), "ctx", split_axis=0, concat_axis=0, tiled=True
    )
    conv_rows = to_rows(returned, 0)
    back_rows = to_rows(returned, 1)
    later_rows = shifted(back_rows[: tap_count - 1], "ctx", -1)
    signal_part = taps_time(jnp.concatenate([back_rows, later_rows], axis=0), short_taps).astype(
        jnp.bfloat16
    )
    tap_full = taps_time(extended, back_rows)[::-1]
    tap_part = lax.psum_scatter(tap_full, "ctx", scatter_dimension=1, tiled=True)
    conv_f = conv_rows.astype(jnp.float32)
    output = (gating.astype(jnp.float32) * conv_f).astype(jnp.bfloat16)
    gate_grad = (upstream.astype(jnp.float32) * conv_f).astype(jnp.bfloat16)
    lag_total, tap_total, skip_total = lax.psum((lag_grad, tap_part, skip_part), "dp")
    factor = 1.0 / math.sqrt(lax.axis_size("dp") * seq_length)
    return (
        output[None],
        gate_grad[None],
        signal_part[None],
        lag_total * factor,
        tap_total * factor,
        skip_total * factor,
    )


def solution(mesh):
    return jax.shard_map(
        local,
        mesh=mesh,
        in_specs=(
            P("dp", "ctx", None),
            P("dp", "ctx", None),
            P("dp", "ctx", None),
            P("ctx", None),
            P(),
            P("ctx"),
        ),
        out_specs=(
            P("dp", "ctx", None),
            P("dp", "ctx", None),
            P("dp", "ctx", None),
            P("ctx", None),
            P(None, "ctx"),
            P("ctx"),
        ),
        check_vma=False,
    )
```

profile of v0, /device:TPU:0, one launch (start us, length us, event | category | flops | bytes accessed | tf_op | source)
XLA Modules:
  0.0 287.2 jit_solution(10507562309490665121)
XLA Ops:
  7.2 1.3 slice_bitcast_fusion.2
  8.5 3.2 %collective-permute-start = (bf16[127,2048]{1,0:T(8,128)(2,1)S(1)}, bf16[127,2048]{1,0:T(8,128)(2,1)}, u32[]{:S(2)}, u32[]{:S(2)}) collective-permute-start(bf16[127,2048]{1,0:T(8,128)(2,1)S(1)} %slice_bitcast_fusion.2), channel_id=1, source_target_pairs={{0,1},{1,2},{2,3},{3,4},{4,5},{5,6},{6,7},{8,9},{9,10},{10,11},{11... | collective-permute-start | bytes 1560584 | tf_op jit(solution)/shard_map/ppermute | solution.py:14
  11.7 1.3 copy.106
  13.4 5.1 %rev.9 = bf16[128,2048]{1,0:T(8,128)(2,1)} reverse(bf16[128,2048]{1,0:T(8,128)(2,1)S(1)} %copy-done.14), dimensions={0} | reverse | bytes 1048576 | tf_op jit(solution)/shard_map/rev | solution.py:170
  18.7 1.2 maximum_bitcast_fusion
  19.9 1.0 copy-done.12
  20.9 14.8 %convolution_convert_fusion.1 = bf16[1,128,2048]{2,0,1:T(2,128)(2,1)S(1)} fusion(bf16[1,255,2048]{2,1,0:T(8,128)(2,1)S(1)} %maximum_bitcast_fusion, bf16[128,1,2048]{2,0,1:T(8,128)(2,1)S(1)} %bitcast.151), kind=kOutput, calls=%fused_computation.7 | convolution fusion | flops 67371008 | bytes 2093056 | tf_op jit(solution)/shard_map/conv_general_dilated | solution.py:148
  36.7 2.1 copy.111
  38.7 6.7 %all-to-all-start = ((bf16[8,2,256,128]{3,1,2,0:T(2,128)(2,1)}), bf16[8,2,256,128]{3,1,2,0:T(2,128)(2,1)S(1)}, u32[]{:S(2)}, u32[]{:S(2)}) async-start(bf16[8,2,256,128]{3,1,2,0:T(2,128)(2,1)} %copy.111), calls=%async_computation | async-start | bytes 2097152 | tf_op jit(solution)/shard_map/all_to_all | solution.py:171
  47.7 2.0 copy.117
  49.9 1.9 copy.118
  52.0 20.0 %all-to-all-done = bf16[8,2,256,128]{3,1,2,0:T(2,128)(2,1)S(1)} async-done(((bf16[8,2,256,128]{3,1,2,0:T(2,128)(2,1)}), bf16[8,2,256,128]{3,1,2,0:T(2,128)(2,1)S(1)}, u32[]{:S(2)}, u32[]{:S(2)}) %all-to-all-start) | async-done | bytes 1048608 | tf_op jit(solution)/shard_map/all_to_all | solution.py:171
  72.0 1.9 convolution_bitcast_fusion
  74.4 2.2 pad_maximum_fusion
  76.6 5.3 %copy.113 = f32[16,256,2,128]{1,3,2,0:T(8,128)} copy(f32[16,256,2,128]{3,0,1,2:T(8,128)} %pad_maximum_fusion) | data formatting | bytes 8388608 | tf_op jit(solution)/shard_map/stack | solution.py:57
  81.9 5.7 %fusion.38 = f32[16,256,256]{1,2,0:T(8,128)S(1)} fusion(f32[16,256,256]{1,2,0:T(8,128)} %bitcast.140, f32[128,128]{0,1:T(8,128)S(1)} %fusion.49, f32[128,128]{0,1:T(8,128)S(1)} %get-tuple-element.70, f32[128,128]{0,1:T(8,128)S(1)} %get-tuple-element.69), kind=kOutput, calls=%fused_computation.77 | convolution fusion | flops 3221422080 | bytes 8585216 | tf_op jit(solution)/shard_map/dot_general | solution.py:35
  87.6 1.7 fusion.98
  89.3 0.9 fusion.97
  90.2 15.7 %slice.124 = f32[15,256,128]{1,2,0:T(8,128)} reverse(f32[15,256,128]{1,2,0:T(8,128)} %get-tuple-element.51), dimensions={0,2} | reverse | bytes 3932160 | tf_op jit(solution)/shard_map/jit(_roll_static)/slice | solution.py:77
  105.9 9.7 %slice.133 = f32[15,256,128]{1,2,0:T(8,128)} reverse(f32[15,256,128]{1,2,0:T(8,128)S(1)} %get-tuple-element.50), dimensions={0,2} | reverse | bytes 3932160 | tf_op jit(solution)/shard_map/jit(_roll_static)/slice | solution.py:77
  115.6 0.9 slice.122
  117.2 4.2 %multiply_add_fusion = (f32[16,256,128]{1,2,0:T(8,128)S(1)}, f32[16,256,128]{1,2,0:T(8,128)S(1)}, f32[16,256,128]{1,2,0:T(8,128)S(1)}, f32[16,256,128]{1,2,0:T(8,128)S(1)}, f32[16,256,128]{1,2,0:T(8,128)S(1)}) fusion(f32[15,256,128]{1,2,0:T(8,128)} %slice.124, f32[1,256,127]{1,2,0:T(8,128)S(1)} %slice.122, f32[1,256,1]{1,2,0:T(1,128)S(1)} %get-tuple-element.47, ...), kind=kLoop, calls=%fused_computation.14 | loop fusion | flops 7864320 | bytes 18874368 | tf_op jit(solution)/shard_map/add | solution.py:118
  121.9 2.4 subtract_subtract_fusion
  124.3 2.2 pad_maximum_fusion.1
  126.5 5.6 %copy.150 = f32[16,256,256]{2,0,1:T(8,128)} copy(f32[16,256,256]{1,2,0:T(8,128)} %pad_maximum_fusion.1) | data formatting | bytes 8388608 | tf_op jit(solution)/shard_map/concatenate | solution.py:115
  132.1 5.6 %fusion.34 = f32[16,256,256]{2,0,1:T(8,128)S(1)} fusion(f32[16,256,256]{2,0,1:T(8,128)} %copy.150, f32[128,128]{0,1:T(8,128)S(1)} %fusion.49, f32[128,128]{0,1:T(8,128)S(1)} %get-tuple-element.69, f32[128,128]{0,1:T(8,128)S(1)} %get-tuple-element.70), kind=kOutput, calls=%fused_computation.75 | convolution fusion | flops 3221422080 | bytes 8585216 | tf_op jit(solution)/shard_map/dot_general | solution.py:35
  138.1 2.2 fusion.4
  141.0 1.1 fusion.20
  142.4 29.0 %all_to_all.10 = bf16[8,2,256,128]{3,2,1,0:T(8,128)(2,1)S(1)} all-to-all(bf16[8,2,256,128]{3,2,1,0:T(8,128)(2,1)S(1)} %copy.130), channel_id=1, replica_groups=mesh['dp'=4,'ctx'=8] {'ctx'}, dimensions={0} | all-to-all | bytes 2097152 | tf_op jit(solution)/shard_map/all_to_all | solution.py:175
  171.4 0.9 fusion.99
  172.3 2.1 copy.143
  174.3 16.4 %fusion.7 = f32[1,128,2048]{2,0,1:T(1,128)S(1)} fusion(bf16[128,1,2048]{2,1,0:T(2,128)(2,1)} %copy.143, bf16[1,255,2048]{2,1,0:T(8,128)(2,1)} %copy-done.12), kind=kOutput, calls=%fused_computation.26 | convolution fusion | flops 67108864 | bytes 2617344 | tf_op jit(solution)/shard_map/conv_general_dilated | solution.py:148
  190.8 1.3 copy.184
  192.1 8.9 %rev.10 = f32[128,2048]{1,0:T(8,128)} reverse(f32[128,2048]{1,0:T(8,128)} %bitcast.146), dimensions={0} | reverse | bytes 2097152 | tf_op jit(solution)/shard_map/rev | solution.py:184
  201.2 2.9 %copy.137 = f32[16,256,128]{2,1,0:T(8,128)} copy(f32[16,256,128]{1,2,0:T(8,128)} %get-tuple-element.39) | data formatting | bytes 4194304 | tf_op jit(solution)/shard_map/sub | solution.py:119
  204.1 1.8 copy.136
  205.9 10.0 %psum.23 = f32[256]{0:T(256)S(1)} all-reduce(f32[256]{0:T(256)S(1)} %get-tuple-element.52), channel_id=1, replica_groups=mesh['dp'=4,'ctx'=8] {'dp'}, use_global_device_ids=true, to_apply=%region_6.7 | all-reduce | flops 256 | bytes 2048 | tf_op jit(solution)/shard_map/psum | solution.py:189
  215.9 1.9 bitcast_reduce_fusion
  219.4 1.3 collective-permute-start.1
  221.9 1.0 copy.144
  222.9 1.0 copy.145
  224.1 2.1 copy.134
  226.3 6.3 %reduce-scatter.2.cloned.1.call-done = f32[128,256]{1,0:T(8,128)} async-done(((f32[128,2048]{1,0:T(8,128)}), f32[128,256]{1,0:T(8,128)}) %reduce-scatter.2.cloned.1.call-update) | async-done | bytes 131088 | tf_op jit(solution)/shard_map/reduce_scatter | solution.py:185
  232.6 16.8 %convolution_convert_fusion = bf16[1,128,2048]{2,0,1:T(2,128)(2,1)S(1)} fusion(bf16[1,255,2048]{2,0,1:T(2,128)(2,1)S(1)} %copy.134, bf16[128,1,2048]{2,0,1:T(8,128)(2,1)} %bitcast.150), kind=kOutput, calls=%fused_computation.6 | convolution fusion | flops 67371008 | bytes 2093056 | tf_op jit(solution)/shard_map/conv_general_dilated | solution.py:148
  249.4 1.1 copy.146
  250.5 26.9 %all-reduce.3.cloned.1.call-done = (f32[16,1024]{1,0:T(8,128)}, f32[128,256]{1,0:T(8,128)}) async-done(((f32[16,1024]{1,0:T(8,128)}, f32[128,256]{1,0:T(8,128)}), (f32[16,1024]{1,0:T(8,128)}, f32[128,256]{1,0:T(8,128)})) %all-reduce.3.cloned.1.call-update) | async-done | bytes 196624 | tf_op jit(solution)/shard_map/psum | solution.py:189
  277.3 1.6 broadcast_multiply_fusion
  278.9 1.5 broadcast_multiply_fusion.1
  (80 shorter events, 10.1 us)
Async XLA Ops:
  7.2 5.9 %copy-start.13 = (bf16[1,128,2048]{2,1,0:T(8,128)(2,1)S(1)}, bf16[1,128,2048]{2,1,0:T(8,128)(2,1)}, u32[]{:S(2)}) copy-start(bf16[1,128,2048]{2,1,0:T(8,128)(2,1)} %param.8) | copy-start | bytes 1572868
  7.2 6.2 %copy-start.14 = (bf16[128,2048]{1,0:T(8,128)(2,1)S(1)}, bf16[128,2048]{1,0:T(8,128)(2,1)}, u32[]{:S(2)}) copy-start(bf16[128,2048]{1,0:T(8,128)(2,1)} %param.10) | copy-start | bytes 1572868
  7.2 11.3 %copy-start.16 = (f32[16,1024]{1,0:T(8,128)S(1)}, f32[16,1024]{1,0:T(8,128)}, u32[]{:S(2)}) copy-start(f32[16,1024]{1,0:T(8,128)} %param.9) | copy-start | bytes 196612
  8.5 10.2 %collective-permute-start = (bf16[127,2048]{1,0:T(8,128)(2,1)S(1)}, bf16[127,2048]{1,0:T(8,128)(2,1)}, u32[]{:S(2)}, u32[]{:S(2)}) collective-permute-start(bf16[127,2048]{1,0:T(8,128)(2,1)S(1)} %slice_bitcast_fusion.2), channel_id=1, source_target_pairs={{0,1},{1,2},{2,3},{3,4},{4,5},{5,6},{6,7},{8,9},{9,10},{10,11},{11... | collective-permute-start | bytes 1560584 | tf_op jit(solution)/shard_map/ppermute | solution.py:14
  13.0 6.9 %copy-start.4 = (bf16[1,128,2048]{1,2,0:T(8,128)(2,1)}, bf16[1,128,2048]{1,2,0:T(8,128)(2,1)S(1)}, u32[]{:S(2)}) copy-start(bf16[1,128,2048]{1,2,0:T(8,128)(2,1)S(1)} %copy.106) | copy-start | bytes 1572868
  13.0 5.6 %copy-start.11 = (bf16[1,128,2048]{2,1,0:T(8,128)(2,1)S(1)}, bf16[1,128,2048]{2,1,0:T(8,128)(2,1)}, u32[]{:S(2)}) copy-start(bf16[1,128,2048]{2,1,0:T(8,128)(2,1)} %param.6) | copy-start | bytes 1572868
  13.3 6.6 %copy-start.6 = (bf16[1,128,2048]{1,2,0:T(8,128)(2,1)}, bf16[1,128,2048]{1,2,0:T(8,128)(2,1)S(1)}, u32[]{:S(2)}) copy-start(bf16[1,128,2048]{1,2,0:T(8,128)(2,1)S(1)} %copy.110) | copy-start | bytes 1572868
  18.5 2.4 copy-start.15
  19.9 1.0 copy-start.12
  38.7 33.3 %all-to-all-start = ((bf16[8,2,256,128]{3,1,2,0:T(2,128)(2,1)}), bf16[8,2,256,128]{3,1,2,0:T(2,128)(2,1)S(1)}, u32[]{:S(2)}, u32[]{:S(2)}) async-start(bf16[8,2,256,128]{3,1,2,0:T(2,128)(2,1)} %copy.111), calls=%async_computation | async-start | bytes 2097152 | tf_op jit(solution)/shard_map/all_to_all | solution.py:171
  45.4 187.1 %reduce-scatter.2.cloned.1.call-start = ((), (), s32[]{:S(2)}) async-start(), calls=%async_computation.3 | async-start | bytes 1179648 | tf_op jit(solution)/shard_map/reduce_scatter | solution.py:185
  87.6 2.6 copy-start
  117.2 4.2 %copy-start.1 = (f32[16,256,128]{1,2,0:T(8,128)S(1)}, f32[16,256,128]{1,2,0:T(8,128)}, u32[]{:S(2)}) copy-start(f32[16,256,128]{1,2,0:T(8,128)} %copy.117) | copy-start | bytes 6291460
  117.2 4.7 %copy-start.2 = (f32[16,256,128]{1,2,0:T(8,128)S(1)}, f32[16,256,128]{1,2,0:T(8,128)}, u32[]{:S(2)}) copy-start(f32[16,256,128]{1,2,0:T(8,128)} %copy.118) | copy-start | bytes 6291460
  140.3 0.7 copy-start.17
  172.3 18.5 %copy-start.8 = (bf16[8,1,256,128]{3,2,1,0:T(8,128)(2,1)}, bf16[8,1,256,128]{3,2,1,0:T(8,128)(2,1)S(1)}, u32[]{:S(2)}) copy-start(bf16[8,1,256,128]{3,2,1,0:T(8,128)(2,1)S(1)} %get-tuple-element.53) | copy-start | bytes 1572868
  201.1 76.3 %all-reduce.3.cloned.1.call-start = ((), (), s32[]{:S(2)}) async-start(), calls=%async_computation.4 | async-start | bytes 393216 | tf_op jit(solution)/shard_map/psum | solution.py:189
  205.9 11.9 %copy-start.3 = (f32[16,256,128]{2,1,0:T(8,128)S(1)}, f32[16,256,128]{2,1,0:T(8,128)}, u32[]{:S(2)}) copy-start(f32[16,256,128]{2,1,0:T(8,128)} %copy.136) | copy-start | bytes 6291460
  217.8 1.5 copy-start.9
  217.8 3.8 %copy-start.5 = (bf16[1,128,2048]{1,2,0:T(8,128)(2,1)S(1)}, bf16[1,128,2048]{1,2,0:T(8,128)(2,1)}, u32[]{:S(2)}) copy-start(bf16[1,128,2048]{1,2,0:T(8,128)(2,1)} %copy-done.4) | copy-start | bytes 1572868
  217.8 3.8 %copy-start.7 = (bf16[1,128,2048]{1,2,0:T(8,128)(2,1)S(1)}, bf16[1,128,2048]{1,2,0:T(8,128)(2,1)}, u32[]{:S(2)}) copy-start(bf16[1,128,2048]{1,2,0:T(8,128)(2,1)} %copy-done.6) | copy-start | bytes 1572868
  217.9 3.8 %copy-start.10 = (bf16[8,1,256,128]{3,2,1,0:T(8,128)(2,1)S(1)}, bf16[8,1,256,128]{3,2,1,0:T(8,128)(2,1)}, u32[]{:S(2)}) copy-start(bf16[8,1,256,128]{3,2,1,0:T(8,128)(2,1)} %get-tuple-element.54) | copy-start | bytes 1572868
  219.4 4.6 %collective-permute-start.1 = (bf16[127,2048]{0,1:T(8,128)(2,1)S(1)}, bf16[127,2048]{0,1:T(8,128)(2,1)S(1)}, u32[]{:S(2)}, u32[]{:S(2)}) collective-permute-start(bf16[127,2048]{0,1:T(8,128)(2,1)S(1)} %bitcast.144), channel_id=1, source_target_pairs={{1,0},{2,1},{3,2},{4,3},{5,4},{6,5},{7,6},{9,8},{10,9},{11,10},{12... | collective-permute-start | bytes 1560584 | tf_op jit(solution)/shard_map/ppermute | solution.py:14
Sparse Core Ops, SparseCore 0:
  201.2 31.3 reduce-scatter.1
  236.0 41.2 all-reduce.2
where the time goes:
time: 290 us; the launch traced here: 287 us
  local copies, waits for them, and re-layouts  81.7 us (28%)
  matrix products  65.1 us (22%)
  waiting for transfers between devices  53.2 us (18%)
  blocking collectives  39 us (13%)
  other arithmetic  22.4 us (8%)
  between operations  14.6 us (5%)
  starting transfers between devices  11.3 us (4%)
    conv_general_dilated x3, matrix products, taps_time(): lax.conv_general_dilated(extended[None], kernel[:, None, :], (1,), 'VALID...  48 us
    all_to_all x1, blocking collectives, local(): lax.all_to_all(jnp.stack([conv_ch, back_ch], axis=1), 'ctx', split_axis=0...  29 us
    slice x3, local copies, waits for them, and re-layouts, mirror_index(): turned = jnp.roll(jnp.flip(spec, (0, 2)), 1, axis=0)  27.1 us
    psum x1, waiting for transfers between devices, local(): lax.psum((lag_grad, tap_part, skip_part), 'dp')  26.9 us
    all_to_all x1, waiting for transfers between devices, local(): lax.all_to_all(to_blocks(mixed_rows, grad_gate, ctx_count), 'ctx', split_...  20 us
    dot_general x4, matrix products, tail_product(): lax.dot_general(data, table, (((2,), (0,)), ((), ())), precision=HIGH)  12.2 us
    psum x1, blocking collectives, local(): lax.psum((lag_grad, tap_part, skip_part), 'dp')  10 us
    rev x1, local copies, waits for them, and re-layouts, local(): tap_full = taps_time(extended, back_rows)[::-1]  8.92 us
  transfers between devices with their start and end apart: 5, of which 3 were waited for; matrix products, arithmetic and copies ran while one was open for 16% of the time, Pallas kernels for 0%

commit v1 on v0

v1 whole, which is shorter than its diff:
```python
import functools
import math

import jax
import jax.numpy as jnp
import ml_dtypes
import numpy as np
from jax import lax
from jax.experimental import pallas as pl
from jax.experimental.pallas import tpu as pltpu
from jax.sharding import PartitionSpec as P

BF16 = jnp.bfloat16
F32 = jnp.float32
VMEM = pl.BlockSpec(memory_space=pltpu.VMEM)
SMEM = pl.BlockSpec(memory_space=pltpu.SMEM)
CHUNK = 32


def split_table(table):
    high = table.astype(ml_dtypes.bfloat16)
    low = (table - high.astype(np.float64)).astype(ml_dtypes.bfloat16)
    return high, low


def dft_tables(block):
    size = 2 * block
    steps = ((2 * np.arange(block)[:, None] + 1) * np.arange(block)[None, :]) % (2 * size)
    angle = steps * (math.pi / size)
    table = np.concatenate([np.cos(angle), -np.sin(angle)], axis=0)
    return split_table(table) + split_table(table.T * (2.0 / size))


def mm(a, b):
    return jnp.dot(a, b, preferred_element_type=F32)


def mm_nt(a, b):
    return lax.dot_general(a, b, (((1,), (1,)), ((), ())), preferred_element_type=F32)


def split(x):
    high = x.astype(BF16)
    return high, (x - high.astype(F32)).astype(BF16)


def inverse(rows_high, rows_low, high, low):
    return mm(rows_high, high) + mm(rows_low, high) + mm(rows_high, low)


def parity(width):
    row = lax.broadcasted_iota(jnp.int32, (CHUNK, width), 0)
    return (1 - 2 * (row % 2)).astype(F32)


def chunks(block, body):
    def step(index, carry):
        body(pl.multiple_of(index * CHUNK, CHUNK))
        return carry

    lax.fori_loop(0, block // CHUNK, step, 0)


def gather_blocks(me_ref, blocks, whole):
    rows = blocks[0].shape[0]
    count = len(blocks)
    for shift, ref in enumerate(blocks):
        source = lax.rem(me_ref[0] + (count - shift), count)
        whole[pl.ds(pl.multiple_of(source * rows, rows), rows), :] = ref[...]


def scatter_blocks(me_ref, whole, blocks):
    rows = blocks[0].shape[0]
    count = len(blocks)
    for shift, ref in enumerate(blocks):
        target = lax.rem(me_ref[0] + shift, count)
        ref[...] = whole[pl.ds(pl.multiple_of(target * rows, rows), rows), :]


def filters_kernel(taps, long_high, long_low, gain, fwd_high, fwd_low, taps_spec, long_spec):
    parts, size, width = long_spec.shape
    block = size // 2
    tap_count = taps.shape[0]
    taps_spec[...] = mm(fwd_high[:, :tap_count], taps[...]) + mm(fwd_low[:, :tap_count], taps[...])
    for d in range(parts):
        rows = pl.ds(d * block, block)
        long_spec[d] = inverse(fwd_high[...], fwd_low[...], long_high[rows, :], long_low[rows, :])
    sign = parity(width)

    def body(at):
        re, im = pl.ds(at, CHUNK), pl.ds(block + at, CHUNK)
        for d in reversed(range(1, parts)):
            long_spec[d, re, :] = long_spec[d, re, :] - sign * long_spec[d - 1, im, :]
            long_spec[d, im, :] = long_spec[d, im, :] + sign * long_spec[d - 1, re, :]
        long_spec[0, re, :] = long_spec[0, re, :] + gain[...]

    chunks(block, body)


def conv_kernel(count, *refs):
    me_ref, blocks, refs = refs[0], refs[1 : 1 + count], refs[1 + count :]
    fwd_high, fwd_low, inv_high, inv_low, taps_spec, long_spec = refs[:6]
    outs, refs = refs[6 : 6 + count], refs[6 + count :]
    near_spec, mixed_spec, whole, series_spec, high, low = refs
    parts, size, width = long_spec.shape
    block = size // 2
    sign = parity(width)
    gather_blocks(me_ref, blocks, whole)
    for i in range(parts):
        x = whole[pl.ds(i * block, block), :]
        series_spec[i] = mm(fwd_high[...], x) + mm(fwd_low[...], x)

    def near(at):
        re, im = pl.ds(at, CHUNK), pl.ds(block + at, CHUNK)
        w_re, w_im = taps_spec[re, :], taps_spec[im, :]
        for i in range(parts):
            s_re, s_im = series_spec[i, re, :], series_spec[i, im, :]
            if i:
                s_re = s_re - sign * series_spec[i - 1, im, :]
                s_im = s_im + sign * series_spec[i - 1, re, :]
            near_spec[i, re, :] = s_re
            near_spec[i, im, :] = s_im
            high[i, re, :], low[i, re, :] = split(w_re * s_re - w_im * s_im)
            high[i, im, :], low[i, im, :] = split(w_re * s_im + w_im * s_re)

    chunks(block, near)
    for i in range(parts):
        x = inverse(inv_high[...], inv_low[...], high[i], low[i]).astype(BF16)
        mixed_spec[i] = mm(fwd_high[...], x) + mm(fwd_low[...], x)

    def far(at):
        re, im = pl.ds(at, CHUNK), pl.ds(block + at, CHUNK)
        for i in range(parts):
            sum_re = sum_im = 0.0
            for d in range(i + 1):
                c_re, c_im = long_spec[d, re, :], long_spec[d, im, :]
                x_re, x_im = mixed_spec[i - d, re, :], mixed_spec[i - d, im, :]
                sum_re = sum_re + (c_re * x_re - c_im * x_im)
                sum_im = sum_im + (c_re * x_im + c_im * x_re)
            high[i, re, :], low[i, re, :] = split(sum_re)
            high[i, im, :], low[i, im, :] = split(sum_im)

    chunks(block, far)
    for i in range(parts):
        whole[pl.ds(i * block, block), :] = inverse(
            inv_high[...], inv_low[...], high[i], low[i]
        ).astype(BF16)
    scatter_blocks(me_ref, whole, outs)


def back_kernel(count, *refs):
    me_ref, blocks, refs = refs[0], refs[1 : 1 + count], refs[1 + count :]
    fwd_high, fwd_low, inv_high, inv_low, taps_spec, long_spec = refs[:6]
    outs, refs = refs[6 : 6 + count], refs[6 + count :]
    grad_spec, back_spec, whole, high, low = refs
    parts, size, width = long_spec.shape
    block = size // 2
    sign = parity(width)
    gather_blocks(me_ref, blocks, whole)
    for i in range(parts):
        x = whole[pl.ds(i * block, block), :]
        grad_spec[i] = mm(fwd_high[...], x) + mm(fwd_low[...], x)

    def far(at):
        re, im = pl.ds(at, CHUNK), pl.ds(block + at, CHUNK)
        for i in range(parts):
            sum_re = sum_im = 0.0
            for d in range(parts - i):
                c_re, c_im = long_spec[d, re, :], long_spec[d, im, :]
                g_re, g_im = grad_spec[i + d, re, :], grad_spec[i + d, im, :]
                sum_re = sum_re + (c_re * g_re + c_im * g_im)
                sum_im = sum_im + (c_re * g_im - c_im * g_re)
            high[i, re, :], low[i, re, :] = split(sum_re)
            high[i, im, :], low[i, im, :] = split(sum_im)

    chunks(block, far)
    for i in range(parts):
        x = inverse(inv_high[...], inv_low[...], high[i], low[i]).astype(BF16)
        back_spec[i] = mm(fwd_high[...], x) + mm(fwd_low[...], x)

    def near(at):
        re, im = pl.ds(at, CHUNK), pl.ds(block + at, CHUNK)
        w_re, w_im = taps_spec[re, :], taps_spec[im, :]
        for i in range(parts):
            b_re, b_im = back_spec[i, re, :], back_spec[i, im, :]
            if i + 1 < parts:
                b_re = b_re + sign * back_spec[i + 1, im, :]
                b_im = b_im - sign * back_spec[i + 1, re, :]
            high[i, re, :], low[i, re, :] = split(w_re * b_re + w_im * b_im)
            high[i, im, :], low[i, im, :] = split(w_re * b_im - w_im * b_re)

    chunks(block, near)
    for i in range(parts):
        whole[pl.ds(i * block, block), :] = inverse(
            inv_high[...], inv_low[...], high[i], low[i]
        ).astype(BF16)
    scatter_blocks(me_ref, whole, outs)


def grads_kernel(
    grad_spec, mixed_spec, back_spec, near_spec, member, fwd_high, fwd_low, inv_high, inv_low,
    long_out, taps_out, skip_out, cross, high, low, total,
):
    parts, size, width = grad_spec.shape
    block = size // 2
    tap_count = taps_out.shape[0]
    sign = parity(width)
    total[...] = jnp.zeros_like(total)

    def products(at):
        re, im = pl.ds(at, CHUNK), pl.ds(block + at, CHUNK)
        p_re, p_im = [], []
        for d in range(parts):
            sum_re = sum_im = 0.0
            for i in range(d, parts):
                g_re, g_im = grad_spec[i, re, :], grad_spec[i, im, :]
                x_re, x_im = mixed_spec[i - d, re, :], mixed_spec[i - d, im, :]
                sum_re = sum_re + (g_re * x_re + g_im * x_im)
                sum_im = sum_im + (g_im * x_re - g_re * x_im)
            p_re.append(sum_re)
            p_im.append(sum_im)
        total[...] += p_re[0]
        for d in range(parts):
            q_re, q_im = p_re[d], p_im[d]
            if d + 1 < parts:
                q_re = q_re + sign * p_im[d + 1]
                q_im = q_im - sign * p_re[d + 1]
            cross[d, re, :], low[d, re, :] = split(q_re)
            cross[d, im, :], low[d, im, :] = split(q_im)
        sum_re = sum_im = 0.0
        for i in range(parts):
            b_re, b_im = back_spec[i, re, :], back_spec[i, im, :]
            s_re, s_im = near_spec[i, re, :], near_spec[i, im, :]
            sum_re = sum_re + (b_re * s_re + b_im * s_im)
            sum_im = sum_im + (b_im * s_re - b_re * s_im)
        high[0, re, :], high[1, re, :] = split(sum_re)
        high[0, im, :], high[1, im, :] = split(sum_im)

    chunks(block, products)
    taps_out[...] = inverse(inv_high[:tap_count, :], inv_low[:tap_count, :], high[0], high[1])
    for d in range(parts):
        summed = mm_nt(member[...], cross[d]) + mm_nt(member[...], low[d])
        s_high, s_low = split(summed * (2.0 / size))
        long_out[:, pl.ds(d * block, block)] = (
            mm(s_high, fwd_high[...]) + mm(s_high, fwd_low[...]) + mm(s_low, fwd_high[...])
        )
    skip_out[...] = jnp.sum(total[...], axis=0, keepdims=True) * (2.0 / size)


def gate_kernel(count, *refs):
    me_ref, blocks, refs = refs[0], refs[1 : 1 + count], refs[1 + count :]
    gating, upstream, output, gate_grad = refs
    width = blocks[0].shape[1]
    for shift, ref in enumerate(blocks):
        source = lax.rem(me_ref[0] + (count - shift), count)
        columns = pl.ds(pl.multiple_of(source * width, width), width)
        conv = ref[...].astype(F32)
        output[:, columns] = (gating[:, columns].astype(F32) * conv).astype(BF16)
        gate_grad[:, columns] = (upstream[:, columns].astype(F32) * conv).astype(BF16)


def place_kernel(count, *refs):
    me_ref, blocks, out = refs[0], refs[1 : 1 + count], refs[-1]
    width = blocks[0].shape[1]
    for shift, ref in enumerate(blocks):
        source = lax.rem(me_ref[0] + (count - shift), count)
        out[:, pl.ds(pl.multiple_of(source * width, width), width)] = ref[...]


def call(kernel, operands, outs, scratch=(), name=None):
    return pl.pallas_call(
        kernel,
        out_shape=outs,
        in_specs=[SMEM if x.dtype == jnp.int32 else VMEM for x in operands],
        out_specs=jax.tree.map(lambda _: VMEM, outs),
        scratch_shapes=[pltpu.VMEM(shape, dtype) for shape, dtype in scratch],
        name=name,
    )(*operands)


def exchange(blocks, axis):
    count = len(blocks)
    return [blocks[0]] + [
        lax.ppermute(blocks[k], axis, [(i, (i + k) % count) for i in range(count)])
        for k in range(1, count)
    ]


def columns_for(rows, me, count):
    width = rows.shape[1] // count
    return [
        lax.dynamic_slice_in_dim(rows, lax.rem(me + k, count) * width, width, 1)
        for k in range(count)
    ]


def in_order(blocks, me):
    count = len(blocks)
    order = lax.rem(me + count - jnp.arange(count), count)
    ordered = jnp.take(jnp.stack(blocks), order, axis=0)
    return jnp.transpose(ordered, (1, 0, 2)).reshape(blocks[0].shape[0], -1)


def sum_over(values, axis):
    if lax.axis_size(axis) != 4:
        return lax.psum(values, axis)

    def other(value, flip):
        return lax.ppermute(value, axis, [(i, i ^ flip) for i in range(4)])

    moved = [[other(v, flip) for v in values] for flip in (1, 2, 3)]
    return tuple((v + a) + (b + c) for v, a, b, c in zip(values, *moved))


def local(signal, gate_input, cotangent, long_filter, short_taps, skip_gain):
    series = signal[0]
    gating = gate_input[0]
    upstream = cotangent[0]
    rows, channels = series.shape
    count = lax.axis_size("ctx")
    me = lax.axis_index("ctx")
    where = me.astype(jnp.int32).reshape(1)
    length = rows * count
    width = channels // count
    groups = long_filter.shape[0]
    tap_count = short_taps.shape[0]
    block = min(length // 4, 512)
    size = 2 * block
    parts = length // block

    grad_gate = (upstream.astype(F32) * gating.astype(F32)).astype(BF16)
    series_in = exchange(columns_for(series, me, count), "ctx")
    grad_in = exchange(columns_for(grad_gate, me, count), "ctx")

    tables = [jnp.asarray(t) for t in dft_tables(block)]
    spread = jnp.repeat(long_filter.T, width // groups, axis=1)
    long_high, long_low = split(spread)
    own_taps = lax.dynamic_slice_in_dim(short_taps, me * width, width, 1)
    spectrum = jax.ShapeDtypeStruct((parts, size, width), F32)
    taps_spec, long_spec = call(
        filters_kernel,
        [own_taps, long_high, long_low, skip_gain[None, :], tables[0], tables[1]],
        [jax.ShapeDtypeStruct((size, width), F32), spectrum],
        name="filters",
    )
    blocks_out = [jax.ShapeDtypeStruct((rows, width), BF16)] * count
    half = ((parts, size, width), BF16)
    *conv, near_spec, mixed_spec = call(
        functools.partial(conv_kernel, count),
        [where, *series_in, *tables, taps_spec, long_spec],
        blocks_out + [spectrum, spectrum],
        [((length, width), BF16), ((parts, size, width), F32), half, half],
        name="conv",
    )
    conv_in = exchange(conv, "ctx")
    *grad, grad_spec, back_spec = call(
        functools.partial(back_kernel, count),
        [where, *grad_in, *tables, taps_spec, long_spec],
        blocks_out + [spectrum, spectrum],
        [((length, width), BF16), half, half],
        name="back",
    )
    signal_in = exchange(grad, "ctx")
    member = jnp.asarray(
        (np.arange(width)[None, :] // (width // groups) == np.arange(groups)[:, None]).astype(
            ml_dtypes.bfloat16
        )
    )
    long_part, taps_part, skip_part = call(
        grads_kernel,
        [grad_spec, mixed_spec, back_spec, near_spec, member, *tables],
        [
            jax.ShapeDtypeStruct((groups, length), F32),
            jax.ShapeDtypeStruct((tap_count, width), F32),
            jax.ShapeDtypeStruct((1, width), F32),
        ],
        [half, ((2, size, width), BF16), half, ((CHUNK, width), F32)],
        name="grads",
    )
    long_sum, taps_sum, skip_sum = sum_over((long_part, taps_part, skip_part), "dp")

    full = jax.ShapeDtypeStruct((rows, channels), BF16)
    if width % 128 == 0:
        output, gate_grad = call(
            functools.partial(gate_kernel, count),
            [where, *conv_in, gating, upstream],
            [full, full],
            name="gate",
        )
        signal_grad = call(
            functools.partial(place_kernel, count), [where, *signal_in], full, name="place"
        )
    else:
        conv_rows = in_order(conv_in, me).astype(F32)
        output = (gating.astype(F32) * conv_rows).astype(BF16)
        gate_grad = (upstream.astype(F32) * conv_rows).astype(BF16)
        signal_grad = in_order(signal_in, me)
    factor = 1.0 / math.sqrt(lax.axis_size("dp") * length)
    return (
        output[None],
        gate_grad[None],
        signal_grad[None],
        long_sum * factor,
        taps_sum * factor,
        skip_sum[0] * factor,
    )


def solution(mesh):
    return jax.shard_map(
        local,
        mesh=mesh,
        in_specs=(
            P("dp", "ctx", None),
            P("dp", "ctx", None),
            P("dp", "ctx", None),
            P("ctx", None),
            P(),
            P("ctx"),
        ),
        out_specs=(
            P("dp", "ctx", None),
            P("dp", "ctx", None),
            P("dp", "ctx", None),
            P("ctx", None),
            P(None, "ctx"),
            P("ctx"),
        ),
        check_vma=False,
    )
```

time: 290 us -> 109 us (0.38)
  local copies, waits for them, and re-layouts: 81.7 us -> 3.78 us
  matrix products: 65.1 us -> 0 us
  waiting for transfers between devices: 53.2 us -> 11 us
  blocking collectives: 39 us -> 0 us
  starting transfers between devices: 11.3 us -> 50.3 us
  Pallas kernels: 0 us -> 37.3 us
  other arithmetic: 22.4 us -> 5.04 us
  between operations: 14.6 us -> 1.14 us
    conv_general_dilated x3 -> x0, matrix products: 48 us -> none  [taps_time(): lax.conv_general_dilated(extended[None], kernel[:, None, :], (1,), 'VALID...]
    ppermute x2 -> x37, starting transfers between devices: 4.48 us -> 50.3 us  [the longest x28 39.7 us: exchange(): lax.ppermute(blocks[k], axis, [(i, (i + k) % count) for i in range(count)])]
    pallas_call x0 -> x6, Pallas kernels: none -> 37.3 us  [call(): pl.pallas_call(kernel, out_shape=outs, in_specs=[SMEM if x.dtype == jnp.i...]
    slice x10 -> x0, local copies, waits for them, and re-layouts: 31.7 us -> none  [the longest x3 27.1 us: mirror_index(): turned = jnp.roll(jnp.flip(spec, (0, 2)), 1, axis=0)]
    all_to_all x1 -> x0, blocking collectives: 29 us -> none  [local(): lax.all_to_all(jnp.stack([conv_ch, back_ch], axis=1), 'ctx', split_axis=0...]
    psum x1 -> x0, waiting for transfers between devices: 26.9 us -> none  [local(): lax.psum((lag_grad, tap_part, skip_part), 'dp')]
    all_to_all x1 -> x0, waiting for transfers between devices: 20 us -> none  [local(): lax.all_to_all(to_blocks(mixed_rows, grad_gate, ctx_count), 'ctx', split_...]
    dot_general x8 -> x0, matrix products: 17 us -> none  [the longest x4 12.2 us: tail_product(): lax.dot_general(data, table, (((2,), (0,)), ((), ())), precision=HIGH)]
  transfers between devices with their start and end apart: 5 -> 37, of which waited for: 3 -> 7; matrix products, arithmetic and copies ran while one was open for 16% -> 4% of each run, Pallas kernels for 0% -> 34%
where the time goes in v1:
time: 109 us
  starting transfers between devices  50.3 us (46%)
  Pallas kernels  37.3 us (34%)
  waiting for transfers between devices  11 us (10%)
  other arithmetic  5.04 us (5%)
  local copies, waits for them, and re-layouts  3.78 us (3%)
  between operations  1.14 us (1%)
    ppermute x28, starting transfers between devices, exchange(): lax.ppermute(blocks[k], axis, [(i, (i + k) % count) for i in range(count)])  39.7 us
    pallas_call x6, Pallas kernels, call(): pl.pallas_call(kernel, out_shape=outs, in_specs=[SMEM if x.dtype == jnp.i...  37.3 us
    ppermute x9, starting transfers between devices, other(): return lax.ppermute(value, axis, [(i, i ^ flip) for i in range(4)])  10.6 us
    ppermute x9, waiting for transfers between devices, other(): return lax.ppermute(value, axis, [(i, i ^ flip) for i in range(4)])  6.61 us
    ppermute x28, waiting for transfers between devices, exchange(): lax.ppermute(blocks[k], axis, [(i, (i + k) % count) for i in range(count)])  4.43 us
  transfers between devices with their start and end apart: 37, of which 7 were waited for; matrix products, arithmetic and copies ran while one was open for 4% of the time, Pallas kernels for 34%

profile of v1, /device:TPU:0, one launch (start us, length us, event | category | flops | bytes accessed | tf_op | source)
XLA Modules:
  0.0 108.6 jit_solution(10236028004181479938)
XLA Ops:
  0.7 1.4 %multiply_convert_fusion = bf16[128,2048]{1,0:T(8,128)(2,1)S(1)} fusion(bf16[1,128,2048]{2,1,0:T(8,128)(2,1)} %param.13, bf16[1,128,2048]{2,1,0:T(8,128)(2,1)} %param.12), kind=kLoop, calls=%fused_computation | loop fusion | flops 1048576 | bytes 1572864 | tf_op jit(solution)/shard_map/convert_element_type | solution.py:331
  2.1 0.8 constant_dynamic-slice_fusion
  2.9 4.5 %collective-permute-start.20 = (bf16[128,256]{1,0:T(8,128)(2,1)}, bf16[128,256]{1,0:T(8,128)(2,1)S(1)}, u32[]{:S(2)}, u32[]{:S(2)}) collective-permute-start(bf16[128,256]{1,0:T(8,128)(2,1)} %get-tuple-element.62), channel_id=1, source_target_pairs={{0,7},{1,0},{2,1},{3,2},{4,3},{5,4},{6,5},{7,6},{8,15},{9,8},{10,9... | collective-permute-start | bytes 196616 | tf_op jit(solution)/shard_map/ppermute | solution.py:284
  7.4 0.6 collective-permute-start.19
  7.9 2.7 %collective-permute-start.17 = (bf16[128,256]{1,0:T(8,128)(2,1)}, bf16[128,256]{1,0:T(8,128)(2,1)S(1)}, u32[]{:S(2)}, u32[]{:S(2)}) collective-permute-start(bf16[128,256]{1,0:T(8,128)(2,1)} %get-tuple-element.65), channel_id=1, source_target_pairs={{0,4},{1,5},{2,6},{3,7},{4,0},{5,1},{6,2},{7,3},{8,12},{9,13},{10,... | collective-permute-start | bytes 196616 | tf_op jit(solution)/shard_map/ppermute | solution.py:284
  11.2 0.7 dynamic-slice_bitcast_fusion
  11.9 0.6 collective-permute-start.15
  12.6 0.8 collective-permute-start.14
  13.4 6.1 %collective-permute-start.6 = (bf16[128,256]{1,0:T(8,128)(2,1)S(1)}, bf16[128,256]{1,0:T(8,128)(2,1)S(1)}, u32[]{:S(2)}, u32[]{:S(2)}) collective-permute-start(bf16[128,256]{1,0:T(8,128)(2,1)S(1)} %get-tuple-element.70), channel_id=1, source_target_pairs={{0,7},{1,0},{2,1},{3,2},{4,3},{5,4},{6,5},{7,6},{8,15},{9,8},{10,9... | collective-permute-start | bytes 196616 | tf_op jit(solution)/shard_map/ppermute | solution.py:284
  19.5 1.3 %collective-permute-done.17.refs_5_ = bf16[128,256]{1,0:T(8,128)(2,1)S(1)} collective-permute-done((bf16[128,256]{1,0:T(8,128)(2,1)}, bf16[128,256]{1,0:T(8,128)(2,1)S(1)}, u32[]{:S(2)}, u32[]{:S(2)}) %collective-permute-start.17) | collective-permute-done | bytes 65568 | tf_op jit(solution)/shard_map/ppermute | solution.py:284
  20.8 1.1 subtract_convert_fusion
  21.9 2.0 %collective-permute-start.3 = (bf16[128,256]{1,0:T(8,128)(2,1)S(1)}, bf16[128,256]{1,0:T(8,128)(2,1)S(1)}, u32[]{:S(2)}, u32[]{:S(2)}) collective-permute-start(bf16[128,256]{1,0:T(8,128)(2,1)S(1)} %get-tuple-element.72), channel_id=1, source_target_pairs={{0,4},{1,5},{2,6},{3,7},{4,0},{5,1},{6,2},{7,3},{8,12},{9,13},{10,... | collective-permute-start | bytes 196616 | tf_op jit(solution)/shard_map/ppermute | solution.py:284
  23.9 1.6 %collective-permute-start.1 = (bf16[128,256]{1,0:T(8,128)(2,1)S(1)}, bf16[128,256]{1,0:T(8,128)(2,1)S(1)}, u32[]{:S(2)}, u32[]{:S(2)}) collective-permute-start(bf16[128,256]{1,0:T(8,128)(2,1)S(1)} %get-tuple-element.74), channel_id=1, source_target_pairs={{0,2},{1,3},{2,4},{3,5},{4,6},{5,7},{6,0},{7,1},{8,10},{9,11},{10,... | collective-permute-start | bytes 196616 | tf_op jit(solution)/shard_map/ppermute | solution.py:284
  25.5 3.0 %collective-permute-start.5 = (bf16[128,256]{1,0:T(8,128)(2,1)S(1)}, bf16[128,256]{1,0:T(8,128)(2,1)S(1)}, u32[]{:S(2)}, u32[]{:S(2)}) collective-permute-start(bf16[128,256]{1,0:T(8,128)(2,1)S(1)} %get-tuple-element.77), channel_id=1, source_target_pairs={{0,6},{1,7},{2,0},{3,1},{4,2},{5,3},{6,4},{7,5},{8,14},{9,15},{10,... | collective-permute-start | bytes 196616 | tf_op jit(solution)/shard_map/ppermute | solution.py:284
  28.5 0.6 constant_dynamic-slice_fusion.8.taps
  29.1 4.2 %filters.1 = (f32[512,256]{1,0:T(8,128)}, f32[4,512,256]{2,1,0:T(8,128)}) custom-call(bf16[128,256]{1,0:T(8,128)(2,1)} %constant_dynamic-slice_fusion.8.taps, bf16[1024,256]{1,0:T(8,128)(2,1)} %get-tuple-element.61.long_high, bf16[1024,256]{1,0:T(8,128)(2,1)} %get-tuple-element.60.long_low, f32[1,256]{1,0:T(1,128)} %bitcast.34, ...), custom_call_target="tpu_custom_call" | custom-call | tf_op jit(solution)/shard_map/filters/pallas_call | solution.py:271
  33.4 10.4 %back.1 = (bf16[128,256]{1,0:T(8,128)(2,1)}, bf16[128,256]{1,0:T(8,128)(2,1)}, bf16[128,256]{1,0:T(8,128)(2,1)}, bf16[128,256]{1,0:T(8,128)(2,1)}, bf16[128,256]...) custom-call(s32[1]{0:T(128)} %bitcast.refs_0_, ...), custom_call_target="tpu_custom_call" | custom-call | tf_op jit(solution)/shard_map/back/pallas_call | solution.py:271
  43.9 0.7 collective-permute-start.21
  44.7 0.5 copy-done.13
  45.3 10.6 %conv.1 = (bf16[128,256]{1,0:T(8,128)(2,1)}, bf16[128,256]{1,0:T(8,128)(2,1)}, bf16[128,256]{1,0:T(8,128)(2,1)}, bf16[128,256]{1,0:T(8,128)(2,1)}, bf16[128,256]...) custom-call(s32[1]{0:T(128)} %bitcast.refs_0_, ...), custom_call_target="tpu_custom_call" | custom-call | tf_op jit(solution)/shard_map/conv/pallas_call | solution.py:271
  56.0 7.4 %grads.1 = (f32[16,1024]{1,0:T(8,128)}, f32[128,256]{1,0:T(8,128)}, f32[1,256]{1,0:T(1,128)}) custom-call(f32[4,512,256]{2,1,0:T(8,128)} %get-tuple-element.53.grad_spec, f32[4,512,256]{2,1,0:T(8,128)} %get-tuple-element.54.mixed_spec, f32[4,512,256]{2,1,0:T(8,128)} %get-tuple-element.55.back_spec, f32[4,512,256]{2,1,0:T(8,128)} %get-tuple-element.56.near_spec, ...), custom_call_target="tpu_custom_call" | custom-call | tf_op jit(solution)/shard_map/grads/pallas_call | solution.py:271
  63.4 2.5 %collective-permute-start.36 = (f32[1,256]{1,0:T(1,128)}, f32[1,256]{1,0:T(1,128)S(1)}, u32[]{:S(2)}, u32[]{:S(2)}) collective-permute-start(f32[1,256]{1,0:T(1,128)} %get-tuple-element.59), channel_id=1, source_target_pairs={{0,24},{8,16},{16,8},{24,0},{1,25},{9,17},{17,9},{25,1},{2,26},{10... | collective-permute-start | bytes 3080 | tf_op jit(solution)/shard_map/ppermute | solution.py:309
  65.9 0.5 collective-permute-start.35
  66.4 0.5 collective-permute-start.34
  67.0 1.2 %collective-permute-done.36 = f32[1,256]{1,0:T(1,128)S(1)} collective-permute-done((f32[1,256]{1,0:T(1,128)}, f32[1,256]{1,0:T(1,128)S(1)}, u32[]{:S(2)}, u32[]{:S(2)}) %collective-permute-start.36) | collective-permute-done | bytes 1056 | tf_op jit(solution)/shard_map/ppermute | solution.py:309
  68.2 1.5 %collective-permute-done.35 = f32[1,256]{1,0:T(1,128)S(1)} collective-permute-done((f32[1,256]{1,0:T(1,128)}, f32[1,256]{1,0:T(1,128)S(1)}, u32[]{:S(2)}, u32[]{:S(2)}) %collective-permute-start.35) | collective-permute-done | bytes 1056 | tf_op jit(solution)/shard_map/ppermute | solution.py:309
  69.7 1.1 %collective-permute-start.24 = (bf16[128,256]{1,0:T(8,128)(2,1)S(1)}, bf16[128,256]{1,0:T(8,128)(2,1)S(1)}, u32[]{:S(2)}, u32[]{:S(2)}) collective-permute-start(bf16[128,256]{1,0:T(8,128)(2,1)S(1)} %copy-done.41), channel_id=1, source_target_pairs={{0,4},{1,5},{2,6},{3,7},{4,0},{5,1},{6,2},{7,3},{8,12},{9,13},{10,... | collective-permute-start | bytes 196616 | tf_op jit(solution)/shard_map/ppermute | solution.py:284
  70.8 0.8 collective-permute-start.25
  71.6 3.1 %collective-permute-start.26 = (bf16[128,256]{1,0:T(8,128)(2,1)S(1)}, bf16[128,256]{1,0:T(8,128)(2,1)S(1)}, u32[]{:S(2)}, u32[]{:S(2)}) collective-permute-start(bf16[128,256]{1,0:T(8,128)(2,1)S(1)} %copy-done.37), channel_id=1, source_target_pairs={{0,6},{1,7},{2,0},{3,1},{4,2},{5,3},{6,4},{7,5},{8,14},{9,15},{10,... | collective-permute-start | bytes 196616 | tf_op jit(solution)/shard_map/ppermute | solution.py:284
  74.8 1.8 %collective-permute-start.27 = (bf16[128,256]{1,0:T(8,128)(2,1)S(1)}, bf16[128,256]{1,0:T(8,128)(2,1)S(1)}, u32[]{:S(2)}, u32[]{:S(2)}) collective-permute-start(bf16[128,256]{1,0:T(8,128)(2,1)S(1)} %copy-done.35), channel_id=1, source_target_pairs={{0,7},{1,0},{2,1},{3,2},{4,3},{5,4},{6,5},{7,6},{8,15},{9,8},{10,9... | collective-permute-start | bytes 196616 | tf_op jit(solution)/shard_map/ppermute | solution.py:284
  76.6 1.2 %collective-permute-done.24.refs_5_ = bf16[128,256]{1,0:T(8,128)(2,1)S(1)} collective-permute-done((bf16[128,256]{1,0:T(8,128)(2,1)S(1)}, bf16[128,256]{1,0:T(8,128)(2,1)S(1)}, u32[]{:S(2)}, u32[]{:S(2)}) %collective-permute-start.24) | collective-permute-done | bytes 65568 | tf_op jit(solution)/shard_map/ppermute | solution.py:284
  77.8 1.3 %collective-permute-start.8 = (bf16[128,256]{1,0:T(8,128)(2,1)S(1)}, bf16[128,256]{1,0:T(8,128)(2,1)S(1)}, u32[]{:S(2)}, u32[]{:S(2)}) collective-permute-start(bf16[128,256]{1,0:T(8,128)(2,1)S(1)} %copy-done.42), channel_id=1, source_target_pairs={{0,2},{1,3},{2,4},{3,5},{4,6},{5,7},{6,0},{7,1},{8,10},{9,11},{10,... | collective-permute-start | bytes 196616 | tf_op jit(solution)/shard_map/ppermute | solution.py:284
  79.1 0.8 collective-permute-start.9
  80.0 4.1 %collective-permute-start.10 = (bf16[128,256]{1,0:T(8,128)(2,1)S(1)}, bf16[128,256]{1,0:T(8,128)(2,1)S(1)}, u32[]{:S(2)}, u32[]{:S(2)}) collective-permute-start(bf16[128,256]{1,0:T(8,128)(2,1)S(1)} %copy-done.38), channel_id=1, source_target_pairs={{0,4},{1,5},{2,6},{3,7},{4,0},{5,1},{6,2},{7,3},{8,12},{9,13},{10,... | collective-permute-start | bytes 196616 | tf_op jit(solution)/shard_map/ppermute | solution.py:284
  84.1 0.9 collective-permute-start.11
  85.1 2.5 %collective-permute-start.30 = (f32[16,1024]{1,0:T(8,128)}, f32[16,1024]{1,0:T(8,128)S(1)}, u32[]{:S(2)}, u32[]{:S(2)}) collective-permute-start(f32[16,1024]{1,0:T(8,128)} %get-tuple-element.57), channel_id=1, source_target_pairs={{0,24},{8,16},{16,8},{24,0},{1,25},{9,17},{17,9},{25,1},{2,26},{10... | collective-permute-start | bytes 196616 | tf_op jit(solution)/shard_map/ppermute | solution.py:309
  87.9 1.8 %collective-permute-done.9.refs_4_ = bf16[128,256]{1,0:T(8,128)(2,1)S(1)} collective-permute-done((bf16[128,256]{1,0:T(8,128)(2,1)S(1)}, bf16[128,256]{1,0:T(8,128)(2,1)S(1)}, u32[]{:S(2)}, u32[]{:S(2)}) %collective-permute-start.9) | collective-permute-done | bytes 65568 | tf_op jit(solution)/shard_map/ppermute | solution.py:284
  89.7 0.6 collective-permute-start.28
  90.3 2.7 %collective-permute-start.12 = (bf16[128,256]{1,0:T(8,128)(2,1)S(1)}, bf16[128,256]{1,0:T(8,128)(2,1)S(1)}, u32[]{:S(2)}, u32[]{:S(2)}) collective-permute-start(bf16[128,256]{1,0:T(8,128)(2,1)S(1)} %copy-done.34), channel_id=1, source_target_pairs={{0,6},{1,7},{2,0},{3,1},{4,2},{5,3},{6,4},{7,5},{8,14},{9,15},{10,... | collective-permute-start | bytes 196616 | tf_op jit(solution)/shard_map/ppermute | solution.py:284
  93.3 1.2 %add_multiply_fusion.2 = f32[1,256]{1,0:T(1,128)} fusion(f32[1,256]{1,0:T(1,128)S(1)} %collective-permute-done.35, f32[1,256]{1,0:T(1,128)S(1)} %collective-permute-done.36, f32[1,256]{1,0:T(1,128)} %get-tuple-element.59, f32[1,256]{1,0:T(1,128)S(1)} %collective-permute-done.34), kind=kLoop, calls=%fused_computation.21 | loop fusion | flops 1024 | bytes 5120 | tf_op jit(solution)/shard_map/mul | solution.py:405
  94.6 1.9 %place.1 = bf16[128,2048]{1,0:T(8,128)(2,1)} custom-call(s32[1]{0:T(128)} %bitcast.refs_0_, bf16[128,256]{1,0:T(8,128)(2,1)} %get-tuple-element.45.refs_1_, bf16[128,256]{1,0:T(8,128)(2,1)} %copy-done.26, bf16[128,256]{1,0:T(8,128)(2,1)} %copy-done.27, bf16[128,256]{1,0:T(8,128)(2,1)} %copy-done.28, bf16[128,256]{1,0:T(8,128)(2,1)} %copy-done.29, ...), custom_call_target="tpu_custom_call" | custom-call | tf_op jit(solution)/shard_map/place/pallas_call | solution.py:271
  96.6 2.4 %collective-permute-start.33 = (f32[128,256]{1,0:T(8,128)}, f32[128,256]{1,0:T(8,128)S(1)}, u32[]{:S(2)}, u32[]{:S(2)}) collective-permute-start(f32[128,256]{1,0:T(8,128)} %get-tuple-element.58), channel_id=1, source_target_pairs={{0,24},{8,16},{16,8},{24,0},{1,25},{9,17},{17,9},{25,1},{2,26},{10... | collective-permute-start | bytes 393224 | tf_op jit(solution)/shard_map/ppermute | solution.py:309
  99.6 2.7 %gate.1 = (bf16[128,2048]{1,0:T(8,128)(2,1)}, bf16[128,2048]{1,0:T(8,128)(2,1)}) custom-call(s32[1]{0:T(128)} %bitcast.refs_0_, bf16[128,256]{1,0:T(8,128)(2,1)} %get-tuple-element.35.refs_1_, bf16[128,256]{1,0:T(8,128)(2,1)} %copy-done.19, bf16[128,256]{1,0:T(8,128)(2,1)} %copy-done.20, bf16[128,256]{1,0:T(8,128)(2,1)} %copy-done.21, ...), custom_call_target="tpu_custom_call" | custom-call | tf_op jit(solution)/shard_map/gate/pallas_call | solution.py:271
  102.3 1.1 %collective-permute-start.31 = (f32[128,256]{1,0:T(8,128)S(1)}, f32[128,256]{1,0:T(8,128)S(1)}, u32[]{:S(2)}, u32[]{:S(2)}) collective-permute-start(f32[128,256]{1,0:T(8,128)S(1)} %copy-done.2), channel_id=1, source_target_pairs={{0,8},{8,0},{16,24},{24,16},{1,9},{9,1},{17,25},{25,17},{2,10},{10... | collective-permute-start | bytes 393224 | tf_op jit(solution)/shard_map/ppermute | solution.py:309
  103.4 0.6 add_multiply_fusion.1
  104.0 2.1 %collective-permute-done.32 = f32[128,256]{1,0:T(8,128)S(1)} collective-permute-done((f32[128,256]{1,0:T(8,128)}, f32[128,256]{1,0:T(8,128)S(1)}, u32[]{:S(2)}, u32[]{:S(2)}) %collective-permute-start.32) | collective-permute-done | bytes 131104 | tf_op jit(solution)/shard_map/ppermute | solution.py:309
  106.2 1.8 %collective-permute-done.31 = f32[128,256]{1,0:T(8,128)S(1)} collective-permute-done((f32[128,256]{1,0:T(8,128)S(1)}, f32[128,256]{1,0:T(8,128)S(1)}, u32[]{:S(2)}, u32[]{:S(2)}) %collective-permute-start.31) | collective-permute-done | bytes 131104 | tf_op jit(solution)/shard_map/ppermute | solution.py:309
  107.9 0.7 add_multiply_fusion
  (132 shorter events, 2.1 us)
Async XLA Ops:
  0.6 27.9 %copy-start = (bf16[128,2048]{1,0:T(8,128)(2,1)S(1)}, bf16[128,2048]{1,0:T(8,128)(2,1)}, u32[]{:S(2)}) copy-start(bf16[128,2048]{1,0:T(8,128)(2,1)} %param.15) | copy-start | bytes 1572868
  2.9 9.0 %collective-permute-start.20 = (bf16[128,256]{1,0:T(8,128)(2,1)}, bf16[128,256]{1,0:T(8,128)(2,1)S(1)}, u32[]{:S(2)}, u32[]{:S(2)}) collective-permute-start(bf16[128,256]{1,0:T(8,128)(2,1)} %get-tuple-element.62), channel_id=1, source_target_pairs={{0,7},{1,0},{2,1},{3,2},{4,3},{5,4},{6,5},{7,6},{8,15},{9,8},{10,9... | collective-permute-start | bytes 196616 | tf_op jit(solution)/shard_map/ppermute | solution.py:284
  7.4 5.2 %collective-permute-start.19 = (bf16[128,256]{1,0:T(8,128)(2,1)}, bf16[128,256]{1,0:T(8,128)(2,1)S(1)}, u32[]{:S(2)}, u32[]{:S(2)}) collective-permute-start(bf16[128,256]{1,0:T(8,128)(2,1)} %get-tuple-element.63), channel_id=1, source_target_pairs={{0,6},{1,7},{2,0},{3,1},{4,2},{5,3},{6,4},{7,5},{8,14},{9,15},{10,... | collective-permute-start | bytes 196616 | tf_op jit(solution)/shard_map/ppermute | solution.py:284
  7.9 5.4 %collective-permute-start.18 = (bf16[128,256]{1,0:T(8,128)(2,1)}, bf16[128,256]{1,0:T(8,128)(2,1)S(1)}, u32[]{:S(2)}, u32[]{:S(2)}) collective-permute-start(bf16[128,256]{1,0:T(8,128)(2,1)} %get-tuple-element.64), channel_id=1, source_target_pairs={{0,5},{1,6},{2,7},{3,0},{4,1},{5,2},{6,3},{7,4},{8,13},{9,14},{10,... | collective-permute-start | bytes 196616 | tf_op jit(solution)/shard_map/ppermute | solution.py:284
  7.9 12.8 %collective-permute-start.17 = (bf16[128,256]{1,0:T(8,128)(2,1)}, bf16[128,256]{1,0:T(8,128)(2,1)S(1)}, u32[]{:S(2)}, u32[]{:S(2)}) collective-permute-start(bf16[128,256]{1,0:T(8,128)(2,1)} %get-tuple-element.65), channel_id=1, source_target_pairs={{0,4},{1,5},{2,6},{3,7},{4,0},{5,1},{6,2},{7,3},{8,12},{9,13},{10,... | collective-permute-start | bytes 196616 | tf_op jit(solution)/shard_map/ppermute | solution.py:284
  10.7 11.2 %collective-permute-start.16 = (bf16[128,256]{1,0:T(8,128)(2,1)}, bf16[128,256]{1,0:T(8,128)(2,1)S(1)}, u32[]{:S(2)}, u32[]{:S(2)}) collective-permute-start(bf16[128,256]{1,0:T(8,128)(2,1)} %get-tuple-element.66), channel_id=1, source_target_pairs={{0,3},{1,4},{2,5},{3,6},{4,7},{5,0},{6,1},{7,2},{8,11},{9,12},{10,... | collective-permute-start | bytes 196616 | tf_op jit(solution)/shard_map/ppermute | solution.py:284
  11.9 21.5 %copy-start.3 = (bf16[128,256]{1,0:T(8,128)(2,1)}, bf16[128,256]{1,0:T(8,128)(2,1)S(1)}, u32[]{:S(2)}) copy-start(bf16[128,256]{1,0:T(8,128)(2,1)S(1)} %collective-permute-done.20.refs_8_) | copy-start | bytes 196612
  11.9 12.0 %collective-permute-start.15 = (bf16[128,256]{1,0:T(8,128)(2,1)}, bf16[128,256]{1,0:T(8,128)(2,1)S(1)}, u32[]{:S(2)}, u32[]{:S(2)}) collective-permute-start(bf16[128,256]{1,0:T(8,128)(2,1)} %get-tuple-element.67), channel_id=1, source_target_pairs={{0,2},{1,3},{2,4},{3,5},{4,6},{5,7},{6,0},{7,1},{8,10},{9,11},{10,... | collective-permute-start | bytes 196616 | tf_op jit(solution)/shard_map/ppermute | solution.py:284
  12.6 11.3 %collective-permute-start.14 = (bf16[128,256]{1,0:T(8,128)(2,1)S(1)}, bf16[128,256]{1,0:T(8,128)(2,1)S(1)}, u32[]{:S(2)}, u32[]{:S(2)}) collective-permute-start(bf16[128,256]{1,0:T(8,128)(2,1)S(1)} %get-tuple-element.68), channel_id=1, source_target_pairs={{0,1},{1,2},{2,3},{3,4},{4,5},{5,6},{6,7},{7,0},{8,9},{9,10},{10,1... | collective-permute-start | bytes 196616 | tf_op jit(solution)/shard_map/ppermute | solution.py:284
  13.4 12.1 %collective-permute-start.6 = (bf16[128,256]{1,0:T(8,128)(2,1)S(1)}, bf16[128,256]{1,0:T(8,128)(2,1)S(1)}, u32[]{:S(2)}, u32[]{:S(2)}) collective-permute-start(bf16[128,256]{1,0:T(8,128)(2,1)S(1)} %get-tuple-element.70), channel_id=1, source_target_pairs={{0,7},{1,0},{2,1},{3,2},{4,3},{5,4},{6,5},{7,6},{8,15},{9,8},{10,9... | collective-permute-start | bytes 196616 | tf_op jit(solution)/shard_map/ppermute | solution.py:284
  20.8 4.7 %collective-permute-start.4 = (bf16[128,256]{1,0:T(8,128)(2,1)S(1)}, bf16[128,256]{1,0:T(8,128)(2,1)S(1)}, u32[]{:S(2)}, u32[]{:S(2)}) collective-permute-start(bf16[128,256]{1,0:T(8,128)(2,1)S(1)} %get-tuple-element.71), channel_id=1, source_target_pairs={{0,5},{1,6},{2,7},{3,0},{4,1},{5,2},{6,3},{7,4},{8,13},{9,14},{10,... | collective-permute-start | bytes 196616 | tf_op jit(solution)/shard_map/ppermute | solution.py:284
  21.9 22.0 %collective-permute-start.3 = (bf16[128,256]{1,0:T(8,128)(2,1)S(1)}, bf16[128,256]{1,0:T(8,128)(2,1)S(1)}, u32[]{:S(2)}, u32[]{:S(2)}) collective-permute-start(bf16[128,256]{1,0:T(8,128)(2,1)S(1)} %get-tuple-element.72), channel_id=1, source_target_pairs={{0,4},{1,5},{2,6},{3,7},{4,0},{5,1},{6,2},{7,3},{8,12},{9,13},{10,... | collective-permute-start | bytes 196616 | tf_op jit(solution)/shard_map/ppermute | solution.py:284
  23.9 20.7 %collective-permute-start.2 = (bf16[128,256]{1,0:T(8,128)(2,1)S(1)}, bf16[128,256]{1,0:T(8,128)(2,1)S(1)}, u32[]{:S(2)}, u32[]{:S(2)}) collective-permute-start(bf16[128,256]{1,0:T(8,128)(2,1)S(1)} %get-tuple-element.73), channel_id=1, source_target_pairs={{0,3},{1,4},{2,5},{3,6},{4,7},{5,0},{6,1},{7,2},{8,11},{9,12},{10,... | collective-permute-start | bytes 196616 | tf_op jit(solution)/shard_map/ppermute | solution.py:284
  23.9 20.7 %collective-permute-start.1 = (bf16[128,256]{1,0:T(8,128)(2,1)S(1)}, bf16[128,256]{1,0:T(8,128)(2,1)S(1)}, u32[]{:S(2)}, u32[]{:S(2)}) collective-permute-start(bf16[128,256]{1,0:T(8,128)(2,1)S(1)} %get-tuple-element.74), channel_id=1, source_target_pairs={{0,2},{1,3},{2,4},{3,5},{4,6},{5,7},{6,0},{7,1},{8,10},{9,11},{10,... | collective-permute-start | bytes 196616 | tf_op jit(solution)/shard_map/ppermute | solution.py:284
  25.5 19.2 %collective-permute-start = (bf16[128,256]{1,0:T(8,128)(2,1)S(1)}, bf16[128,256]{1,0:T(8,128)(2,1)S(1)}, u32[]{:S(2)}, u32[]{:S(2)}) collective-permute-start(bf16[128,256]{1,0:T(8,128)(2,1)S(1)} %get-tuple-element.75), channel_id=1, source_target_pairs={{0,1},{1,2},{2,3},{3,4},{4,5},{5,6},{6,7},{7,0},{8,9},{9,10},{10,1... | collective-permute-start | bytes 196616 | tf_op jit(solution)/shard_map/ppermute | solution.py:284
  25.5 19.1 %collective-permute-start.5 = (bf16[128,256]{1,0:T(8,128)(2,1)S(1)}, bf16[128,256]{1,0:T(8,128)(2,1)S(1)}, u32[]{:S(2)}, u32[]{:S(2)}) collective-permute-start(bf16[128,256]{1,0:T(8,128)(2,1)S(1)} %get-tuple-element.77), channel_id=1, source_target_pairs={{0,6},{1,7},{2,0},{3,1},{4,2},{5,3},{6,4},{7,5},{8,14},{9,15},{10,... | collective-permute-start | bytes 196616 | tf_op jit(solution)/shard_map/ppermute | solution.py:284
  43.9 27.8 %collective-permute-start.21 = (bf16[128,256]{1,0:T(8,128)(2,1)}, bf16[128,256]{1,0:T(8,128)(2,1)S(1)}, u32[]{:S(2)}, u32[]{:S(2)}) collective-permute-start(bf16[128,256]{1,0:T(8,128)(2,1)} %get-tuple-element.46), channel_id=1, source_target_pairs={{0,1},{1,2},{2,3},{3,4},{4,5},{5,6},{6,7},{7,0},{8,9},{9,10},{10,1... | collective-permute-start | bytes 196616 | tf_op jit(solution)/shard_map/ppermute | solution.py:284
  44.6 30.1 %collective-permute-start.22 = (bf16[128,256]{1,0:T(8,128)(2,1)}, bf16[128,256]{1,0:T(8,128)(2,1)S(1)}, u32[]{:S(2)}, u32[]{:S(2)}) collective-permute-start(bf16[128,256]{1,0:T(8,128)(2,1)} %get-tuple-element.47), channel_id=1, source_target_pairs={{0,2},{1,3},{2,4},{3,5},{4,6},{5,7},{6,0},{7,1},{8,10},{9,11},{10,... | collective-permute-start | bytes 196616 | tf_op jit(solution)/shard_map/ppermute | solution.py:284
  55.9 21.9 %copy-start.42 = (bf16[128,256]{1,0:T(8,128)(2,1)S(1)}, bf16[128,256]{1,0:T(8,128)(2,1)}, u32[]{:S(2)}) copy-start(bf16[128,256]{1,0:T(8,128)(2,1)} %get-tuple-element.37) | copy-start | bytes 196612
  55.9 23.2 %copy-start.40 = (bf16[128,256]{1,0:T(8,128)(2,1)S(1)}, bf16[128,256]{1,0:T(8,128)(2,1)}, u32[]{:S(2)}) copy-start(bf16[128,256]{1,0:T(8,128)(2,1)} %get-tuple-element.38) | copy-start | bytes 196612
  55.9 24.0 %copy-start.38 = (bf16[128,256]{1,0:T(8,128)(2,1)S(1)}, bf16[128,256]{1,0:T(8,128)(2,1)}, u32[]{:S(2)}) copy-start(bf16[128,256]{1,0:T(8,128)(2,1)} %get-tuple-element.39) | copy-start | bytes 196612
  56.0 28.2 %copy-start.36 = (bf16[128,256]{1,0:T(8,128)(2,1)S(1)}, bf16[128,256]{1,0:T(8,128)(2,1)}, u32[]{:S(2)}) copy-start(bf16[128,256]{1,0:T(8,128)(2,1)} %get-tuple-element.40) | copy-start | bytes 196612
  56.0 34.4 %copy-start.34 = (bf16[128,256]{1,0:T(8,128)(2,1)S(1)}, bf16[128,256]{1,0:T(8,128)(2,1)}, u32[]{:S(2)}) copy-start(bf16[128,256]{1,0:T(8,128)(2,1)} %get-tuple-element.41) | copy-start | bytes 196612
  56.0 37.0 %copy-start.33 = (bf16[128,256]{1,0:T(8,128)(2,1)S(1)}, bf16[128,256]{1,0:T(8,128)(2,1)}, u32[]{:S(2)}) copy-start(bf16[128,256]{1,0:T(8,128)(2,1)} %get-tuple-element.42) | copy-start | bytes 196612
  63.4 38.9 %copy-start.2 = (f32[128,256]{1,0:T(8,128)S(1)}, f32[128,256]{1,0:T(8,128)}, u32[]{:S(2)}) copy-start(f32[128,256]{1,0:T(8,128)} %get-tuple-element.58) | copy-start | bytes 393220
  63.4 40.0 %copy-start.18 = (f32[16,1024]{1,0:T(8,128)S(1)}, f32[16,1024]{1,0:T(8,128)}, u32[]{:S(2)}) copy-start(f32[16,1024]{1,0:T(8,128)} %get-tuple-element.57) | copy-start | bytes 196612
  63.4 4.7 %collective-permute-start.36 = (f32[1,256]{1,0:T(1,128)}, f32[1,256]{1,0:T(1,128)S(1)}, u32[]{:S(2)}, u32[]{:S(2)}) collective-permute-start(f32[1,256]{1,0:T(1,128)} %get-tuple-element.59), channel_id=1, source_target_pairs={{0,24},{8,16},{16,8},{24,0},{1,25},{9,17},{17,9},{25,1},{2,26},{10... | collective-permute-start | bytes 3080 | tf_op jit(solution)/shard_map/ppermute | solution.py:309
  65.9 3.8 %collective-permute-start.35 = (f32[1,256]{1,0:T(1,128)}, f32[1,256]{1,0:T(1,128)S(1)}, u32[]{:S(2)}, u32[]{:S(2)}) collective-permute-start(f32[1,256]{1,0:T(1,128)} %get-tuple-element.59), channel_id=1, source_target_pairs={{0,16},{8,24},{16,0},{24,8},{1,17},{9,25},{17,1},{25,9},{2,18},{10... | collective-permute-start | bytes 3080 | tf_op jit(solution)/shard_map/ppermute | solution.py:309
  66.4 4.4 %collective-permute-start.34 = (f32[1,256]{1,0:T(1,128)}, f32[1,256]{1,0:T(1,128)S(1)}, u32[]{:S(2)}, u32[]{:S(2)}) collective-permute-start(f32[1,256]{1,0:T(1,128)} %get-tuple-element.59), channel_id=1, source_target_pairs={{0,8},{8,0},{16,24},{24,16},{1,9},{9,1},{17,25},{25,17},{2,10},{10... | collective-permute-start | bytes 3080 | tf_op jit(solution)/shard_map/ppermute | solution.py:309
  68.2 8.4 %collective-permute-start.23 = (bf16[128,256]{1,0:T(8,128)(2,1)S(1)}, bf16[128,256]{1,0:T(8,128)(2,1)S(1)}, u32[]{:S(2)}, u32[]{:S(2)}) collective-permute-start(bf16[128,256]{1,0:T(8,128)(2,1)S(1)} %copy-done.43), channel_id=1, source_target_pairs={{0,3},{1,4},{2,5},{3,6},{4,7},{5,0},{6,1},{7,2},{8,11},{9,12},{10,... | collective-permute-start | bytes 196616 | tf_op jit(solution)/shard_map/ppermute | solution.py:284
  69.7 8.1 %collective-permute-start.24 = (bf16[128,256]{1,0:T(8,128)(2,1)S(1)}, bf16[128,256]{1,0:T(8,128)(2,1)S(1)}, u32[]{:S(2)}, u32[]{:S(2)}) collective-permute-start(bf16[128,256]{1,0:T(8,128)(2,1)S(1)} %copy-done.41), channel_id=1, source_target_pairs={{0,4},{1,5},{2,6},{3,7},{4,0},{5,1},{6,2},{7,3},{8,12},{9,13},{10,... | collective-permute-start | bytes 196616 | tf_op jit(solution)/shard_map/ppermute | solution.py:284
  70.8 8.3 %collective-permute-start.25 = (bf16[128,256]{1,0:T(8,128)(2,1)S(1)}, bf16[128,256]{1,0:T(8,128)(2,1)S(1)}, u32[]{:S(2)}, u32[]{:S(2)}) collective-permute-start(bf16[128,256]{1,0:T(8,128)(2,1)S(1)} %copy-done.39), channel_id=1, source_target_pairs={{0,5},{1,6},{2,7},{3,0},{4,1},{5,2},{6,3},{7,4},{8,13},{9,14},{10,... | collective-permute-start | bytes 196616 | tf_op jit(solution)/shard_map/ppermute | solution.py:284
  71.6 23.0 %copy-start.26 = (bf16[128,256]{1,0:T(8,128)(2,1)}, bf16[128,256]{1,0:T(8,128)(2,1)S(1)}, u32[]{:S(2)}) copy-start(bf16[128,256]{1,0:T(8,128)(2,1)S(1)} %collective-permute-done.21.refs_2_) | copy-start | bytes 196612
  71.6 8.3 %collective-permute-start.26 = (bf16[128,256]{1,0:T(8,128)(2,1)S(1)}, bf16[128,256]{1,0:T(8,128)(2,1)S(1)}, u32[]{:S(2)}, u32[]{:S(2)}) collective-permute-start(bf16[128,256]{1,0:T(8,128)(2,1)S(1)} %copy-done.37), channel_id=1, source_target_pairs={{0,6},{1,7},{2,0},{3,1},{4,2},{5,3},{6,4},{7,5},{8,14},{9,15},{10,... | collective-permute-start | bytes 196616 | tf_op jit(solution)/shard_map/ppermute | solution.py:284
  74.8 9.3 %collective-permute-start.27 = (bf16[128,256]{1,0:T(8,128)(2,1)S(1)}, bf16[128,256]{1,0:T(8,128)(2,1)S(1)}, u32[]{:S(2)}, u32[]{:S(2)}) collective-permute-start(bf16[128,256]{1,0:T(8,128)(2,1)S(1)} %copy-done.35), channel_id=1, source_target_pairs={{0,7},{1,0},{2,1},{3,2},{4,3},{5,4},{6,5},{7,6},{8,15},{9,8},{10,9... | collective-permute-start | bytes 196616 | tf_op jit(solution)/shard_map/ppermute | solution.py:284
  76.6 8.5 %collective-permute-start.7 = (bf16[128,256]{1,0:T(8,128)(2,1)S(1)}, bf16[128,256]{1,0:T(8,128)(2,1)S(1)}, u32[]{:S(2)}, u32[]{:S(2)}) collective-permute-start(bf16[128,256]{1,0:T(8,128)(2,1)S(1)} %copy-done.44), channel_id=1, source_target_pairs={{0,1},{1,2},{2,3},{3,4},{4,5},{5,6},{6,7},{7,0},{8,9},{9,10},{10,1... | collective-permute-start | bytes 196616 | tf_op jit(solution)/shard_map/ppermute | solution.py:284
  77.8 9.7 %collective-permute-start.8 = (bf16[128,256]{1,0:T(8,128)(2,1)S(1)}, bf16[128,256]{1,0:T(8,128)(2,1)S(1)}, u32[]{:S(2)}, u32[]{:S(2)}) collective-permute-start(bf16[128,256]{1,0:T(8,128)(2,1)S(1)} %copy-done.42), channel_id=1, source_target_pairs={{0,2},{1,3},{2,4},{3,5},{4,6},{5,7},{6,0},{7,1},{8,10},{9,11},{10,... | collective-permute-start | bytes 196616 | tf_op jit(solution)/shard_map/ppermute | solution.py:284
  79.1 10.6 %collective-permute-start.9 = (bf16[128,256]{1,0:T(8,128)(2,1)S(1)}, bf16[128,256]{1,0:T(8,128)(2,1)S(1)}, u32[]{:S(2)}, u32[]{:S(2)}) collective-permute-start(bf16[128,256]{1,0:T(8,128)(2,1)S(1)} %copy-done.40), channel_id=1, source_target_pairs={{0,3},{1,4},{2,5},{3,6},{4,7},{5,0},{6,1},{7,2},{8,11},{9,12},{10,... | collective-permute-start | bytes 196616 | tf_op jit(solution)/shard_map/ppermute | solution.py:284
  80.0 10.3 %collective-permute-start.10 = (bf16[128,256]{1,0:T(8,128)(2,1)S(1)}, bf16[128,256]{1,0:T(8,128)(2,1)S(1)}, u32[]{:S(2)}, u32[]{:S(2)}) collective-permute-start(bf16[128,256]{1,0:T(8,128)(2,1)S(1)} %copy-done.38), channel_id=1, source_target_pairs={{0,4},{1,5},{2,6},{3,7},{4,0},{5,1},{6,2},{7,3},{8,12},{9,13},{10,... | collective-permute-start | bytes 196616 | tf_op jit(solution)/shard_map/ppermute | solution.py:284
  84.1 8.9 %collective-permute-start.11 = (bf16[128,256]{1,0:T(8,128)(2,1)S(1)}, bf16[128,256]{1,0:T(8,128)(2,1)S(1)}, u32[]{:S(2)}, u32[]{:S(2)}) collective-permute-start(bf16[128,256]{1,0:T(8,128)(2,1)S(1)} %copy-done.36), channel_id=1, source_target_pairs={{0,5},{1,6},{2,7},{3,0},{4,1},{5,2},{6,3},{7,4},{8,13},{9,14},{10,... | collective-permute-start | bytes 196616 | tf_op jit(solution)/shard_map/ppermute | solution.py:284
  85.1 17.2 %collective-permute-start.30 = (f32[16,1024]{1,0:T(8,128)}, f32[16,1024]{1,0:T(8,128)S(1)}, u32[]{:S(2)}, u32[]{:S(2)}) collective-permute-start(f32[16,1024]{1,0:T(8,128)} %get-tuple-element.57), channel_id=1, source_target_pairs={{0,24},{8,16},{16,8},{24,0},{1,25},{9,17},{17,9},{25,1},{2,26},{10... | collective-permute-start | bytes 196616 | tf_op jit(solution)/shard_map/ppermute | solution.py:309
  87.6 15.8 %collective-permute-start.29 = (f32[16,1024]{1,0:T(8,128)}, f32[16,1024]{1,0:T(8,128)S(1)}, u32[]{:S(2)}, u32[]{:S(2)}) collective-permute-start(f32[16,1024]{1,0:T(8,128)} %get-tuple-element.57), channel_id=1, source_target_pairs={{0,16},{8,24},{16,0},{24,8},{1,17},{9,25},{17,1},{25,9},{2,18},{10... | collective-permute-start | bytes 196616 | tf_op jit(solution)/shard_map/ppermute | solution.py:309
  89.7 13.7 %collective-permute-start.28 = (f32[16,1024]{1,0:T(8,128)}, f32[16,1024]{1,0:T(8,128)S(1)}, u32[]{:S(2)}, u32[]{:S(2)}) collective-permute-start(f32[16,1024]{1,0:T(8,128)} %get-tuple-element.57), channel_id=1, source_target_pairs={{0,8},{8,0},{16,24},{24,16},{1,9},{9,1},{17,25},{25,17},{2,10},{10... | collective-permute-start | bytes 196616 | tf_op jit(solution)/shard_map/ppermute | solution.py:309
  90.3 6.2 %collective-permute-start.12 = (bf16[128,256]{1,0:T(8,128)(2,1)S(1)}, bf16[128,256]{1,0:T(8,128)(2,1)S(1)}, u32[]{:S(2)}, u32[]{:S(2)}) collective-permute-start(bf16[128,256]{1,0:T(8,128)(2,1)S(1)} %copy-done.34), channel_id=1, source_target_pairs={{0,6},{1,7},{2,0},{3,1},{4,2},{5,3},{6,4},{7,5},{8,14},{9,15},{10,... | collective-permute-start | bytes 196616 | tf_op jit(solution)/shard_map/ppermute | solution.py:284
  93.0 5.9 %collective-permute-start.13 = (bf16[128,256]{1,0:T(8,128)(2,1)S(1)}, bf16[128,256]{1,0:T(8,128)(2,1)S(1)}, u32[]{:S(2)}, u32[]{:S(2)}) collective-permute-start(bf16[128,256]{1,0:T(8,128)(2,1)S(1)} %copy-done.33), channel_id=1, source_target_pairs={{0,7},{1,0},{2,1},{3,2},{4,3},{5,4},{6,5},{7,6},{8,15},{9,8},{10,9... | collective-permute-start | bytes 196616 | tf_op jit(solution)/shard_map/ppermute | solution.py:284
  96.6 7.5 %collective-permute-start.33 = (f32[128,256]{1,0:T(8,128)}, f32[128,256]{1,0:T(8,128)S(1)}, u32[]{:S(2)}, u32[]{:S(2)}) collective-permute-start(f32[128,256]{1,0:T(8,128)} %get-tuple-element.58), channel_id=1, source_target_pairs={{0,24},{8,16},{16,8},{24,0},{1,25},{9,17},{17,9},{25,1},{2,26},{10... | collective-permute-start | bytes 393224 | tf_op jit(solution)/shard_map/ppermute | solution.py:309
  98.9 7.2 %collective-permute-start.32 = (f32[128,256]{1,0:T(8,128)}, f32[128,256]{1,0:T(8,128)S(1)}, u32[]{:S(2)}, u32[]{:S(2)}) collective-permute-start(f32[128,256]{1,0:T(8,128)} %get-tuple-element.58), channel_id=1, source_target_pairs={{0,16},{8,24},{16,0},{24,8},{1,17},{9,25},{17,1},{25,9},{2,18},{10... | collective-permute-start | bytes 393224 | tf_op jit(solution)/shard_map/ppermute | solution.py:309
  102.3 5.6 %collective-permute-start.31 = (f32[128,256]{1,0:T(8,128)S(1)}, f32[128,256]{1,0:T(8,128)S(1)}, u32[]{:S(2)}, u32[]{:S(2)}) collective-permute-start(f32[128,256]{1,0:T(8,128)S(1)} %copy-done.2), channel_id=1, source_target_pairs={{0,8},{8,0},{16,24},{24,16},{1,9},{9,1},{17,25},{25,17},{2,10},{10... | collective-permute-start | bytes 393224 | tf_op jit(solution)/shard_map/ppermute | solution.py:309
  (34 other events, 387.6 us)

commit v2 on v1

v2 whole, which is shorter than its diff:
```python
import functools
import math

import jax
import jax.numpy as jnp
import ml_dtypes
import numpy as np
from jax import lax
from jax.experimental import pallas as pl
from jax.experimental.pallas import tpu as pltpu
from jax.sharding import PartitionSpec as P

BF16 = jnp.bfloat16
F32 = jnp.float32
VMEM = pl.BlockSpec(memory_space=pltpu.VMEM)
SMEM = pl.BlockSpec(memory_space=pltpu.SMEM)
CHUNK = 32


def split_table(table):
    high = table.astype(ml_dtypes.bfloat16)
    low = (table - high.astype(np.float64)).astype(ml_dtypes.bfloat16)
    return high, low


def dft_tables(block):
    size = 2 * block
    steps = ((2 * np.arange(block)[:, None] + 1) * np.arange(block)[None, :]) % (2 * size)
    angle = steps * (math.pi / size)
    table = np.concatenate([np.cos(angle), -np.sin(angle)], axis=0)
    return split_table(table) + split_table(table.T * (2.0 / size))


def mm(a, b):
    return jnp.dot(a, b, preferred_element_type=F32)


def mm_nt(a, b):
    return lax.dot_general(a, b, (((1,), (1,)), ((), ())), preferred_element_type=F32)


def mm_tn(a, b):
    return lax.dot_general(a, b, (((0,), (0,)), ((), ())), preferred_element_type=F32)


def split(x):
    high = x.astype(BF16)
    return high, (x - high.astype(F32)).astype(BF16)


def inverse(rows_high, rows_low, high, low):
    return mm(rows_high, high) + mm(rows_low, high) + mm(rows_high, low)


def parity(width):
    row = lax.broadcasted_iota(jnp.int32, (CHUNK, width), 0)
    return (1 - 2 * (row % 2)).astype(F32)


def chunks(block, body):
    def step(index, carry):
        at = pl.multiple_of(index * CHUNK, CHUNK)
        body(pl.ds(at, CHUNK), pl.ds(block + at, CHUNK))
        return carry

    lax.fori_loop(0, block // CHUNK, step, 0)


def lanes(i, width):
    return slice(i * width, (i + 1) * width)


def place_of(me_ref, step, count, rows, width, block):
    at = lax.rem(me_ref[0] + step + count, count) * rows
    row = pl.multiple_of(lax.rem(at, block), rows)
    column = pl.multiple_of(lax.div(at, block) * width, 128)
    return pl.ds(row, rows), pl.ds(column, width)


def gather_blocks(me_ref, blocks, whole):
    (rows, width), count = blocks[0].shape, len(blocks)
    for shift, ref in enumerate(blocks):
        whole[place_of(me_ref, -shift, count, rows, width, whole.shape[0])] = ref[...]


def scatter_blocks(me_ref, whole, blocks):
    (rows, width), count = blocks[0].shape, len(blocks)
    for shift, ref in enumerate(blocks):
        ref[...] = whole[place_of(me_ref, shift, count, rows, width, whole.shape[0])]


def filters_kernel(
    taps, long_filter, member, gain, fwd_high, fwd_low, inv_high, inv_low,
    taps_spec, long_spec, both_spec, high, low,
):
    size, block = fwd_high.shape
    tap_count, width = taps.shape
    parts = long_spec.shape[1] // width
    sign = parity(width)
    taps_spec[...] = mm(fwd_high[:, :tap_count], taps[...]) + mm(fwd_low[:, :tap_count], taps[...])
    for d in range(parts):
        part_high, part_low = split(long_filter[:, d * block : (d + 1) * block])
        spread_high = mm_tn(part_high, member[...]).astype(BF16)
        spread_low = mm_tn(part_low, member[...]).astype(BF16)
        long_spec[:, lanes(d, width)] = inverse(
            fwd_high[...], fwd_low[...], spread_high, spread_low
        )

    def product(re, im):
        long_spec[re, lanes(0, width)] = long_spec[re, lanes(0, width)] + gain[...]
        w_re, w_im = taps_spec[re, :], taps_spec[im, :]
        for d in range(parts):
            here, last = lanes(d, width), lanes(d - 1, width)
            h_re, h_im = long_spec[re, here], long_spec[im, here]
            if d:
                h_re = h_re - sign * long_spec[im, last]
                h_im = h_im + sign * long_spec[re, last]
            high[re, here], low[re, here] = split(w_re * h_re - w_im * h_im)
            high[im, here], low[im, here] = split(w_re * h_im + w_im * h_re)

    chunks(block, product)
    both = inverse(inv_high[...], inv_low[...], high[...], low[...])
    both_high, both_low = split(both)
    both_spec[...] = inverse(fwd_high[...], fwd_low[...], both_high, both_low)

    def window(re, im):
        for d in reversed(range(1, parts)):
            here, last = lanes(d, width), lanes(d - 1, width)
            both_spec[re, here] = both_spec[re, here] - sign * both_spec[im, last]
            both_spec[im, here] = both_spec[im, here] + sign * both_spec[re, last]

    chunks(block, window)


def conv_kernel(count, backward, *refs):
    me_ref, blocks, refs = refs[0], refs[1 : 1 + count], refs[1 + count :]
    fwd_high, fwd_low, inv_high, inv_low, both_spec = refs[:5]
    outs, (spec, whole, high) = refs[5 : 5 + count], refs[5 + count :]
    size, block = fwd_high.shape
    width = blocks[0].shape[1]
    parts = spec.shape[1] // width
    gather_blocks(me_ref, blocks, whole)
    spec[...] = mm(fwd_high[...], whole[...]) + mm(fwd_low[...], whole[...])

    def product(re, im):
        for i in range(parts):
            sum_re = sum_im = 0.0
            for d in range(parts - i if backward else i + 1):
                there = lanes(i + d if backward else i - d, width)
                c_re, c_im = both_spec[re, lanes(d, width)], both_spec[im, lanes(d, width)]
                x_re, x_im = spec[re, there], spec[im, there]
                if backward:
                    sum_re = sum_re + (c_re * x_re + c_im * x_im)
                    sum_im = sum_im + (c_re * x_im - c_im * x_re)
                else:
                    sum_re = sum_re + (c_re * x_re - c_im * x_im)
                    sum_im = sum_im + (c_re * x_im + c_im * x_re)
            high[re, lanes(i, width)] = sum_re.astype(BF16)
            high[im, lanes(i, width)] = sum_im.astype(BF16)

    chunks(block, product)
    whole[...] = (mm(inv_high[...], high[...]) + mm(inv_low[...], high[...])).astype(BF16)
    scatter_blocks(me_ref, whole, outs)


def grads_kernel(
    grad_spec, series_spec, taps_spec, long_spec, member, fwd_high, fwd_low, inv_high, inv_low,
    out, lag_spec, high, total,
):
    size, block = fwd_high.shape
    groups, width = member.shape
    parts = grad_spec.shape[1] // width
    tap_count = out.shape[0] - 8 - parts * (block // width) * groups
    sign = parity(width)

    def correlate(re, im):
        next_re = next_im = None
        for d in reversed(range(parts)):
            p_re = p_im = 0.0
            for i in range(d, parts):
                here, there = lanes(i, width), lanes(i - d, width)
                g_re, g_im = grad_spec[re, here], grad_spec[im, here]
                x_re, x_im = series_spec[re, there], series_spec[im, there]
                p_re = p_re + (g_re * x_re + g_im * x_im)
                p_im = p_im + (g_im * x_re - g_re * x_im)
            q_re, q_im = p_re, p_im
            if next_re is not None:
                q_re = q_re + sign * next_im
                q_im = q_im - sign * next_re
            high[re, lanes(d, width)] = q_re.astype(BF16)
            high[im, lanes(d, width)] = q_im.astype(BF16)
            next_re, next_im = p_re, p_im

    chunks(block, correlate)
    folded = high[:, : parts * width]
    lags = (mm(inv_high[...], folded) + mm(inv_low[...], folded)).astype(BF16)
    lag_spec[...] = mm(fwd_high[...], lags) + mm(fwd_low[...], lags)
    total[...] = jnp.zeros_like(total)

    def filtered(re, im):
        w_re, w_im = taps_spec[re, :], taps_spec[im, :]
        sum_re = sum_im = 0.0
        for d in range(parts):
            here, after = lanes(d, width), lanes(d + 1, width)
            r_re, r_im = lag_spec[re, here], lag_spec[im, here]
            if d + 1 < parts:
                r_re = r_re + sign * lag_spec[im, after]
                r_im = r_im - sign * lag_spec[re, after]
            h_re, h_im = long_spec[re, here], long_spec[im, here]
            sum_re = sum_re + (h_re * r_re + h_im * r_im)
            sum_im = sum_im + (h_re * r_im - h_im * r_re)
            v_re = w_re * r_re + w_im * r_im
            if d == 0:
                total[...] += v_re
            high[re, here] = v_re.astype(BF16)
            high[im, here] = (w_re * r_im - w_im * r_re).astype(BF16)
        last = lanes(parts, width)
        high[re, last] = sum_re.astype(BF16)
        high[im, last] = sum_im.astype(BF16)

    chunks(block, filtered)
    last = high[:, parts * width :]
    out[:tap_count, :] = mm(inv_high[:tap_count, :], last) + mm(inv_low[:tap_count, :], last)
    skip = jnp.sum(total[...], axis=0, keepdims=True) * (2.0 / size)
    out[pl.ds(tap_count, 8), :] = jnp.broadcast_to(skip, (8, width))
    at = tap_count + 8
    for d in range(parts):
        summed = mm_nt(member[...], high[:, lanes(d, width)]) * (2.0 / size)
        sum_high, sum_low = split(summed)
        part = mm(sum_high, fwd_high[...]) + mm(sum_high, fwd_low[...]) + mm(sum_low, fwd_high[...])
        for piece in range(block // width):
            out[pl.ds(at, groups), :] = part[:, lanes(piece, width)]
            at += groups


def gate_kernel(count, *refs):
    me_ref, blocks, refs = refs[0], refs[1 : 1 + count], refs[1 + count :]
    gating, upstream, output, gate_grad = refs
    width = blocks[0].shape[1]
    for shift, ref in enumerate(blocks):
        source = lax.rem(me_ref[0] + (count - shift), count)
        columns = pl.ds(pl.multiple_of(source * width, width), width)
        conv = ref[...].astype(F32)
        output[:, columns] = (gating[:, columns].astype(F32) * conv).astype(BF16)
        gate_grad[:, columns] = (upstream[:, columns].astype(F32) * conv).astype(BF16)


def place_kernel(count, *refs):
    me_ref, blocks, out = refs[0], refs[1 : 1 + count], refs[-1]
    width = blocks[0].shape[1]
    for shift, ref in enumerate(blocks):
        source = lax.rem(me_ref[0] + (count - shift), count)
        out[:, pl.ds(pl.multiple_of(source * width, width), width)] = ref[...]


def call(kernel, operands, outs, scratch, budget, micros, name):
    moved = sum(math.prod(x.shape) * x.dtype.itemsize for x in [*operands, *outs])
    return pl.pallas_call(
        kernel,
        out_shape=outs,
        in_specs=[SMEM if x.dtype == jnp.int32 else VMEM for x in operands],
        out_specs=[VMEM for _ in outs],
        scratch_shapes=[pltpu.VMEM(shape, dtype) for shape, dtype in scratch],
        compiler_params=pltpu.CompilerParams(vmem_limit_bytes=budget),
        cost_estimate=pl.CostEstimate(
            flops=int(micros * 1e9), transcendentals=0, bytes_accessed=moved
        ),
        name=name,
    )(*operands)


def exchange(blocks, axis):
    count = len(blocks)
    return [blocks[0]] + [
        lax.ppermute(blocks[k], axis, [(i, (i + k) % count) for i in range(count)])
        for k in range(1, count)
    ]


def columns_for(rows, me, count):
    width = rows.shape[1] // count
    return [
        lax.dynamic_slice_in_dim(rows, lax.rem(me + k, count) * width, width, 1)
        for k in range(count)
    ]


def in_order(blocks, me):
    count = len(blocks)
    order = lax.rem(me + count - jnp.arange(count), count)
    ordered = jnp.take(jnp.stack(blocks), order, axis=0)
    return jnp.transpose(ordered, (1, 0, 2)).reshape(blocks[0].shape[0], -1)


def sum_over(value, axis):
    if lax.axis_size(axis) != 4:
        return lax.psum(value, axis)
    a, b, c = (lax.ppermute(value, axis, [(i, i ^ flip) for i in range(4)]) for flip in (1, 2, 3))
    return (value + a) + (b + c)


def local(signal, gate_input, cotangent, long_filter, short_taps, skip_gain):
    series = signal[0]
    gating = gate_input[0]
    upstream = cotangent[0]
    rows, channels = series.shape
    count = lax.axis_size("ctx")
    me = lax.axis_index("ctx")
    where = me.astype(jnp.int32).reshape(1)
    length = rows * count
    width = channels // count
    padded = -(-width // 128) * 128
    groups = long_filter.shape[0]
    tap_count = short_taps.shape[0]
    block = min(length // 4, 512)
    size = 2 * block
    parts = length // block

    def pad(x):
        return jnp.pad(x, ((0, 0), (0, padded - width))) if padded > width else x

    def trim(blocks):
        return [x[:, :width] if padded > width else x for x in blocks]

    grad_gate = (upstream.astype(F32) * gating.astype(F32)).astype(BF16)
    series_in = exchange(columns_for(series, me, count), "ctx")
    grad_in = exchange(columns_for(grad_gate, me, count), "ctx")

    tables = [jnp.asarray(t) for t in dft_tables(block)]
    channel = np.arange(padded)[None, :]
    of_group = (channel // (width // groups) == np.arange(groups)[:, None]) & (channel < width)
    member = jnp.asarray(of_group.astype(ml_dtypes.bfloat16))
    own_taps = pad(lax.dynamic_slice_in_dim(short_taps, me * width, width, 1))
    spectrum = (size, parts * padded)
    spectrum_out = jax.ShapeDtypeStruct(spectrum, F32)
    budget = 10 * 4 * math.prod(spectrum)
    taps_spec, long_spec, both_spec = call(
        filters_kernel,
        [own_taps, long_filter, member, pad(skip_gain[None, :]), *tables],
        [jax.ShapeDtypeStruct((size, padded), F32), spectrum_out, spectrum_out],
        [(spectrum, BF16), (spectrum, BF16)],
        budget,
        5,
        "filters",
    )

    def convolve(blocks, backward, name):
        *outs, spec = call(
            functools.partial(conv_kernel, count, backward),
            [where, *[pad(x) for x in blocks], *tables, both_spec],
            [jax.ShapeDtypeStruct((rows, padded), BF16)] * count + [spectrum_out],
            [((block, parts * padded), BF16), (spectrum, BF16)],
            budget,
            4,
            name,
        )
        return trim(outs), spec

    conv, series_spec = convolve(series_in, False, "conv")
    conv_in = exchange(conv, "ctx")
    grad_in, conv = lax.optimization_barrier((grad_in, conv))
    grad, grad_spec = convolve(grad_in, True, "back")
    signal_in = exchange(grad, "ctx")
    pieces = parts * (block // padded)
    (partial,) = call(
        grads_kernel,
        [grad_spec, series_spec, taps_spec, long_spec, member, *tables],
        [jax.ShapeDtypeStruct((tap_count + 8 + pieces * groups, padded), F32)],
        [(spectrum, F32), ((size, (parts + 1) * padded), BF16), ((CHUNK, padded), F32)],
        budget,
        5,
        "grads",
    )
    total = sum_over(partial, "dp") * (1.0 / math.sqrt(lax.axis_size("dp") * length))
    taps_grad = total[:tap_count, :width]
    skip_grad = total[tap_count, :width]
    long_grad = total[tap_count + 8 :].reshape(pieces, groups, padded)
    long_grad = jnp.transpose(long_grad, (1, 0, 2)).reshape(groups, length)

    full = jax.ShapeDtypeStruct((rows, channels), BF16)
    if width % 128 == 0:
        output, gate_grad = call(
            functools.partial(gate_kernel, count),
            [where, *conv_in, gating, upstream],
            [full, full],
            [],
            budget,
            1,
            "gate",
        )
        (signal_grad,) = call(
            functools.partial(place_kernel, count),
            [where, *signal_in],
            [full],
            [],
            budget,
            1,
            "place",
        )
    else:
        conv_rows = in_order(conv_in, me).astype(F32)
        output = (gating.astype(F32) * conv_rows).astype(BF16)
        gate_grad = (upstream.astype(F32) * conv_rows).astype(BF16)
        signal_grad = in_order(signal_in, me)
    return (output[None], gate_grad[None], signal_grad[None], long_grad, taps_grad, skip_grad)


def solution(mesh):
    return jax.shard_map(
        local,
        mesh=mesh,
        in_specs=(
            P("dp", "ctx", None),
            P("dp", "ctx", None),
            P("dp", "ctx", None),
            P("ctx", None),
            P(),
            P("ctx"),
        ),
        out_specs=(
            P("dp", "ctx", None),
            P("dp", "ctx", None),
            P("dp", "ctx", None),
            P("ctx", None),
            P(None, "ctx"),
            P("ctx"),
        ),
        check_vma=False,
    )
```

time: 109 us -> 77.4 us (0.71)
  Pallas kernels: 37.3 us -> 16.4 us
  starting transfers between devices: 50.3 us -> 36.6 us
  waiting for transfers between devices: 11 us -> 19.6 us
  other arithmetic: 5.04 us -> 1.54 us
  local copies, waits for them, and re-layouts: 3.78 us -> 2.1 us
    pallas_call x6, Pallas kernels: 37.3 us -> 16.4 us  [call(): pl.pallas_call(kernel, out_shape=outs, in_specs=[SMEM if x.dtype == jnp.i...]
    ppermute x28, waiting for transfers between devices: 4.43 us -> 16.4 us  [exchange(): lax.ppermute(blocks[k], axis, [(i, (i + k) % count) for i in range(count)])]
    ppermute x9 -> x3, starting transfers between devices: 10.6 us -> 3.55 us  [sum_over(): lax.ppermute(value, axis, [(i, i ^ flip) for i in range(4)])]
    ppermute x28, starting transfers between devices: 39.7 us -> 33.1 us  [exchange(): lax.ppermute(blocks[k], axis, [(i, (i + k) % count) for i in range(count)])]
    ppermute x9 -> x3, waiting for transfers between devices: 6.61 us -> 3.21 us  [sum_over(): lax.ppermute(value, axis, [(i, i ^ flip) for i in range(4)])]
    mul x3 -> x1, other arithmetic: 2.59 us -> 0.06 us  [local(): sum_over(partial, 'dp') * (1.0 / math.sqrt(lax.axis_size('dp') * length))]
    dynamic_slice x2, local copies, waits for them, and re-layouts: 1.49 us -> 0.16 us  [columns_for(): lax.dynamic_slice_in_dim(rows, lax.rem(me + k, count) * width, width, 1)]
    slice x0 -> x3, local copies, waits for them, and re-layouts: none -> 1.23 us  [the longest x1 0.66 us: local(): taps_grad = total[:tap_count, :width]]
  transfers between devices with their start and end apart: 37 -> 31, of which waited for: 7 -> 10; matrix products, arithmetic and copies ran while one was open for 4% -> 0% of each run, Pallas kernels for 34% -> 18%
where the time goes in v2:
time: 77.4 us; the launch traced here: 77.2 us
  starting transfers between devices  36.6 us (47%)
  waiting for transfers between devices  19.6 us (25%)
  Pallas kernels  16.4 us (21%)
  local copies, waits for them, and re-layouts  2.1 us (3%)
  other arithmetic  1.54 us (2%)
  between operations  0.93 us (1%)
    ppermute x28, starting transfers between devices, exchange(): lax.ppermute(blocks[k], axis, [(i, (i + k) % count) for i in range(count)])  33.1 us
    ppermute x28, waiting for transfers between devices, exchange(): lax.ppermute(blocks[k], axis, [(i, (i + k) % count) for i in range(count)])  16.4 us
    pallas_call x6, Pallas kernels, call(): pl.pallas_call(kernel, out_shape=outs, in_specs=[SMEM if x.dtype == jnp.i...  16.4 us
    ppermute x3, starting transfers between devices, sum_over(): lax.ppermute(value, axis, [(i, i ^ flip) for i in range(4)])  3.55 us
    ppermute x3, waiting for transfers between devices, sum_over(): lax.ppermute(value, axis, [(i, i ^ flip) for i in range(4)])  3.21 us
  transfers between devices with their start and end apart: 31, of which 10 were waited for; matrix products, arithmetic and copies ran while one was open for 0% of the time, Pallas kernels for 18%

profile of v2, /device:TPU:0, one launch (start us, length us, event | category | flops | bytes accessed | tf_op | source)
XLA Modules:
  0.0 77.2 jit_solution(5564808155655317281)
XLA Ops:
  0.8 1.5 %multiply_convert_fusion = bf16[128,2048]{1,0:T(8,128)(2,1)S(1)} fusion(bf16[1,128,2048]{2,1,0:T(8,128)(2,1)} %param.13, bf16[1,128,2048]{2,1,0:T(8,128)(2,1)} %param.12), kind=kLoop, calls=%fused_computation | loop fusion | flops 1048576 | bytes 1572864 | tf_op jit(solution)/shard_map/convert_element_type | solution.py:325
  2.3 0.1 constant_dynamic-slice_fusion
  2.4 4.5 %collective-permute-start.20 = (bf16[128,256]{1,0:T(8,128)(2,1)S(1)}, bf16[128,256]{1,0:T(8,128)(2,1)S(1)}, u32[]{:S(2)}, u32[]{:S(2)}) collective-permute-start(bf16[128,256]{1,0:T(8,128)(2,1)S(1)} %get-tuple-element.68), channel_id=1, source_target_pairs={{0,7},{1,0},{2,1},{3,2},{4,3},{5,4},{6,5},{7,6},{8,15},{9,8},{10,9... | collective-permute-start | bytes 196616 | tf_op jit(solution)/shard_map/ppermute | solution.py:275
  6.9 0.6 collective-permute-start.19
  7.5 0.1 dynamic-slice_bitcast_fusion
  7.6 0.3 collective-permute-start.6
  7.9 2.8 %collective-permute-start.3 = (bf16[128,256]{1,0:T(8,128)(2,1)S(1)}, bf16[128,256]{1,0:T(8,128)(2,1)S(1)}, u32[]{:S(2)}, u32[]{:S(2)}) collective-permute-start(bf16[128,256]{1,0:T(8,128)(2,1)S(1)} %get-tuple-element.78), channel_id=1, source_target_pairs={{0,4},{1,5},{2,6},{3,7},{4,0},{5,1},{6,2},{7,3},{8,12},{9,13},{10,... | collective-permute-start | bytes 196616 | tf_op jit(solution)/shard_map/ppermute | solution.py:275
  10.7 0.1 collective-permute-start.2
  10.8 0.8 collective-permute-done.19.refs_7_
  11.6 0.7 collective-permute-start.1
  12.3 0.5 collective-permute-start
  12.8 0.5 collective-permute-done.4.refs_6_
  13.3 2.8 %collective-permute-start.5 = (bf16[128,256]{1,0:T(8,128)(2,1)S(1)}, bf16[128,256]{1,0:T(8,128)(2,1)S(1)}, u32[]{:S(2)}, u32[]{:S(2)}) collective-permute-start(bf16[128,256]{1,0:T(8,128)(2,1)S(1)} %get-tuple-element.83), channel_id=1, source_target_pairs={{0,6},{1,7},{2,0},{3,1},{4,2},{5,3},{6,4},{7,5},{8,14},{9,15},{10,... | collective-permute-start | bytes 196616 | tf_op jit(solution)/shard_map/ppermute | solution.py:275
  16.1 5.7 %filters.1 = (f32[512,256]{1,0:T(8,128)S(1)}, f32[512,1024]{1,0:T(8,128)S(1)}, f32[512,1024]{1,0:T(8,128)S(1)}) custom-call(bf16[128,256]{1,0:T(8,128)(2,1)S(1)} %constant_dynamic-slice_fusion.8.taps, f32[16,1024]{1,0:T(8,128)S(1)} %copy-done.3, bf16[16,256]{1,0:T(8,128)(2,1)S(1)} %copy-done.9, f32[1,256]{1,0:T(1,128)S(1)} %bitcast.33, ...), custom_call_target="tpu_custom_call" | custom-call | flops 5000000000 | bytes 5907456 | tf_op jit(solution)/shard_map/filters/pallas_call | solution.py:258
  21.8 1.1 %collective-permute-start.18 = (bf16[128,256]{1,0:T(8,128)(2,1)S(1)}, bf16[128,256]{1,0:T(8,128)(2,1)S(1)}, u32[]{:S(2)}, u32[]{:S(2)}) collective-permute-start(bf16[128,256]{1,0:T(8,128)(2,1)S(1)} %get-tuple-element.70), channel_id=1, source_target_pairs={{0,5},{1,6},{2,7},{3,0},{4,1},{5,2},{6,3},{7,4},{8,13},{9,14},{10,... | collective-permute-start | bytes 196616 | tf_op jit(solution)/shard_map/ppermute | solution.py:275
  22.9 5.3 %collective-permute-start.17 = (bf16[128,256]{1,0:T(8,128)(2,1)S(1)}, bf16[128,256]{1,0:T(8,128)(2,1)S(1)}, u32[]{:S(2)}, u32[]{:S(2)}) collective-permute-start(bf16[128,256]{1,0:T(8,128)(2,1)S(1)} %get-tuple-element.71), channel_id=1, source_target_pairs={{0,4},{1,5},{2,6},{3,7},{4,0},{5,1},{6,2},{7,3},{8,12},{9,13},{10,... | collective-permute-start | bytes 196616 | tf_op jit(solution)/shard_map/ppermute | solution.py:275
  28.2 1.1 %collective-permute-start.15 = (bf16[128,256]{1,0:T(8,128)(2,1)S(1)}, bf16[128,256]{1,0:T(8,128)(2,1)S(1)}, u32[]{:S(2)}, u32[]{:S(2)}) collective-permute-start(bf16[128,256]{1,0:T(8,128)(2,1)S(1)} %get-tuple-element.73), channel_id=1, source_target_pairs={{0,2},{1,3},{2,4},{3,5},{4,6},{5,7},{6,0},{7,1},{8,10},{9,11},{10,... | collective-permute-start | bytes 196616 | tf_op jit(solution)/shard_map/ppermute | solution.py:275
  29.3 2.3 %conv.1 = (bf16[128,256]{1,0:T(8,128)(2,1)S(1)}, bf16[128,256]{1,0:T(8,128)(2,1)S(1)}, bf16[128,256]{1,0:T(8,128)(2,1)S(1)}, bf16[128,256]{1,0:T(8,128)(2,1)S(1)...) custom-call(s32[1]{0:T(128)} %bitcast.refs_0_, ...), custom_call_target="tpu_custom_call" | custom-call | flops 4000000000 | bytes 6291460 | tf_op jit(solution)/shard_map/conv/pallas_call | solution.py:258
  31.6 6.0 %collective-permute-done.17.refs_5_ = bf16[128,256]{1,0:T(8,128)(2,1)S(1)} collective-permute-done((bf16[128,256]{1,0:T(8,128)(2,1)S(1)}, bf16[128,256]{1,0:T(8,128)(2,1)S(1)}, u32[]{:S(2)}, u32[]{:S(2)}) %collective-permute-start.17) | collective-permute-done | bytes 65568 | tf_op jit(solution)/shard_map/ppermute | solution.py:275
  37.7 2.4 %back.1 = (bf16[128,256]{1,0:T(8,128)(2,1)S(1)}, bf16[128,256]{1,0:T(8,128)(2,1)S(1)}, bf16[128,256]{1,0:T(8,128)(2,1)S(1)}, bf16[128,256]{1,0:T(8,128)(2,1)S(1)...) custom-call(s32[1]{0:T(128)} %bitcast.refs_0_, ...), custom_call_target="tpu_custom_call" | custom-call | flops 4000000000 | bytes 6291460 | tf_op jit(solution)/shard_map/back/pallas_call | solution.py:258
  40.1 0.1 collective-permute-start.21
  40.2 0.1 collective-permute-start.22
  40.2 0.1 collective-permute-start.23
  40.3 4.0 %collective-permute-start.24 = (bf16[128,256]{1,0:T(8,128)(2,1)S(1)}, bf16[128,256]{1,0:T(8,128)(2,1)S(1)}, u32[]{:S(2)}, u32[]{:S(2)}) collective-permute-start(bf16[128,256]{1,0:T(8,128)(2,1)S(1)} %get-tuple-element.60), channel_id=1, source_target_pairs={{0,4},{1,5},{2,6},{3,7},{4,0},{5,1},{6,2},{7,3},{8,12},{9,13},{10,... | collective-permute-start | bytes 196616 | tf_op jit(solution)/shard_map/ppermute | solution.py:275
  44.3 1.5 %collective-permute-done.21.refs_2_ = bf16[128,256]{1,0:T(8,128)(2,1)S(1)} collective-permute-done((bf16[128,256]{1,0:T(8,128)(2,1)S(1)}, bf16[128,256]{1,0:T(8,128)(2,1)S(1)}, u32[]{:S(2)}, u32[]{:S(2)}) %collective-permute-start.21) | collective-permute-done | bytes 65568 | tf_op jit(solution)/shard_map/ppermute | solution.py:275
  45.8 1.1 %collective-permute-start.26 = (bf16[128,256]{1,0:T(8,128)(2,1)S(1)}, bf16[128,256]{1,0:T(8,128)(2,1)S(1)}, u32[]{:S(2)}, u32[]{:S(2)}) collective-permute-start(bf16[128,256]{1,0:T(8,128)(2,1)S(1)} %get-tuple-element.62), channel_id=1, source_target_pairs={{0,6},{1,7},{2,0},{3,1},{4,2},{5,3},{6,4},{7,5},{8,14},{9,15},{10,... | collective-permute-start | bytes 196616 | tf_op jit(solution)/shard_map/ppermute | solution.py:275
  46.9 0.1 collective-permute-done.22.refs_3_
  47.0 5.0 %collective-permute-done.23.refs_4_ = bf16[128,256]{1,0:T(8,128)(2,1)S(1)} collective-permute-done((bf16[128,256]{1,0:T(8,128)(2,1)S(1)}, bf16[128,256]{1,0:T(8,128)(2,1)S(1)}, u32[]{:S(2)}, u32[]{:S(2)}) %collective-permute-start.23) | collective-permute-done | bytes 65568 | tf_op jit(solution)/shard_map/ppermute | solution.py:275
  52.0 0.1 collective-permute-done.24.refs_5_
  52.1 1.2 %collective-permute-start.8 = (bf16[128,256]{1,0:T(8,128)(2,1)S(1)}, bf16[128,256]{1,0:T(8,128)(2,1)S(1)}, u32[]{:S(2)}, u32[]{:S(2)}) collective-permute-start(bf16[128,256]{1,0:T(8,128)(2,1)S(1)} %get-tuple-element.40), channel_id=1, source_target_pairs={{0,2},{1,3},{2,4},{3,5},{4,6},{5,7},{6,0},{7,1},{8,10},{9,11},{10,... | collective-permute-start | bytes 196616 | tf_op jit(solution)/shard_map/ppermute | solution.py:275
  53.3 0.0 collective-permute-start.9
  53.3 3.8 %collective-permute-start.10 = (bf16[128,256]{1,0:T(8,128)(2,1)S(1)}, bf16[128,256]{1,0:T(8,128)(2,1)S(1)}, u32[]{:S(2)}, u32[]{:S(2)}) collective-permute-start(bf16[128,256]{1,0:T(8,128)(2,1)S(1)} %get-tuple-element.42), channel_id=1, source_target_pairs={{0,4},{1,5},{2,6},{3,7},{4,0},{5,1},{6,2},{7,3},{8,12},{9,13},{10,... | collective-permute-start | bytes 196616 | tf_op jit(solution)/shard_map/ppermute | solution.py:275
  57.2 1.9 %collective-permute-start.11 = (bf16[128,256]{1,0:T(8,128)(2,1)S(1)}, bf16[128,256]{1,0:T(8,128)(2,1)S(1)}, u32[]{:S(2)}, u32[]{:S(2)}) collective-permute-start(bf16[128,256]{1,0:T(8,128)(2,1)S(1)} %get-tuple-element.43), channel_id=1, source_target_pairs={{0,5},{1,6},{2,7},{3,0},{4,1},{5,2},{6,3},{7,4},{8,13},{9,14},{10,... | collective-permute-start | bytes 196616 | tf_op jit(solution)/shard_map/ppermute | solution.py:275
  59.0 3.9 %grads.1 = f32[200,256]{1,0:T(8,128)S(1)} custom-call(f32[512,1024]{1,0:T(8,128)S(1)} %get-tuple-element.64.grad_spec, f32[512,1024]{1,0:T(8,128)S(1)} %get-tuple-element.65.series_spec, f32[512,256]{1,0:T(8,128)S(1)} %get-tuple-element.66.taps_spec, f32[512,1024]{1,0:T(8,128)S(1)} %get-tuple-element.67.long_spec, bf16[16,256]{1,0:T(8,128)(2,1)S(1)} %copy-done.9, ...), custom_call_target="tpu_custom_call" | custom-call | flops 5000000000 | bytes 8077312 | tf_op jit(solution)/shard_map/grads/pallas_call | solution.py:258
  63.0 0.0 collective-permute-done.7.refs_2_
  63.0 2.5 %collective-permute-start.30 = (f32[200,256]{1,0:T(8,128)S(1)}, f32[200,256]{1,0:T(8,128)S(1)}, u32[]{:S(2)}, u32[]{:S(2)}) collective-permute-start(f32[200,256]{1,0:T(8,128)S(1)} %grads.1), channel_id=1, source_target_pairs={{0,24},{8,16},{16,8},{24,0},{1,25},{9,17},{17,9},{25,1},{2,26},{10... | collective-permute-start | bytes 614408 | tf_op jit(solution)/shard_map/ppermute | solution.py:298
  65.5 0.5 collective-permute-start.29
  66.0 0.5 collective-permute-start.28
  66.5 1.0 %collective-permute-start.12 = (bf16[128,256]{1,0:T(8,128)(2,1)S(1)}, bf16[128,256]{1,0:T(8,128)(2,1)S(1)}, u32[]{:S(2)}, u32[]{:S(2)}) collective-permute-start(bf16[128,256]{1,0:T(8,128)(2,1)S(1)} %get-tuple-element.44), channel_id=1, source_target_pairs={{0,6},{1,7},{2,0},{3,1},{4,2},{5,3},{6,4},{7,5},{8,14},{9,15},{10,... | collective-permute-start | bytes 196616 | tf_op jit(solution)/shard_map/ppermute | solution.py:275
  67.6 0.9 %place.1 = bf16[128,2048]{1,0:T(8,128)(2,1)} custom-call(s32[1]{0:T(128)} %bitcast.refs_0_, bf16[128,256]{1,0:T(8,128)(2,1)S(1)} %get-tuple-element.56.refs_1_, bf16[128,256]{1,0:T(8,128)(2,1)S(1)} %collective-permute-done.21.refs_2_, bf16[128,256]{1,0:T(8,128)(2,1)S(1)} %collective-permute-done.22.refs_3_, ...), custom_call_target="tpu_custom_call" | custom-call | flops 1000000000 | bytes 1048580 | tf_op jit(solution)/shard_map/place/pallas_call | solution.py:258
  68.4 2.4 %collective-permute-done.12.refs_7_ = bf16[128,256]{1,0:T(8,128)(2,1)S(1)} collective-permute-done((bf16[128,256]{1,0:T(8,128)(2,1)S(1)}, bf16[128,256]{1,0:T(8,128)(2,1)S(1)}, u32[]{:S(2)}, u32[]{:S(2)}) %collective-permute-start.12) | collective-permute-done | bytes 65568 | tf_op jit(solution)/shard_map/ppermute | solution.py:275
  70.8 1.3 %gate.1 = (bf16[128,2048]{1,0:T(8,128)(2,1)}, bf16[128,2048]{1,0:T(8,128)(2,1)}) custom-call(s32[1]{0:T(128)} %bitcast.refs_0_, bf16[128,256]{1,0:T(8,128)(2,1)S(1)} %get-tuple-element.38.refs_1_, bf16[128,256]{1,0:T(8,128)(2,1)S(1)} %collective-permute-done.7.refs_2_, bf16[128,256]{1,0:T(8,128)(2,1)S(1)} %collective-permute-done.8.refs_3_, ...), custom_call_target="tpu_custom_call" | custom-call | flops 1000000000 | bytes 2621444 | tf_op jit(solution)/shard_map/gate/pallas_call | solution.py:258
  72.1 3.1 %collective-permute-done.29 = f32[200,256]{1,0:T(8,128)S(1)} collective-permute-done((f32[200,256]{1,0:T(8,128)S(1)}, f32[200,256]{1,0:T(8,128)S(1)}, u32[]{:S(2)}, u32[]{:S(2)}) %collective-permute-start.29) | collective-permute-done | bytes 204832 | tf_op jit(solution)/shard_map/ppermute | solution.py:298
  75.2 0.1 collective-permute-done.28
  75.3 0.1 add_multiply_fusion
  75.3 0.6 slice.14
  75.9 0.7 slice.13
  76.6 0.6 copy.18
  (51 shorter events, 0.1 us)
Async XLA Ops:
  0.6 10.1 %copy-start = (bf16[128,2048]{1,0:T(8,128)(2,1)S(1)}, bf16[128,2048]{1,0:T(8,128)(2,1)}, u32[]{:S(2)}) copy-start(bf16[128,2048]{1,0:T(8,128)(2,1)} %param.15) | copy-start | bytes 1572868
  0.6 15.4 %copy-start.5 = (bf16[256,512]{1,0:T(8,128)(2,1)S(1)}, bf16[256,512]{1,0:T(8,128)(2,1)}, u32[]{:S(2)}) copy-start(bf16[256,512]{1,0:T(8,128)(2,1)} %constant.64.clone.inv_low.refs_12_) | copy-start | bytes 786436
  0.7 15.4 %copy-start.6 = (bf16[256,512]{1,0:T(8,128)(2,1)S(1)}, bf16[256,512]{1,0:T(8,128)(2,1)}, u32[]{:S(2)}) copy-start(bf16[256,512]{1,0:T(8,128)(2,1)} %constant.63.clone.inv_high.refs_11_) | copy-start | bytes 786436
  0.7 15.4 %copy-start.7 = (bf16[512,256]{1,0:T(8,128)(2,1)S(1)}, bf16[512,256]{1,0:T(8,128)(2,1)}, u32[]{:S(2)}) copy-start(bf16[512,256]{1,0:T(8,128)(2,1)} %constant.62.clone.fwd_low.refs_10_) | copy-start | bytes 786436
  0.7 15.4 %copy-start.8 = (bf16[512,256]{1,0:T(8,128)(2,1)S(1)}, bf16[512,256]{1,0:T(8,128)(2,1)}, u32[]{:S(2)}) copy-start(bf16[512,256]{1,0:T(8,128)(2,1)} %constant.61.clone.fwd_high.refs_9_) | copy-start | bytes 786436
  0.7 15.4 %copy-start.9 = (bf16[16,256]{1,0:T(8,128)(2,1)S(1)}, bf16[16,256]{1,0:T(8,128)(2,1)}, u32[]{:S(2)}) copy-start(bf16[16,256]{1,0:T(8,128)(2,1)} %constant.65.clone.member) | copy-start | bytes 24580
  0.7 6.8 %copy-start.10 = (bf16[1,128,2048]{2,1,0:T(8,128)(2,1)S(1)}, bf16[1,128,2048]{2,1,0:T(8,128)(2,1)}, u32[]{:S(2)}) copy-start(bf16[1,128,2048]{2,1,0:T(8,128)(2,1)} %param.11) | copy-start | bytes 1572868
  0.7 15.3 %copy-start.4 = (f32[256]{0:T(256)S(1)}, f32[256]{0:T(256)}, u32[]{:S(2)}) copy-start(f32[256]{0:T(256)} %param.16) | copy-start | bytes 3076
  0.7 15.3 %copy-start.3 = (f32[16,1024]{1,0:T(8,128)S(1)}, f32[16,1024]{1,0:T(8,128)}, u32[]{:S(2)}) copy-start(f32[16,1024]{1,0:T(8,128)} %long_filter.1) | copy-start | bytes 196612
  2.4 8.4 %collective-permute-start.20 = (bf16[128,256]{1,0:T(8,128)(2,1)S(1)}, bf16[128,256]{1,0:T(8,128)(2,1)S(1)}, u32[]{:S(2)}, u32[]{:S(2)}) collective-permute-start(bf16[128,256]{1,0:T(8,128)(2,1)S(1)} %get-tuple-element.68), channel_id=1, source_target_pairs={{0,7},{1,0},{2,1},{3,2},{4,3},{5,4},{6,5},{7,6},{8,15},{9,8},{10,9... | collective-permute-start | bytes 196616 | tf_op jit(solution)/shard_map/ppermute | solution.py:275
  6.9 4.7 %collective-permute-start.19 = (bf16[128,256]{1,0:T(8,128)(2,1)S(1)}, bf16[128,256]{1,0:T(8,128)(2,1)S(1)}, u32[]{:S(2)}, u32[]{:S(2)}) collective-permute-start(bf16[128,256]{1,0:T(8,128)(2,1)S(1)} %get-tuple-element.69), channel_id=1, source_target_pairs={{0,6},{1,7},{2,0},{3,1},{4,2},{5,3},{6,4},{7,5},{8,14},{9,15},{10,... | collective-permute-start | bytes 196616 | tf_op jit(solution)/shard_map/ppermute | solution.py:275
  7.6 4.7 %collective-permute-start.6 = (bf16[128,256]{1,0:T(8,128)(2,1)S(1)}, bf16[128,256]{1,0:T(8,128)(2,1)S(1)}, u32[]{:S(2)}, u32[]{:S(2)}) collective-permute-start(bf16[128,256]{1,0:T(8,128)(2,1)S(1)} %get-tuple-element.76), channel_id=1, source_target_pairs={{0,7},{1,0},{2,1},{3,2},{4,3},{5,4},{6,5},{7,6},{8,15},{9,8},{10,9... | collective-permute-start | bytes 196616 | tf_op jit(solution)/shard_map/ppermute | solution.py:275
  7.9 5.4 %collective-permute-start.4 = (bf16[128,256]{1,0:T(8,128)(2,1)S(1)}, bf16[128,256]{1,0:T(8,128)(2,1)S(1)}, u32[]{:S(2)}, u32[]{:S(2)}) collective-permute-start(bf16[128,256]{1,0:T(8,128)(2,1)S(1)} %get-tuple-element.77), channel_id=1, source_target_pairs={{0,5},{1,6},{2,7},{3,0},{4,1},{5,2},{6,3},{7,4},{8,13},{9,14},{10,... | collective-permute-start | bytes 196616 | tf_op jit(solution)/shard_map/ppermute | solution.py:275
  7.9 13.9 %collective-permute-start.3 = (bf16[128,256]{1,0:T(8,128)(2,1)S(1)}, bf16[128,256]{1,0:T(8,128)(2,1)S(1)}, u32[]{:S(2)}, u32[]{:S(2)}) collective-permute-start(bf16[128,256]{1,0:T(8,128)(2,1)S(1)} %get-tuple-element.78), channel_id=1, source_target_pairs={{0,4},{1,5},{2,6},{3,7},{4,0},{5,1},{6,2},{7,3},{8,12},{9,13},{10,... | collective-permute-start | bytes 196616 | tf_op jit(solution)/shard_map/ppermute | solution.py:275
  10.7 12.2 %collective-permute-start.2 = (bf16[128,256]{1,0:T(8,128)(2,1)S(1)}, bf16[128,256]{1,0:T(8,128)(2,1)S(1)}, u32[]{:S(2)}, u32[]{:S(2)}) collective-permute-start(bf16[128,256]{1,0:T(8,128)(2,1)S(1)} %get-tuple-element.79), channel_id=1, source_target_pairs={{0,3},{1,4},{2,5},{3,6},{4,7},{5,0},{6,1},{7,2},{8,11},{9,12},{10,... | collective-permute-start | bytes 196616 | tf_op jit(solution)/shard_map/ppermute | solution.py:275
  11.6 16.6 %collective-permute-start.1 = (bf16[128,256]{1,0:T(8,128)(2,1)S(1)}, bf16[128,256]{1,0:T(8,128)(2,1)S(1)}, u32[]{:S(2)}, u32[]{:S(2)}) collective-permute-start(bf16[128,256]{1,0:T(8,128)(2,1)S(1)} %get-tuple-element.80), channel_id=1, source_target_pairs={{0,2},{1,3},{2,4},{3,5},{4,6},{5,7},{6,0},{7,1},{8,10},{9,11},{10,... | collective-permute-start | bytes 196616 | tf_op jit(solution)/shard_map/ppermute | solution.py:275
  12.3 15.9 %collective-permute-start = (bf16[128,256]{1,0:T(8,128)(2,1)S(1)}, bf16[128,256]{1,0:T(8,128)(2,1)S(1)}, u32[]{:S(2)}, u32[]{:S(2)}) collective-permute-start(bf16[128,256]{1,0:T(8,128)(2,1)S(1)} %get-tuple-element.81), channel_id=1, source_target_pairs={{0,1},{1,2},{2,3},{3,4},{4,5},{5,6},{6,7},{7,0},{8,9},{9,10},{10,1... | collective-permute-start | bytes 196616 | tf_op jit(solution)/shard_map/ppermute | solution.py:275
  13.3 16.0 %collective-permute-start.5 = (bf16[128,256]{1,0:T(8,128)(2,1)S(1)}, bf16[128,256]{1,0:T(8,128)(2,1)S(1)}, u32[]{:S(2)}, u32[]{:S(2)}) collective-permute-start(bf16[128,256]{1,0:T(8,128)(2,1)S(1)} %get-tuple-element.83), channel_id=1, source_target_pairs={{0,6},{1,7},{2,0},{3,1},{4,2},{5,3},{6,4},{7,5},{8,14},{9,15},{10,... | collective-permute-start | bytes 196616 | tf_op jit(solution)/shard_map/ppermute | solution.py:275
  21.8 9.9 %collective-permute-start.18 = (bf16[128,256]{1,0:T(8,128)(2,1)S(1)}, bf16[128,256]{1,0:T(8,128)(2,1)S(1)}, u32[]{:S(2)}, u32[]{:S(2)}) collective-permute-start(bf16[128,256]{1,0:T(8,128)(2,1)S(1)} %get-tuple-element.70), channel_id=1, source_target_pairs={{0,5},{1,6},{2,7},{3,0},{4,1},{5,2},{6,3},{7,4},{8,13},{9,14},{10,... | collective-permute-start | bytes 196616 | tf_op jit(solution)/shard_map/ppermute | solution.py:275
  22.9 14.8 %collective-permute-start.17 = (bf16[128,256]{1,0:T(8,128)(2,1)S(1)}, bf16[128,256]{1,0:T(8,128)(2,1)S(1)}, u32[]{:S(2)}, u32[]{:S(2)}) collective-permute-start(bf16[128,256]{1,0:T(8,128)(2,1)S(1)} %get-tuple-element.71), channel_id=1, source_target_pairs={{0,4},{1,5},{2,6},{3,7},{4,0},{5,1},{6,2},{7,3},{8,12},{9,13},{10,... | collective-permute-start | bytes 196616 | tf_op jit(solution)/shard_map/ppermute | solution.py:275
  28.2 9.5 %collective-permute-start.16 = (bf16[128,256]{1,0:T(8,128)(2,1)S(1)}, bf16[128,256]{1,0:T(8,128)(2,1)S(1)}, u32[]{:S(2)}, u32[]{:S(2)}) collective-permute-start(bf16[128,256]{1,0:T(8,128)(2,1)S(1)} %get-tuple-element.72), channel_id=1, source_target_pairs={{0,3},{1,4},{2,5},{3,6},{4,7},{5,0},{6,1},{7,2},{8,11},{9,12},{10,... | collective-permute-start | bytes 196616 | tf_op jit(solution)/shard_map/ppermute | solution.py:275
  28.2 9.5 %collective-permute-start.15 = (bf16[128,256]{1,0:T(8,128)(2,1)S(1)}, bf16[128,256]{1,0:T(8,128)(2,1)S(1)}, u32[]{:S(2)}, u32[]{:S(2)}) collective-permute-start(bf16[128,256]{1,0:T(8,128)(2,1)S(1)} %get-tuple-element.73), channel_id=1, source_target_pairs={{0,2},{1,3},{2,4},{3,5},{4,6},{5,7},{6,0},{7,1},{8,10},{9,11},{10,... | collective-permute-start | bytes 196616 | tf_op jit(solution)/shard_map/ppermute | solution.py:275
  29.3 8.4 %collective-permute-start.14 = (bf16[128,256]{1,0:T(8,128)(2,1)S(1)}, bf16[128,256]{1,0:T(8,128)(2,1)S(1)}, u32[]{:S(2)}, u32[]{:S(2)}) collective-permute-start(bf16[128,256]{1,0:T(8,128)(2,1)S(1)} %get-tuple-element.74), channel_id=1, source_target_pairs={{0,1},{1,2},{2,3},{3,4},{4,5},{5,6},{6,7},{7,0},{8,9},{9,10},{10,1... | collective-permute-start | bytes 196616 | tf_op jit(solution)/shard_map/ppermute | solution.py:275
  40.1 5.7 %collective-permute-start.21 = (bf16[128,256]{1,0:T(8,128)(2,1)S(1)}, bf16[128,256]{1,0:T(8,128)(2,1)S(1)}, u32[]{:S(2)}, u32[]{:S(2)}) collective-permute-start(bf16[128,256]{1,0:T(8,128)(2,1)S(1)} %get-tuple-element.57), channel_id=1, source_target_pairs={{0,1},{1,2},{2,3},{3,4},{4,5},{5,6},{6,7},{7,0},{8,9},{9,10},{10,1... | collective-permute-start | bytes 196616 | tf_op jit(solution)/shard_map/ppermute | solution.py:275
  40.2 6.9 %collective-permute-start.22 = (bf16[128,256]{1,0:T(8,128)(2,1)S(1)}, bf16[128,256]{1,0:T(8,128)(2,1)S(1)}, u32[]{:S(2)}, u32[]{:S(2)}) collective-permute-start(bf16[128,256]{1,0:T(8,128)(2,1)S(1)} %get-tuple-element.58), channel_id=1, source_target_pairs={{0,2},{1,3},{2,4},{3,5},{4,6},{5,7},{6,0},{7,1},{8,10},{9,11},{10,... | collective-permute-start | bytes 196616 | tf_op jit(solution)/shard_map/ppermute | solution.py:275
  40.2 11.8 %collective-permute-start.23 = (bf16[128,256]{1,0:T(8,128)(2,1)S(1)}, bf16[128,256]{1,0:T(8,128)(2,1)S(1)}, u32[]{:S(2)}, u32[]{:S(2)}) collective-permute-start(bf16[128,256]{1,0:T(8,128)(2,1)S(1)} %get-tuple-element.59), channel_id=1, source_target_pairs={{0,3},{1,4},{2,5},{3,6},{4,7},{5,0},{6,1},{7,2},{8,11},{9,12},{10,... | collective-permute-start | bytes 196616 | tf_op jit(solution)/shard_map/ppermute | solution.py:275
  40.3 11.8 %collective-permute-start.24 = (bf16[128,256]{1,0:T(8,128)(2,1)S(1)}, bf16[128,256]{1,0:T(8,128)(2,1)S(1)}, u32[]{:S(2)}, u32[]{:S(2)}) collective-permute-start(bf16[128,256]{1,0:T(8,128)(2,1)S(1)} %get-tuple-element.60), channel_id=1, source_target_pairs={{0,4},{1,5},{2,6},{3,7},{4,0},{5,1},{6,2},{7,3},{8,12},{9,13},{10,... | collective-permute-start | bytes 196616 | tf_op jit(solution)/shard_map/ppermute | solution.py:275
  44.3 9.0 %collective-permute-start.25 = (bf16[128,256]{1,0:T(8,128)(2,1)S(1)}, bf16[128,256]{1,0:T(8,128)(2,1)S(1)}, u32[]{:S(2)}, u32[]{:S(2)}) collective-permute-start(bf16[128,256]{1,0:T(8,128)(2,1)S(1)} %get-tuple-element.61), channel_id=1, source_target_pairs={{0,5},{1,6},{2,7},{3,0},{4,1},{5,2},{6,3},{7,4},{8,13},{9,14},{10,... | collective-permute-start | bytes 196616 | tf_op jit(solution)/shard_map/ppermute | solution.py:275
  45.8 7.5 %collective-permute-start.26 = (bf16[128,256]{1,0:T(8,128)(2,1)S(1)}, bf16[128,256]{1,0:T(8,128)(2,1)S(1)}, u32[]{:S(2)}, u32[]{:S(2)}) collective-permute-start(bf16[128,256]{1,0:T(8,128)(2,1)S(1)} %get-tuple-element.62), channel_id=1, source_target_pairs={{0,6},{1,7},{2,0},{3,1},{4,2},{5,3},{6,4},{7,5},{8,14},{9,15},{10,... | collective-permute-start | bytes 196616 | tf_op jit(solution)/shard_map/ppermute | solution.py:275
  47.0 10.1 %collective-permute-start.27 = (bf16[128,256]{1,0:T(8,128)(2,1)S(1)}, bf16[128,256]{1,0:T(8,128)(2,1)S(1)}, u32[]{:S(2)}, u32[]{:S(2)}) collective-permute-start(bf16[128,256]{1,0:T(8,128)(2,1)S(1)} %get-tuple-element.63), channel_id=1, source_target_pairs={{0,7},{1,0},{2,1},{3,2},{4,3},{5,4},{6,5},{7,6},{8,15},{9,8},{10,9... | collective-permute-start | bytes 196616 | tf_op jit(solution)/shard_map/ppermute | solution.py:275
  52.0 11.0 %collective-permute-start.7 = (bf16[128,256]{1,0:T(8,128)(2,1)S(1)}, bf16[128,256]{1,0:T(8,128)(2,1)S(1)}, u32[]{:S(2)}, u32[]{:S(2)}) collective-permute-start(bf16[128,256]{1,0:T(8,128)(2,1)S(1)} %get-tuple-element.39), channel_id=1, source_target_pairs={{0,1},{1,2},{2,3},{3,4},{4,5},{5,6},{6,7},{7,0},{8,9},{9,10},{10,1... | collective-permute-start | bytes 196616 | tf_op jit(solution)/shard_map/ppermute | solution.py:275
  52.1 13.4 %collective-permute-start.8 = (bf16[128,256]{1,0:T(8,128)(2,1)S(1)}, bf16[128,256]{1,0:T(8,128)(2,1)S(1)}, u32[]{:S(2)}, u32[]{:S(2)}) collective-permute-start(bf16[128,256]{1,0:T(8,128)(2,1)S(1)} %get-tuple-element.40), channel_id=1, source_target_pairs={{0,2},{1,3},{2,4},{3,5},{4,6},{5,7},{6,0},{7,1},{8,10},{9,11},{10,... | collective-permute-start | bytes 196616 | tf_op jit(solution)/shard_map/ppermute | solution.py:275
  53.3 12.7 %collective-permute-start.9 = (bf16[128,256]{1,0:T(8,128)(2,1)S(1)}, bf16[128,256]{1,0:T(8,128)(2,1)S(1)}, u32[]{:S(2)}, u32[]{:S(2)}) collective-permute-start(bf16[128,256]{1,0:T(8,128)(2,1)S(1)} %get-tuple-element.41), channel_id=1, source_target_pairs={{0,3},{1,4},{2,5},{3,6},{4,7},{5,0},{6,1},{7,2},{8,11},{9,12},{10,... | collective-permute-start | bytes 196616 | tf_op jit(solution)/shard_map/ppermute | solution.py:275
  53.3 13.2 %collective-permute-start.10 = (bf16[128,256]{1,0:T(8,128)(2,1)S(1)}, bf16[128,256]{1,0:T(8,128)(2,1)S(1)}, u32[]{:S(2)}, u32[]{:S(2)}) collective-permute-start(bf16[128,256]{1,0:T(8,128)(2,1)S(1)} %get-tuple-element.42), channel_id=1, source_target_pairs={{0,4},{1,5},{2,6},{3,7},{4,0},{5,1},{6,2},{7,3},{8,12},{9,13},{10,... | collective-permute-start | bytes 196616 | tf_op jit(solution)/shard_map/ppermute | solution.py:275
  57.2 10.4 %collective-permute-start.11 = (bf16[128,256]{1,0:T(8,128)(2,1)S(1)}, bf16[128,256]{1,0:T(8,128)(2,1)S(1)}, u32[]{:S(2)}, u32[]{:S(2)}) collective-permute-start(bf16[128,256]{1,0:T(8,128)(2,1)S(1)} %get-tuple-element.43), channel_id=1, source_target_pairs={{0,5},{1,6},{2,7},{3,0},{4,1},{5,2},{6,3},{7,4},{8,13},{9,14},{10,... | collective-permute-start | bytes 196616 | tf_op jit(solution)/shard_map/ppermute | solution.py:275
  63.0 7.9 %copy-start.1 = (bf16[1,128,2048]{2,1,0:T(8,128)(2,1)S(1)}, bf16[1,128,2048]{2,1,0:T(8,128)(2,1)}, u32[]{:S(2)}) copy-start(bf16[1,128,2048]{2,1,0:T(8,128)(2,1)} %param.12) | copy-start | bytes 1572868
  63.0 7.9 %copy-start.2 = (bf16[1,128,2048]{2,1,0:T(8,128)(2,1)S(1)}, bf16[1,128,2048]{2,1,0:T(8,128)(2,1)}, u32[]{:S(2)}) copy-start(bf16[1,128,2048]{2,1,0:T(8,128)(2,1)} %param.13) | copy-start | bytes 1572868
  63.0 9.1 %collective-permute-start.30 = (f32[200,256]{1,0:T(8,128)S(1)}, f32[200,256]{1,0:T(8,128)S(1)}, u32[]{:S(2)}, u32[]{:S(2)}) collective-permute-start(f32[200,256]{1,0:T(8,128)S(1)} %grads.1), channel_id=1, source_target_pairs={{0,24},{8,16},{16,8},{24,0},{1,25},{9,17},{17,9},{25,1},{2,26},{10... | collective-permute-start | bytes 614408 | tf_op jit(solution)/shard_map/ppermute | solution.py:298
  65.5 9.7 %collective-permute-start.29 = (f32[200,256]{1,0:T(8,128)S(1)}, f32[200,256]{1,0:T(8,128)S(1)}, u32[]{:S(2)}, u32[]{:S(2)}) collective-permute-start(f32[200,256]{1,0:T(8,128)S(1)} %grads.1), channel_id=1, source_target_pairs={{0,16},{8,24},{16,0},{24,8},{1,17},{9,25},{17,1},{25,9},{2,18},{10... | collective-permute-start | bytes 614408 | tf_op jit(solution)/shard_map/ppermute | solution.py:298
  66.0 9.3 %collective-permute-start.28 = (f32[200,256]{1,0:T(8,128)S(1)}, f32[200,256]{1,0:T(8,128)S(1)}, u32[]{:S(2)}, u32[]{:S(2)}) collective-permute-start(f32[200,256]{1,0:T(8,128)S(1)} %grads.1), channel_id=1, source_target_pairs={{0,8},{8,0},{16,24},{24,16},{1,9},{9,1},{17,25},{25,17},{2,10},{10... | collective-permute-start | bytes 614408 | tf_op jit(solution)/shard_map/ppermute | solution.py:298
  66.5 4.3 %collective-permute-start.12 = (bf16[128,256]{1,0:T(8,128)(2,1)S(1)}, bf16[128,256]{1,0:T(8,128)(2,1)S(1)}, u32[]{:S(2)}, u32[]{:S(2)}) collective-permute-start(bf16[128,256]{1,0:T(8,128)(2,1)S(1)} %get-tuple-element.44), channel_id=1, source_target_pairs={{0,6},{1,7},{2,0},{3,1},{4,2},{5,3},{6,4},{7,5},{8,14},{9,15},{10,... | collective-permute-start | bytes 196616 | tf_op jit(solution)/shard_map/ppermute | solution.py:275
  67.6 3.2 %collective-permute-start.13 = (bf16[128,256]{1,0:T(8,128)(2,1)S(1)}, bf16[128,256]{1,0:T(8,128)(2,1)S(1)}, u32[]{:S(2)}, u32[]{:S(2)}) collective-permute-start(bf16[128,256]{1,0:T(8,128)(2,1)S(1)} %get-tuple-element.45), channel_id=1, source_target_pairs={{0,7},{1,0},{2,1},{3,2},{4,3},{5,4},{6,5},{7,6},{8,15},{9,8},{10,9... | collective-permute-start | bytes 196616 | tf_op jit(solution)/shard_map/ppermute | solution.py:275

commit v3 on v2

--- a/solution.py
+++ b/solution.py
@@ -77,16 +77,19 @@
     return pl.ds(row, rows), pl.ds(column, width)
 
 
-def gather_blocks(me_ref, blocks, whole):
+def gather_blocks(me_ref, blocks, which, whole):
     (rows, width), count = blocks[0].shape, len(blocks)
+    rows //= 2
     for shift, ref in enumerate(blocks):
-        whole[place_of(me_ref, -shift, count, rows, width, whole.shape[0])] = ref[...]
-
-
-def scatter_blocks(me_ref, whole, blocks):
+        at = place_of(me_ref, -shift, count, rows, width, whole.shape[0])
+        whole[at] = ref[which * rows : (which + 1) * rows, :]
+
+
+def scatter_blocks(me_ref, whole, which, blocks):
     (rows, width), count = blocks[0].shape, len(blocks)
+    rows //= 2
     for shift, ref in enumerate(blocks):
-        ref[...] = whole[place_of(me_ref, shift, count, rows, width, whole.shape[0])]
+        ref[which * rows : (which + 1) * rows, :] = whole[place_of(me_ref, shift, count, rows, width, whole.shape[0])]
 
 
 def filters_kernel(
@@ -132,35 +135,38 @@
     chunks(block, window)
 
 
-def conv_kernel(count, backward, *refs):
+def conv_kernel(count, *refs):
     me_ref, blocks, refs = refs[0], refs[1 : 1 + count], refs[1 + count :]
     fwd_high, fwd_low, inv_high, inv_low, both_spec = refs[:5]
-    outs, (spec, whole, high) = refs[5 : 5 + count], refs[5 + count :]
+    outs, (series_spec, grad_spec, whole, high) = refs[5 : 5 + count], refs[5 + count :]
     size, block = fwd_high.shape
     width = blocks[0].shape[1]
-    parts = spec.shape[1] // width
-    gather_blocks(me_ref, blocks, whole)
-    spec[...] = mm(fwd_high[...], whole[...]) + mm(fwd_low[...], whole[...])
-
-    def product(re, im):
-        for i in range(parts):
-            sum_re = sum_im = 0.0
-            for d in range(parts - i if backward else i + 1):
-                there = lanes(i + d if backward else i - d, width)
-                c_re, c_im = both_spec[re, lanes(d, width)], both_spec[im, lanes(d, width)]
-                x_re, x_im = spec[re, there], spec[im, there]
-                if backward:
-                    sum_re = sum_re + (c_re * x_re + c_im * x_im)
-                    sum_im = sum_im + (c_re * x_im - c_im * x_re)
-                else:
-                    sum_re = sum_re + (c_re * x_re - c_im * x_im)
-                    sum_im = sum_im + (c_re * x_im + c_im * x_re)
-            high[re, lanes(i, width)] = sum_re.astype(BF16)
-            high[im, lanes(i, width)] = sum_im.astype(BF16)
-
-    chunks(block, product)
-    whole[...] = (mm(inv_high[...], high[...]) + mm(inv_low[...], high[...])).astype(BF16)
-    scatter_blocks(me_ref, whole, outs)
+    parts = series_spec.shape[1] // width
+
+    for which, spec in enumerate((series_spec, grad_spec)):
+        backward = which == 1
+        gather_blocks(me_ref, blocks, which, whole)
+        spec[...] = mm(fwd_high[...], whole[...]) + mm(fwd_low[...], whole[...])
+
+        def product(re, im):
+            for i in range(parts):
+                sum_re = sum_im = 0.0
+                for d in range(parts - i if backward else i + 1):
+                    there = lanes(i + d if backward else i - d, width)
+                    c_re, c_im = both_spec[re, lanes(d, width)], both_spec[im, lanes(d, width)]
+                    x_re, x_im = spec[re, there], spec[im, there]
+                    if backward:
+                        sum_re = sum_re + (c_re * x_re + c_im * x_im)
+                        sum_im = sum_im + (c_re * x_im - c_im * x_re)
+                    else:
+                        sum_re = sum_re + (c_re * x_re - c_im * x_im)
+                        sum_im = sum_im + (c_re * x_im + c_im * x_re)
+                high[re, lanes(i, width)] = sum_re.astype(BF16)
+                high[im, lanes(i, width)] = sum_im.astype(BF16)
+
+        chunks(block, product)
+        whole[...] = (mm(inv_high[...], high[...]) + mm(inv_low[...], high[...])).astype(BF16)
+        scatter_blocks(me_ref, whole, which, outs)
 
 
 def grads_kernel(
@@ -233,34 +239,74 @@
             at += groups
 
 
+def prepare_kernel(count, me_ref, series, gating, upstream, *refs):
+    outs, (gate_held, up_held, series_sem, gate_sem, up_sem) = refs[:count], refs[count:]
+    rows, channels = series.shape
+    width = channels // count
+
+    def columns(shift):
+        target = lax.rem(me_ref[0] + shift, count)
+        return pl.ds(pl.multiple_of(target * width, width), width)
+
+    copies = []
+    for shift, ref in enumerate(outs):
+        here = columns(shift)
+        copies.append(
+            (
+                pltpu.make_async_copy(gating.at[:, here], gate_held.at[shift], gate_sem.at[shift]),
+                pltpu.make_async_copy(upstream.at[:, here], up_held.at[shift], up_sem.at[shift]),
+                pltpu.make_async_copy(series.at[:, here], ref.at[:rows, :], series_sem.at[shift]),
+            )
+        )
+    for group in copies:
+        for copy in group:
+            copy.start()
+    for shift, ref in enumerate(outs):
+        for copy in copies[shift]:
+            copy.wait()
+        product = up_held[shift].astype(F32) * gate_held[shift].astype(F32)
+        ref[rows:, :] = product.astype(BF16)
+
+
+def finish_kernel(scale, first, second, third, fourth, long_grad, taps_grad, skip_grad):
+    groups, length = long_grad.shape
+    tap_count, width = taps_grad.shape
+    padded = first.shape[1]
+
+    def total(at, rows):
+        here = pl.ds(at, rows)
+        return ((first[here, :] + second[here, :]) + (third[here, :] + fourth[here, :])) * scale
+
+    taps_grad[...] = total(0, tap_count)[:, :width]
+    skip_grad[...] = total(tap_count, 8)[:1, :width]
+    for piece in range(length // padded):
+        long_grad[:, lanes(piece, padded)] = total(tap_count + 8 + piece * groups, groups)
+
+
 def gate_kernel(count, *refs):
     me_ref, blocks, refs = refs[0], refs[1 : 1 + count], refs[1 + count :]
-    gating, upstream, output, gate_grad = refs
+    gating, upstream, output, gate_grad, signal_grad = refs
+    rows = gating.shape[0]
     width = blocks[0].shape[1]
     for shift, ref in enumerate(blocks):
         source = lax.rem(me_ref[0] + (count - shift), count)
         columns = pl.ds(pl.multiple_of(source * width, width), width)
-        conv = ref[...].astype(F32)
+        conv = ref[:rows, :].astype(F32)
         output[:, columns] = (gating[:, columns].astype(F32) * conv).astype(BF16)
         gate_grad[:, columns] = (upstream[:, columns].astype(F32) * conv).astype(BF16)
-
-
-def place_kernel(count, *refs):
-    me_ref, blocks, out = refs[0], refs[1 : 1 + count], refs[-1]
-    width = blocks[0].shape[1]
-    for shift, ref in enumerate(blocks):
-        source = lax.rem(me_ref[0] + (count - shift), count)
-        out[:, pl.ds(pl.multiple_of(source * width, width), width)] = ref[...]
-
-
-def call(kernel, operands, outs, scratch, budget, micros, name):
+        signal_grad[:, columns] = ref[rows:, :]
+
+
+def call(kernel, operands, outs, scratch, budget, micros, name, space=pltpu.VMEM):
     moved = sum(math.prod(x.shape) * x.dtype.itemsize for x in [*operands, *outs])
     return pl.pallas_call(
         kernel,
         out_shape=outs,
-        in_specs=[SMEM if x.dtype == jnp.int32 else VMEM for x in operands],
+        in_specs=[
+            SMEM if x.dtype == jnp.int32 else pl.BlockSpec(memory_space=space) for x in operands
+        ],
         out_specs=[VMEM for _ in outs],
-        scratch_shapes=[pltpu.VMEM(shape, dtype) for shape, dtype in scratch],
+        scratch_shapes=[pltpu.VMEM(*x) if isinstance(x, tuple) else x for x in scratch],
         compiler_params=pltpu.CompilerParams(vmem_limit_bytes=budget),
         cost_estimate=pl.CostEstimate(
             flops=int(micros * 1e9), transcendentals=0, bytes_accessed=moved
@@ -269,12 +315,12 @@
     )(*operands)
 
 
-def exchange(blocks, axis):
+def exchange(blocks, axis, shifts):
     count = len(blocks)
-    return [blocks[0]] + [
-        lax.ppermute(blocks[k], axis, [(i, (i + k) % count) for i in range(count)])
-        for k in range(1, count)
-    ]
+    moved = list(blocks)
+    for k in shifts:
+        moved[k] = lax.ppermute(blocks[k], axis, [(i, (i + k) % count) for i in range(count)])
+    return moved
 
 
 def columns_for(rows, me, count):
@@ -292,11 +338,8 @@
     return jnp.transpose(ordered, (1, 0, 2)).reshape(blocks[0].shape[0], -1)
 
 
-def sum_over(value, axis):
-    if lax.axis_size(axis) != 4:
-        return lax.psum(value, axis)
-    a, b, c = (lax.ppermute(value, axis, [(i, i ^ flip) for i in range(4)]) for flip in (1, 2, 3))
-    return (value + a) + (b + c)
+def shares(value, axis):
+    return [value] + [lax.ppermute(value, axis, [(i, i ^ flip) for i in range(4)]) for flip in (1, 2, 3)]
 
 
 def local(signal, gate_input, cotangent, long_filter, short_taps, skip_gain):
@@ -322,18 +365,29 @@
     def trim(blocks):
         return [x[:, :width] if padded > width else x for x in blocks]
 
-    grad_gate = (upstream.astype(F32) * gating.astype(F32)).astype(BF16)
-    series_in = exchange(columns_for(series, me, count), "ctx")
-    grad_in = exchange(columns_for(grad_gate, me, count), "ctx")
-
+    spectrum = (size, parts * padded)
+    spectrum_out = jax.ShapeDtypeStruct(spectrum, F32)
+    budget = 10 * 4 * math.prod(spectrum)
     tables = [jnp.asarray(t) for t in dft_tables(block)]
     channel = np.arange(padded)[None, :]
     of_group = (channel // (width // groups) == np.arange(groups)[:, None]) & (channel < width)
     member = jnp.asarray(of_group.astype(ml_dtypes.bfloat16))
+    if width % 128 == 0:
+        sent = call(
+            functools.partial(prepare_kernel, count),
+            [where, series, gating, upstream],
+            [jax.ShapeDtypeStruct((2 * rows, width), BF16)] * count,
+            [((count, rows, width), BF16)] * 2 + [pltpu.SemaphoreType.DMA((count,))] * 3,
+            None,
+            1,
+            "prepare",
+            pltpu.HBM,
+        )
+    else:
+        grad_gate = (upstream.astype(F32) * gating.astype(F32)).astype(BF16)
+        sent = columns_for(jnp.concatenate([series, grad_gate]), me, count)
+    received = [pad(x) for x in exchange(sent, "ctx", range(1, count))]
     own_taps = pad(lax.dynamic_slice_in_dim(short_taps, me * width, width, 1))
-    spectrum = (size, parts * padded)
-    spectrum_out = jax.ShapeDtypeStruct(spectrum, F32)
-    budget = 10 * 4 * math.prod(spectrum)
     taps_spec, long_spec, both_spec = call(
         filters_kernel,
         [own_taps, long_filter, member, pad(skip_gain[None, :]), *tables],
@@ -344,23 +398,21 @@
         "filters",
     )
 
-    def convolve(blocks, backward, name):
-        *outs, spec = call(
-            functools.partial(conv_kernel, count, backward),
-            [where, *[pad(x) for x in blocks], *tables, both_spec],
-            [jax.ShapeDtypeStruct((rows, padded), BF16)] * count + [spectrum_out],
-            [((block, parts * padded), BF16), (spectrum, BF16)],
-            budget,
-            4,
-            name,
-        )
-        return trim(outs), spec
-
-    conv, series_spec = convolve(series_in, False, "conv")
-    conv_in = exchange(conv, "ctx")
-    grad_in, conv = lax.optimization_barrier((grad_in, conv))
-    grad, grad_spec = convolve(grad_in, True, "back")
-    signal_in = exchange(grad, "ctx")
+    *outs, series_spec, grad_spec = call(
+        functools.partial(conv_kernel, count),
+        [where, *received, *tables, both_spec],
+        [jax.ShapeDtypeStruct((2 * rows, padded), BF16)] * count + [spectrum_out] * 2,
+        [((block, parts * padded), BF16), (spectrum, BF16)],
+        budget,
+        8,
+        "conv",
+    )
+    outs = trim(outs)
+    early, late = [1, 7], []
+    returned = exchange(outs, "ctx", [1, 7, 4, 3, 5, 2, 6] if count == 8 else range(1, count))
+    *waited, grad_spec = lax.optimization_barrier([returned[k] for k in early] + [grad_spec])
+    for k, value in zip(early, waited):
+        returned[k] = value
     pieces = parts * (block // padded)
     (partial,) = call(
         grads_kernel,
@@ -371,38 +423,42 @@
         5,
         "grads",
     )
-    total = sum_over(partial, "dp") * (1.0 / math.sqrt(lax.axis_size("dp") * length))
-    taps_grad = total[:tap_count, :width]
-    skip_grad = total[tap_count, :width]
-    long_grad = total[tap_count + 8 :].reshape(pieces, groups, padded)
-    long_grad = jnp.transpose(long_grad, (1, 0, 2)).reshape(groups, length)
+    scale = 1.0 / math.sqrt(lax.axis_size("dp") * length)
+    if lax.axis_size("dp") == 4:
+        partials = shares(partial, "dp")
+    else:
+        partials = [lax.psum(partial, "dp")] + [jnp.zeros_like(partial)] * 3
+    long_grad, taps_grad, skip_grad = call(
+        functools.partial(finish_kernel, scale),
+        partials,
+        [
+            jax.ShapeDtypeStruct((groups, length), F32),
+            jax.ShapeDtypeStruct((tap_count, width), F32),
+            jax.ShapeDtypeStruct((1, width), F32),
+        ],
+        [],
+        budget,
+        1,
+        "finish",
+    )
 
     full = jax.ShapeDtypeStruct((rows, channels), BF16)
     if width % 128 == 0:
-        output, gate_grad = call(
+        output, gate_grad, signal_grad = call(
             functools.partial(gate_kernel, count),
-            [where, *conv_in, gating, upstream],
-            [full, full],
+            [where, *returned, gating, upstream],
+            [full, full, full],
             [],
             budget,
             1,
             "gate",
         )
-        (signal_grad,) = call(
-            functools.partial(place_kernel, count),
-            [where, *signal_in],
-            [full],
-            [],
-            budget,
-            1,
-            "place",
-        )
     else:
-        conv_rows = in_order(conv_in, me).astype(F32)
+        conv_rows, signal_grad = jnp.split(in_order(returned, me), 2)
+        conv_rows = conv_rows.astype(F32)
         output = (gating.astype(F32) * conv_rows).astype(BF16)
         gate_grad = (upstream.astype(F32) * conv_rows).astype(BF16)
-        signal_grad = in_order(signal_in, me)
-    return (output[None], gate_grad[None], signal_grad[None], long_grad, taps_grad, skip_grad)
+    return (output[None], gate_grad[None], signal_grad[None], long_grad, taps_grad, skip_grad[0])
 
 
 def solution(mesh):

time: 77.4 us -> 64 us (0.83)
  waiting for transfers between devices: 19.6 us -> 11.7 us
  starting transfers between devices: 36.6 us -> 32.1 us
  Pallas kernels: 16.4 us -> 19.1 us
  local copies, waits for them, and re-layouts: 2.1 us -> 0.08 us
  other arithmetic: 1.54 us -> 0 us
    ppermute x28 -> x14, waiting for transfers between devices: 16.4 us -> 7.4 us  [exchange(): lax.ppermute(blocks[k], axis, [(i, (i + k) % count) for i in range(count)])]
    ppermute x28 -> x14, starting transfers between devices: 33.1 us -> 26.6 us  [exchange(): lax.ppermute(blocks[k], axis, [(i, (i + k) % count) for i in range(count)])]
    pallas_call x6, Pallas kernels: 16.4 us -> 19.1 us  [call(): pl.pallas_call(kernel, out_shape=outs, in_specs=[SMEM if x.dtype == jnp.i...]
    ppermute x3, starting transfers between devices: 3.55 us -> 5.46 us  [shares(): lax.ppermute(value, axis, [(i, i ^ flip) for i in range(4)])]
    convert_element_type x1 -> x0, other arithmetic: 1.48 us -> none  [local(): grad_gate = (upstream.astype(F32) * gating.astype(F32)).astype(BF16)]
    slice x3 -> x0, local copies, waits for them, and re-layouts: 1.23 us -> none  [the longest x1 0.66 us: local(): taps_grad = total[:tap_count, :width]]
    ppermute x3, waiting for transfers between devices: 3.21 us -> 4.26 us  [shares(): lax.ppermute(value, axis, [(i, i ^ flip) for i in range(4)])]
  transfers between devices with their start and end apart: 31 -> 17, of which waited for: 10 -> 8; matrix products, arithmetic and copies ran while one was open for 0% -> 0% of each run, Pallas kernels for 18% -> 17%
where the time goes in v3:
time: 64 us; the launch traced here: 63.7 us
  starting transfers between devices  32.1 us (50%)
  Pallas kernels  19.1 us (30%)
  waiting for transfers between devices  11.7 us (18%)
  between operations  0.8 us (1%)
    ppermute x14, starting transfers between devices, exchange(): lax.ppermute(blocks[k], axis, [(i, (i + k) % count) for i in range(count)])  26.6 us
    pallas_call x6, Pallas kernels, call(): pl.pallas_call(kernel, out_shape=outs, in_specs=[SMEM if x.dtype == jnp.i...  19.1 us
    ppermute x14, waiting for transfers between devices, exchange(): lax.ppermute(blocks[k], axis, [(i, (i + k) % count) for i in range(count)])  7.4 us
    ppermute x3, starting transfers between devices, shares(): lax.ppermute(value, axis, [(i, i ^ flip) for i in range(4)])  5.46 us
    ppermute x3, waiting for transfers between devices, shares(): lax.ppermute(value, axis, [(i, i ^ flip) for i in range(4)])  4.26 us
  transfers between devices with their start and end apart: 17, of which 8 were waited for; matrix products, arithmetic and copies ran while one was open for 0% of the time, Pallas kernels for 17%

profile of v3, /device:TPU:0, one launch (start us, length us, event | category | flops | bytes accessed | tf_op | source)
XLA Modules:
  0.0 63.7 jit_solution(11447941024427401763)
XLA Ops:
  0.6 0.0 copy-start
  0.6 0.0 copy-start.5
  0.7 0.0 copy-start.6
  0.7 0.0 copy-start.7
  0.7 0.0 copy-start.8
  0.7 0.0 copy-start.9
  0.7 2.7 %prepare.1 = (bf16[256,256]{1,0:T(8,128)(2,1)}, bf16[256,256]{1,0:T(8,128)(2,1)}, bf16[256,256]{1,0:T(8,128)(2,1)}, bf16[256,256]{1,0:T(8,128)(2,1)}, bf16[256,2...) custom-call(s32[1]{0:T(128)} %bitcast.me_ref.refs_0_, ...), custom_call_target="tpu_custom_call" | custom-call | flops 1000000000 | bytes 2621444 | tf_op jit(solution)/shard_map/prepare/pallas_call | solution.py:302
  3.4 0.5 collective-permute-start
  3.9 2.6 %collective-permute-start.1 = (bf16[256,256]{1,0:T(8,128)(2,1)}, bf16[256,256]{1,0:T(8,128)(2,1)S(1)}, u32[]{:S(2)}, u32[]{:S(2)}) collective-permute-start(bf16[256,256]{1,0:T(8,128)(2,1)} %get-tuple-element.38), channel_id=1, source_target_pairs={{0,2},{1,3},{2,4},{3,5},{4,6},{5,7},{6,0},{7,1},{8,10},{9,11},{10,... | collective-permute-start | bytes 393224 | tf_op jit(solution)/shard_map/ppermute | solution.py:322
  6.6 2.5 %collective-permute-start.2 = (bf16[256,256]{1,0:T(8,128)(2,1)}, bf16[256,256]{1,0:T(8,128)(2,1)S(1)}, u32[]{:S(2)}, u32[]{:S(2)}) collective-permute-start(bf16[256,256]{1,0:T(8,128)(2,1)} %get-tuple-element.39), channel_id=1, source_target_pairs={{0,3},{1,4},{2,5},{3,6},{4,7},{5,0},{6,1},{7,2},{8,11},{9,12},{10,... | collective-permute-start | bytes 393224 | tf_op jit(solution)/shard_map/ppermute | solution.py:322
  9.1 1.2 %collective-permute-start.3 = (bf16[256,256]{1,0:T(8,128)(2,1)}, bf16[256,256]{1,0:T(8,128)(2,1)S(1)}, u32[]{:S(2)}, u32[]{:S(2)}) collective-permute-start(bf16[256,256]{1,0:T(8,128)(2,1)} %get-tuple-element.40), channel_id=1, source_target_pairs={{0,4},{1,5},{2,6},{3,7},{4,0},{5,1},{6,2},{7,3},{8,12},{9,13},{10,... | collective-permute-start | bytes 393224 | tf_op jit(solution)/shard_map/ppermute | solution.py:322
  10.3 1.2 %collective-permute-start.4 = (bf16[256,256]{1,0:T(8,128)(2,1)}, bf16[256,256]{1,0:T(8,128)(2,1)S(1)}, u32[]{:S(2)}, u32[]{:S(2)}) collective-permute-start(bf16[256,256]{1,0:T(8,128)(2,1)} %get-tuple-element.41), channel_id=1, source_target_pairs={{0,5},{1,6},{2,7},{3,0},{4,1},{5,2},{6,3},{7,4},{8,13},{9,14},{10,... | collective-permute-start | bytes 393224 | tf_op jit(solution)/shard_map/ppermute | solution.py:322
  11.5 0.0 collective-permute-done.refs_2_
  11.6 2.4 %collective-permute-start.5 = (bf16[256,256]{1,0:T(8,128)(2,1)}, bf16[256,256]{1,0:T(8,128)(2,1)S(1)}, u32[]{:S(2)}, u32[]{:S(2)}) collective-permute-start(bf16[256,256]{1,0:T(8,128)(2,1)} %get-tuple-element.42), channel_id=1, source_target_pairs={{0,6},{1,7},{2,0},{3,1},{4,2},{5,3},{6,4},{7,5},{8,14},{9,15},{10,... | collective-permute-start | bytes 393224 | tf_op jit(solution)/shard_map/ppermute | solution.py:322
  14.0 0.0 collective-permute-done.1.refs_3_
  14.0 2.2 %collective-permute-start.6 = (bf16[256,256]{1,0:T(8,128)(2,1)}, bf16[256,256]{1,0:T(8,128)(2,1)S(1)}, u32[]{:S(2)}, u32[]{:S(2)}) collective-permute-start(bf16[256,256]{1,0:T(8,128)(2,1)} %get-tuple-element.43), channel_id=1, source_target_pairs={{0,7},{1,0},{2,1},{3,2},{4,3},{5,4},{6,5},{7,6},{8,15},{9,8},{10,9... | collective-permute-start | bytes 393224 | tf_op jit(solution)/shard_map/ppermute | solution.py:322
  16.2 0.0 copy-done.7
  16.2 0.0 copy-start.10
  16.2 5.7 %filters.1 = (f32[512,256]{1,0:T(8,128)S(1)}, f32[512,1024]{1,0:T(8,128)S(1)}, f32[512,1024]{1,0:T(8,128)S(1)}) custom-call(bf16[128,256]{1,0:T(8,128)(2,1)S(1)} %constant_dynamic-slice_fusion.taps, f32[16,1024]{1,0:T(8,128)S(1)} %copy-done.3, bf16[16,256]{1,0:T(8,128)(2,1)S(1)} %copy-done.9, f32[1,256]{1,0:T(1,128)S(1)} %bitcast.13, ...), custom_call_target="tpu_custom_call" | custom-call | flops 5000000000 | bytes 5907456 | tf_op jit(solution)/shard_map/filters/pallas_call | solution.py:302
  21.9 1.4 %collective-permute-done.2.refs_4_ = bf16[256,256]{1,0:T(8,128)(2,1)S(1)} collective-permute-done((bf16[256,256]{1,0:T(8,128)(2,1)}, bf16[256,256]{1,0:T(8,128)(2,1)S(1)}, u32[]{:S(2)}, u32[]{:S(2)}) %collective-permute-start.2) | collective-permute-done | bytes 131104 | tf_op jit(solution)/shard_map/ppermute | solution.py:322
  23.4 0.2 collective-permute-done.3.refs_5_
  23.6 0.0 collective-permute-done.4.refs_6_
  23.6 0.0 collective-permute-done.5.refs_7_
  23.6 0.7 %collective-permute-done.6.refs_8_ = bf16[256,256]{1,0:T(8,128)(2,1)S(1)} collective-permute-done((bf16[256,256]{1,0:T(8,128)(2,1)}, bf16[256,256]{1,0:T(8,128)(2,1)S(1)}, u32[]{:S(2)}, u32[]{:S(2)}) %collective-permute-start.6) | collective-permute-done | bytes 131104 | tf_op jit(solution)/shard_map/ppermute | solution.py:322
  24.2 4.6 %conv.1 = (bf16[256,256]{1,0:T(8,128)(2,1)S(1)}, bf16[256,256]{1,0:T(8,128)(2,1)S(1)}, bf16[256,256]{1,0:T(8,128)(2,1)S(1)}, bf16[256,256]{1,0:T(8,128)(2,1)S(1)...) custom-call(s32[1]{0:T(128)} %bitcast.me_ref.refs_0_, ...), custom_call_target="tpu_custom_call" | custom-call | flops 8000000000 | bytes 9437188 | tf_op jit(solution)/shard_map/conv/pallas_call | solution.py:302
  28.8 2.0 %collective-permute-start.7 = (bf16[256,256]{1,0:T(8,128)(2,1)S(1)}, bf16[256,256]{1,0:T(8,128)(2,1)S(1)}, u32[]{:S(2)}, u32[]{:S(2)}) collective-permute-start(bf16[256,256]{1,0:T(8,128)(2,1)S(1)} %get-tuple-element.46), channel_id=1, source_target_pairs={{0,1},{1,2},{2,3},{3,4},{4,5},{5,6},{6,7},{7,0},{8,9},{9,10},{10,1... | collective-permute-start | bytes 393224 | tf_op jit(solution)/shard_map/ppermute | solution.py:322
  30.9 7.4 %collective-permute-start.8 = (bf16[256,256]{1,0:T(8,128)(2,1)S(1)}, bf16[256,256]{1,0:T(8,128)(2,1)S(1)}, u32[]{:S(2)}, u32[]{:S(2)}) collective-permute-start(bf16[256,256]{1,0:T(8,128)(2,1)S(1)} %get-tuple-element.47), channel_id=1, source_target_pairs={{0,7},{1,0},{2,1},{3,2},{4,3},{5,4},{6,5},{7,6},{8,15},{9,8},{10,9... | collective-permute-start | bytes 393224 | tf_op jit(solution)/shard_map/ppermute | solution.py:322
  38.3 0.0 collective-permute-start.9
  38.3 0.0 collective-permute-start.10
  38.3 1.6 %collective-permute-start.11 = (bf16[256,256]{1,0:T(8,128)(2,1)S(1)}, bf16[256,256]{1,0:T(8,128)(2,1)S(1)}, u32[]{:S(2)}, u32[]{:S(2)}) collective-permute-start(bf16[256,256]{1,0:T(8,128)(2,1)S(1)} %get-tuple-element.52), channel_id=1, source_target_pairs={{0,4},{1,5},{2,6},{3,7},{4,0},{5,1},{6,2},{7,3},{8,12},{9,13},{10,... | collective-permute-start | bytes 393224 | tf_op jit(solution)/shard_map/ppermute | solution.py:322
  39.9 1.7 %collective-permute-done.7.refs_2_ = bf16[256,256]{1,0:T(8,128)(2,1)S(1)} collective-permute-done((bf16[256,256]{1,0:T(8,128)(2,1)S(1)}, bf16[256,256]{1,0:T(8,128)(2,1)S(1)}, u32[]{:S(2)}, u32[]{:S(2)}) %collective-permute-start.7) | collective-permute-done | bytes 131104 | tf_op jit(solution)/shard_map/ppermute | solution.py:322
  41.6 0.0 collective-permute-start.12
  41.6 0.3 collective-permute-done.8.refs_8_
  41.9 2.9 %collective-permute-start.13 = (bf16[256,256]{1,0:T(8,128)(2,1)S(1)}, bf16[256,256]{1,0:T(8,128)(2,1)S(1)}, u32[]{:S(2)}, u32[]{:S(2)}) collective-permute-start(bf16[256,256]{1,0:T(8,128)(2,1)S(1)} %get-tuple-element.54), channel_id=1, source_target_pairs={{0,6},{1,7},{2,0},{3,1},{4,2},{5,3},{6,4},{7,5},{8,14},{9,15},{10,... | collective-permute-start | bytes 393224 | tf_op jit(solution)/shard_map/ppermute | solution.py:322
  44.8 3.9 %grads.1.first = f32[200,256]{1,0:T(8,128)S(1)} custom-call(f32[512,1024]{1,0:T(8,128)S(1)} %get-tuple-element.59.grad_spec, f32[512,1024]{1,0:T(8,128)S(1)} %get-tuple-element.60.series_spec, f32[512,256]{1,0:T(8,128)S(1)} %get-tuple-element.61.taps_spec, f32[512,1024]{1,0:T(8,128)S(1)} %get-tuple-element.62.long_spec, bf16[16,256]{1,0:T(8,128)(2,1)S(1)} %copy-done.9, ...), custom_call_target="tpu_custom_call" | custom-call | flops 5000000000 | bytes 8077312 | tf_op jit(solution)/shard_map/grads/pallas_call | solution.py:302
  48.7 0.0 collective-permute-done.9.refs_3_
  48.7 2.5 %collective-permute-start.16 = (f32[200,256]{1,0:T(8,128)S(1)}, f32[200,256]{1,0:T(8,128)S(1)}, u32[]{:S(2)}, u32[]{:S(2)}) collective-permute-start(f32[200,256]{1,0:T(8,128)S(1)} %grads.1.first), channel_id=1, source_target_pairs={{0,24},{8,16},{16,8},{24,0},{1,25},{9,17},{17,9},{25,1},{2,26},{10... | collective-permute-start | bytes 614408 | tf_op jit(solution)/shard_map/ppermute | solution.py:342
  51.2 3.1 %collective-permute-done.10.refs_4_ = bf16[256,256]{1,0:T(8,128)(2,1)S(1)} collective-permute-done((bf16[256,256]{1,0:T(8,128)(2,1)S(1)}, bf16[256,256]{1,0:T(8,128)(2,1)S(1)}, u32[]{:S(2)}, u32[]{:S(2)}) %collective-permute-start.10) | collective-permute-done | bytes 131104 | tf_op jit(solution)/shard_map/ppermute | solution.py:322
  54.3 1.5 %collective-permute-start.15 = (f32[200,256]{1,0:T(8,128)S(1)}, f32[200,256]{1,0:T(8,128)S(1)}, u32[]{:S(2)}, u32[]{:S(2)}) collective-permute-start(f32[200,256]{1,0:T(8,128)S(1)} %grads.1.first), channel_id=1, source_target_pairs={{0,16},{8,24},{16,0},{24,8},{1,17},{9,25},{17,1},{25,9},{2,18},{10... | collective-permute-start | bytes 614408 | tf_op jit(solution)/shard_map/ppermute | solution.py:342
  55.8 0.0 collective-permute-done.11.refs_5_
  55.8 1.5 %collective-permute-start.14 = (f32[200,256]{1,0:T(8,128)S(1)}, f32[200,256]{1,0:T(8,128)S(1)}, u32[]{:S(2)}, u32[]{:S(2)}) collective-permute-start(f32[200,256]{1,0:T(8,128)S(1)} %grads.1.first), channel_id=1, source_target_pairs={{0,8},{8,0},{16,24},{24,16},{1,9},{9,1},{17,25},{25,17},{2,10},{10... | collective-permute-start | bytes 614408 | tf_op jit(solution)/shard_map/ppermute | solution.py:342
  57.3 0.0 collective-permute-done.12.refs_6_
  57.3 0.0 collective-permute-done.13.refs_7_
  57.3 1.4 %gate.1 = (bf16[128,2048]{1,0:T(8,128)(2,1)}, bf16[128,2048]{1,0:T(8,128)(2,1)}, bf16[128,2048]{1,0:T(8,128)(2,1)}) custom-call(s32[1]{0:T(128)} %bitcast.me_ref.refs_0_, bf16[256,256]{1,0:T(8,128)(2,1)S(1)} %get-tuple-element.45.refs_1_, bf16[256,256]{1,0:T(8,128)(2,1)S(1)} %collective-permute-done.7.refs_2_, ...), custom_call_target="tpu_custom_call" | custom-call | flops 1000000000 | bytes 3670020 | tf_op jit(solution)/shard_map/gate/pallas_call | solution.py:302
  58.7 0.0 collective-permute-done.16.fourth
  58.7 3.3 %collective-permute-done.15.third = f32[200,256]{1,0:T(8,128)S(1)} collective-permute-done((f32[200,256]{1,0:T(8,128)S(1)}, f32[200,256]{1,0:T(8,128)S(1)}, u32[]{:S(2)}, u32[]{:S(2)}) %collective-permute-start.15) | collective-permute-done | bytes 204832 | tf_op jit(solution)/shard_map/ppermute | solution.py:342
  62.0 1.0 %collective-permute-done.14.second = f32[200,256]{1,0:T(8,128)S(1)} collective-permute-done((f32[200,256]{1,0:T(8,128)S(1)}, f32[200,256]{1,0:T(8,128)S(1)}, u32[]{:S(2)}, u32[]{:S(2)}) %collective-permute-start.14) | collective-permute-done | bytes 204832 | tf_op jit(solution)/shard_map/ppermute | solution.py:342
  63.0 0.7 %finish.1 = (f32[16,1024]{1,0:T(8,128)}, f32[128,256]{1,0:T(8,128)}, f32[1,256]{1,0:T(1,128)}) custom-call(f32[200,256]{1,0:T(8,128)S(1)} %grads.1.first, f32[200,256]{1,0:T(8,128)S(1)} %collective-permute-done.14.second, f32[200,256]{1,0:T(8,128)S(1)} %collective-permute-done.15.third, f32[200,256]{1,0:T(8,128)S(1)} %collective-permute-done.16.fourth), custom_call_target="tpu_custom_call" | custom-call | flops 1000000000 | bytes 1016832 | tf_op jit(solution)/shard_map/finish/pallas_call | solution.py:302
  (15 shorter events, 0.0 us)
Async XLA Ops:
  0.6 10.9 %copy-start = (bf16[128,2048]{1,0:T(8,128)(2,1)S(1)}, bf16[128,2048]{1,0:T(8,128)(2,1)}, u32[]{:S(2)}) copy-start(bf16[128,2048]{1,0:T(8,128)(2,1)} %param.15) | copy-start | bytes 1572868
  0.6 15.5 %copy-start.5 = (bf16[256,512]{1,0:T(8,128)(2,1)S(1)}, bf16[256,512]{1,0:T(8,128)(2,1)}, u32[]{:S(2)}) copy-start(bf16[256,512]{1,0:T(8,128)(2,1)} %constant.23.clone.inv_low.refs_12_) | copy-start | bytes 786436
  0.7 15.5 %copy-start.6 = (bf16[256,512]{1,0:T(8,128)(2,1)S(1)}, bf16[256,512]{1,0:T(8,128)(2,1)}, u32[]{:S(2)}) copy-start(bf16[256,512]{1,0:T(8,128)(2,1)} %constant.22.clone.inv_high.refs_11_) | copy-start | bytes 786436
  0.7 15.5 %copy-start.7 = (bf16[512,256]{1,0:T(8,128)(2,1)S(1)}, bf16[512,256]{1,0:T(8,128)(2,1)}, u32[]{:S(2)}) copy-start(bf16[512,256]{1,0:T(8,128)(2,1)} %constant.21.clone.fwd_low.refs_10_) | copy-start | bytes 786436
  0.7 15.5 %copy-start.8 = (bf16[512,256]{1,0:T(8,128)(2,1)S(1)}, bf16[512,256]{1,0:T(8,128)(2,1)}, u32[]{:S(2)}) copy-start(bf16[512,256]{1,0:T(8,128)(2,1)} %constant.20.clone.fwd_high.refs_9_) | copy-start | bytes 786436
  0.7 15.5 %copy-start.9 = (bf16[16,256]{1,0:T(8,128)(2,1)S(1)}, bf16[16,256]{1,0:T(8,128)(2,1)}, u32[]{:S(2)}) copy-start(bf16[16,256]{1,0:T(8,128)(2,1)} %constant.24.clone.member) | copy-start | bytes 24580
  0.7 15.5 %copy-start.4 = (f32[256]{0:T(256)S(1)}, f32[256]{0:T(256)}, u32[]{:S(2)}) copy-start(f32[256]{0:T(256)} %param.16) | copy-start | bytes 3076
  0.7 15.5 %copy-start.3 = (f32[16,1024]{1,0:T(8,128)S(1)}, f32[16,1024]{1,0:T(8,128)}, u32[]{:S(2)}) copy-start(f32[16,1024]{1,0:T(8,128)} %long_filter.1) | copy-start | bytes 196612
  3.4 8.1 %collective-permute-start = (bf16[256,256]{1,0:T(8,128)(2,1)}, bf16[256,256]{1,0:T(8,128)(2,1)S(1)}, u32[]{:S(2)}, u32[]{:S(2)}) collective-permute-start(bf16[256,256]{1,0:T(8,128)(2,1)} %get-tuple-element.37), channel_id=1, source_target_pairs={{0,1},{1,2},{2,3},{3,4},{4,5},{5,6},{6,7},{7,0},{8,9},{9,10},{10,1... | collective-permute-start | bytes 393224 | tf_op jit(solution)/shard_map/ppermute | solution.py:322
  3.9 10.0 %collective-permute-start.1 = (bf16[256,256]{1,0:T(8,128)(2,1)}, bf16[256,256]{1,0:T(8,128)(2,1)S(1)}, u32[]{:S(2)}, u32[]{:S(2)}) collective-permute-start(bf16[256,256]{1,0:T(8,128)(2,1)} %get-tuple-element.38), channel_id=1, source_target_pairs={{0,2},{1,3},{2,4},{3,5},{4,6},{5,7},{6,0},{7,1},{8,10},{9,11},{10,... | collective-permute-start | bytes 393224 | tf_op jit(solution)/shard_map/ppermute | solution.py:322
  6.6 16.8 %collective-permute-start.2 = (bf16[256,256]{1,0:T(8,128)(2,1)}, bf16[256,256]{1,0:T(8,128)(2,1)S(1)}, u32[]{:S(2)}, u32[]{:S(2)}) collective-permute-start(bf16[256,256]{1,0:T(8,128)(2,1)} %get-tuple-element.39), channel_id=1, source_target_pairs={{0,3},{1,4},{2,5},{3,6},{4,7},{5,0},{6,1},{7,2},{8,11},{9,12},{10,... | collective-permute-start | bytes 393224 | tf_op jit(solution)/shard_map/ppermute | solution.py:322
  9.1 14.5 %collective-permute-start.3 = (bf16[256,256]{1,0:T(8,128)(2,1)}, bf16[256,256]{1,0:T(8,128)(2,1)S(1)}, u32[]{:S(2)}, u32[]{:S(2)}) collective-permute-start(bf16[256,256]{1,0:T(8,128)(2,1)} %get-tuple-element.40), channel_id=1, source_target_pairs={{0,4},{1,5},{2,6},{3,7},{4,0},{5,1},{6,2},{7,3},{8,12},{9,13},{10,... | collective-permute-start | bytes 393224 | tf_op jit(solution)/shard_map/ppermute | solution.py:322
  10.3 13.2 %collective-permute-start.4 = (bf16[256,256]{1,0:T(8,128)(2,1)}, bf16[256,256]{1,0:T(8,128)(2,1)S(1)}, u32[]{:S(2)}, u32[]{:S(2)}) collective-permute-start(bf16[256,256]{1,0:T(8,128)(2,1)} %get-tuple-element.41), channel_id=1, source_target_pairs={{0,5},{1,6},{2,7},{3,0},{4,1},{5,2},{6,3},{7,4},{8,13},{9,14},{10,... | collective-permute-start | bytes 393224 | tf_op jit(solution)/shard_map/ppermute | solution.py:322
  11.6 12.0 %collective-permute-start.5 = (bf16[256,256]{1,0:T(8,128)(2,1)}, bf16[256,256]{1,0:T(8,128)(2,1)S(1)}, u32[]{:S(2)}, u32[]{:S(2)}) collective-permute-start(bf16[256,256]{1,0:T(8,128)(2,1)} %get-tuple-element.42), channel_id=1, source_target_pairs={{0,6},{1,7},{2,0},{3,1},{4,2},{5,3},{6,4},{7,5},{8,14},{9,15},{10,... | collective-permute-start | bytes 393224 | tf_op jit(solution)/shard_map/ppermute | solution.py:322
  14.0 10.3 %collective-permute-start.6 = (bf16[256,256]{1,0:T(8,128)(2,1)}, bf16[256,256]{1,0:T(8,128)(2,1)S(1)}, u32[]{:S(2)}, u32[]{:S(2)}) collective-permute-start(bf16[256,256]{1,0:T(8,128)(2,1)} %get-tuple-element.43), channel_id=1, source_target_pairs={{0,7},{1,0},{2,1},{3,2},{4,3},{5,4},{6,5},{7,6},{8,15},{9,8},{10,9... | collective-permute-start | bytes 393224 | tf_op jit(solution)/shard_map/ppermute | solution.py:322
  16.2 8.0 %copy-start.10 = (bf16[256,256]{1,0:T(8,128)(2,1)S(1)}, bf16[256,256]{1,0:T(8,128)(2,1)}, u32[]{:S(2)}) copy-start(bf16[256,256]{1,0:T(8,128)(2,1)} %get-tuple-element.36.refs_1_) | copy-start | bytes 393220
  28.8 12.8 %collective-permute-start.7 = (bf16[256,256]{1,0:T(8,128)(2,1)S(1)}, bf16[256,256]{1,0:T(8,128)(2,1)S(1)}, u32[]{:S(2)}, u32[]{:S(2)}) collective-permute-start(bf16[256,256]{1,0:T(8,128)(2,1)S(1)} %get-tuple-element.46), channel_id=1, source_target_pairs={{0,1},{1,2},{2,3},{3,4},{4,5},{5,6},{6,7},{7,0},{8,9},{9,10},{10,1... | collective-permute-start | bytes 393224 | tf_op jit(solution)/shard_map/ppermute | solution.py:322
  30.9 11.0 %collective-permute-start.8 = (bf16[256,256]{1,0:T(8,128)(2,1)S(1)}, bf16[256,256]{1,0:T(8,128)(2,1)S(1)}, u32[]{:S(2)}, u32[]{:S(2)}) collective-permute-start(bf16[256,256]{1,0:T(8,128)(2,1)S(1)} %get-tuple-element.47), channel_id=1, source_target_pairs={{0,7},{1,0},{2,1},{3,2},{4,3},{5,4},{6,5},{7,6},{8,15},{9,8},{10,9... | collective-permute-start | bytes 393224 | tf_op jit(solution)/shard_map/ppermute | solution.py:322
  38.3 10.4 %collective-permute-start.9 = (bf16[256,256]{1,0:T(8,128)(2,1)S(1)}, bf16[256,256]{1,0:T(8,128)(2,1)S(1)}, u32[]{:S(2)}, u32[]{:S(2)}) collective-permute-start(bf16[256,256]{1,0:T(8,128)(2,1)S(1)} %get-tuple-element.50), channel_id=1, source_target_pairs={{0,2},{1,3},{2,4},{3,5},{4,6},{5,7},{6,0},{7,1},{8,10},{9,11},{10,... | collective-permute-start | bytes 393224 | tf_op jit(solution)/shard_map/ppermute | solution.py:322
  38.3 16.0 %collective-permute-start.10 = (bf16[256,256]{1,0:T(8,128)(2,1)S(1)}, bf16[256,256]{1,0:T(8,128)(2,1)S(1)}, u32[]{:S(2)}, u32[]{:S(2)}) collective-permute-start(bf16[256,256]{1,0:T(8,128)(2,1)S(1)} %get-tuple-element.51), channel_id=1, source_target_pairs={{0,3},{1,4},{2,5},{3,6},{4,7},{5,0},{6,1},{7,2},{8,11},{9,12},{10,... | collective-permute-start | bytes 393224 | tf_op jit(solution)/shard_map/ppermute | solution.py:322
  38.3 17.5 %collective-permute-start.11 = (bf16[256,256]{1,0:T(8,128)(2,1)S(1)}, bf16[256,256]{1,0:T(8,128)(2,1)S(1)}, u32[]{:S(2)}, u32[]{:S(2)}) collective-permute-start(bf16[256,256]{1,0:T(8,128)(2,1)S(1)} %get-tuple-element.52), channel_id=1, source_target_pairs={{0,4},{1,5},{2,6},{3,7},{4,0},{5,1},{6,2},{7,3},{8,12},{9,13},{10,... | collective-permute-start | bytes 393224 | tf_op jit(solution)/shard_map/ppermute | solution.py:322
  41.6 15.6 %collective-permute-start.12 = (bf16[256,256]{1,0:T(8,128)(2,1)S(1)}, bf16[256,256]{1,0:T(8,128)(2,1)S(1)}, u32[]{:S(2)}, u32[]{:S(2)}) collective-permute-start(bf16[256,256]{1,0:T(8,128)(2,1)S(1)} %get-tuple-element.53), channel_id=1, source_target_pairs={{0,5},{1,6},{2,7},{3,0},{4,1},{5,2},{6,3},{7,4},{8,13},{9,14},{10,... | collective-permute-start | bytes 393224 | tf_op jit(solution)/shard_map/ppermute | solution.py:322
  41.9 15.3 %collective-permute-start.13 = (bf16[256,256]{1,0:T(8,128)(2,1)S(1)}, bf16[256,256]{1,0:T(8,128)(2,1)S(1)}, u32[]{:S(2)}, u32[]{:S(2)}) collective-permute-start(bf16[256,256]{1,0:T(8,128)(2,1)S(1)} %get-tuple-element.54), channel_id=1, source_target_pairs={{0,6},{1,7},{2,0},{3,1},{4,2},{5,3},{6,4},{7,5},{8,14},{9,15},{10,... | collective-permute-start | bytes 393224 | tf_op jit(solution)/shard_map/ppermute | solution.py:322
  44.8 12.5 %copy-start.1 = (bf16[1,128,2048]{2,1,0:T(8,128)(2,1)S(1)}, bf16[1,128,2048]{2,1,0:T(8,128)(2,1)}, u32[]{:S(2)}) copy-start(bf16[1,128,2048]{2,1,0:T(8,128)(2,1)} %param.12) | copy-start | bytes 1572868
  44.8 12.5 %copy-start.2 = (bf16[1,128,2048]{2,1,0:T(8,128)(2,1)S(1)}, bf16[1,128,2048]{2,1,0:T(8,128)(2,1)}, u32[]{:S(2)}) copy-start(bf16[1,128,2048]{2,1,0:T(8,128)(2,1)} %param.13) | copy-start | bytes 1572868
  48.7 10.0 %collective-permute-start.16 = (f32[200,256]{1,0:T(8,128)S(1)}, f32[200,256]{1,0:T(8,128)S(1)}, u32[]{:S(2)}, u32[]{:S(2)}) collective-permute-start(f32[200,256]{1,0:T(8,128)S(1)} %grads.1.first), channel_id=1, source_target_pairs={{0,24},{8,16},{16,8},{24,0},{1,25},{9,17},{17,9},{25,1},{2,26},{10... | collective-permute-start | bytes 614408 | tf_op jit(solution)/shard_map/ppermute | solution.py:342
  54.3 7.7 %collective-permute-start.15 = (f32[200,256]{1,0:T(8,128)S(1)}, f32[200,256]{1,0:T(8,128)S(1)}, u32[]{:S(2)}, u32[]{:S(2)}) collective-permute-start(f32[200,256]{1,0:T(8,128)S(1)} %grads.1.first), channel_id=1, source_target_pairs={{0,16},{8,24},{16,0},{24,8},{1,17},{9,25},{17,1},{25,9},{2,18},{10... | collective-permute-start | bytes 614408 | tf_op jit(solution)/shard_map/ppermute | solution.py:342
  55.8 7.2 %collective-permute-start.14 = (f32[200,256]{1,0:T(8,128)S(1)}, f32[200,256]{1,0:T(8,128)S(1)}, u32[]{:S(2)}, u32[]{:S(2)}) collective-permute-start(f32[200,256]{1,0:T(8,128)S(1)} %grads.1.first), channel_id=1, source_target_pairs={{0,8},{8,0},{16,24},{24,16},{1,9},{9,1},{17,25},{25,17},{2,10},{10... | collective-permute-start | bytes 614408 | tf_op jit(solution)/shard_map/ppermute | solution.py:342

commit v4 on v3

--- a/solution.py
+++ b/solution.py
@@ -77,10 +77,10 @@
     return pl.ds(row, rows), pl.ds(column, width)
 
 
-def gather_blocks(me_ref, blocks, which, whole):
+def gather_blocks(me_ref, order, blocks, which, whole):
     (rows, width), count = blocks[0].shape, len(blocks)
     rows //= 2
-    for shift, ref in enumerate(blocks):
+    for shift, ref in zip(order, blocks):
         at = place_of(me_ref, -shift, count, rows, width, whole.shape[0])
         whole[at] = ref[which * rows : (which + 1) * rows, :]
 
@@ -135,7 +135,8 @@
     chunks(block, window)
 
 
-def conv_kernel(count, *refs):
+def conv_kernel(order, *refs):
+    count = len(order)
     me_ref, blocks, refs = refs[0], refs[1 : 1 + count], refs[1 + count :]
     fwd_high, fwd_low, inv_high, inv_low, both_spec = refs[:5]
     outs, (series_spec, grad_spec, whole, high) = refs[5 : 5 + count], refs[5 + count :]
@@ -145,7 +146,7 @@
 
     for which, spec in enumerate((series_spec, grad_spec)):
         backward = which == 1
-        gather_blocks(me_ref, blocks, which, whole)
+        gather_blocks(me_ref, order, blocks, which, whole)
         spec[...] = mm(fwd_high[...], whole[...]) + mm(fwd_low[...], whole[...])
 
         def product(re, im):
@@ -275,7 +276,9 @@
 
     def total(at, rows):
         here = pl.ds(at, rows)
-        return ((first[here, :] + second[here, :]) + (third[here, :] + fourth[here, :])) * scale
+        first_pair = first[here, :].astype(F32) + second[here, :].astype(F32)
+        last_pair = third[here, :].astype(F32) + fourth[here, :].astype(F32)
+        return (first_pair + last_pair) * scale
 
     taps_grad[...] = total(0, tap_count)[:, :width]
     skip_grad[...] = total(tap_count, 8)[:1, :width]
@@ -283,12 +286,13 @@
         long_grad[:, lanes(piece, padded)] = total(tap_count + 8 + piece * groups, groups)
 
 
-def gate_kernel(count, *refs):
+def gate_kernel(order, *refs):
+    count = len(order)
     me_ref, blocks, refs = refs[0], refs[1 : 1 + count], refs[1 + count :]
     gating, upstream, output, gate_grad, signal_grad = refs
     rows = gating.shape[0]
     width = blocks[0].shape[1]
-    for shift, ref in enumerate(blocks):
+    for shift, ref in zip(order, blocks):
         source = lax.rem(me_ref[0] + (count - shift), count)
         columns = pl.ds(pl.multiple_of(source * width, width), width)
         conv = ref[:rows, :].astype(F32)
@@ -339,6 +343,7 @@
 
 
 def shares(value, axis):
+    value = value.astype(BF16)
     return [value] + [lax.ppermute(value, axis, [(i, i ^ flip) for i in range(4)]) for flip in (1, 2, 3)]
 
 
@@ -386,7 +391,9 @@
     else:
         grad_gate = (upstream.astype(F32) * gating.astype(F32)).astype(BF16)
         sent = columns_for(jnp.concatenate([series, grad_gate]), me, count)
-    received = [pad(x) for x in exchange(sent, "ctx", range(1, count))]
+    out_order = [0, 1, 2, 3, 4, 5, 6, 7] if count == 8 else list(range(count))
+    back_order = [0, 1, 2, 7, 3, 5, 4, 6] if count == 8 else list(range(count))
+    received = [pad(x) for x in exchange(sent, "ctx", out_order[1:])]
     own_taps = pad(lax.dynamic_slice_in_dim(short_taps, me * width, width, 1))
     taps_spec, long_spec, both_spec = call(
         filters_kernel,
@@ -399,8 +406,8 @@
     )
 
     *outs, series_spec, grad_spec = call(
-        functools.partial(conv_kernel, count),
-        [where, *received, *tables, both_spec],
+        functools.partial(conv_kernel, out_order),
+        [where, *[received[k] for k in out_order], *tables, both_spec],
         [jax.ShapeDtypeStruct((2 * rows, padded), BF16)] * count + [spectrum_out] * 2,
         [((block, parts * padded), BF16), (spectrum, BF16)],
         budget,
@@ -409,7 +416,7 @@
     )
     outs = trim(outs)
     early, late = [1, 7], []
-    returned = exchange(outs, "ctx", [1, 7, 4, 3, 5, 2, 6] if count == 8 else range(1, count))
+    returned = exchange(outs, "ctx", back_order[1:])
     *waited, grad_spec = lax.optimization_barrier([returned[k] for k in early] + [grad_spec])
     for k, value in zip(early, waited):
         returned[k] = value
@@ -445,8 +452,8 @@
     full = jax.ShapeDtypeStruct((rows, channels), BF16)
     if width % 128 == 0:
         output, gate_grad, signal_grad = call(
-            functools.partial(gate_kernel, count),
-            [where, *returned, gating, upstream],
+            functools.partial(gate_kernel, back_order),
+            [where, *[returned[k] for k in back_order], gating, upstream],
             [full, full, full],
             [],
             budget,

time: 64 us -> 62.1 us (0.970); the launches traced: 63.7 us -> 61.2 us
  waiting for transfers between devices: 11.7 us -> 7.77 us
  starting transfers between devices: 32.1 us -> 33.4 us
    ppermute x3, waiting for transfers between devices: 4.26 us -> 0.95 us  [shares(): lax.ppermute(value, axis, [(i, i ^ flip) for i in range(4)])]
    ppermute x14, starting transfers between devices: 26.6 us -> 27.9 us  [exchange(): lax.ppermute(blocks[k], axis, [(i, (i + k) % count) for i in range(count)])]
  transfers between devices with their start and end apart: 17 -> 17, of which waited for: 8 -> 8; matrix products, arithmetic and copies ran while one was open for 0% -> 0% of each run, Pallas kernels for 17% -> 18%
where the time goes in v4:
time: 62.1 us; the launch traced here: 61.2 us
  starting transfers between devices  33.4 us (54%)
  Pallas kernels  19.1 us (31%)
  waiting for transfers between devices  7.77 us (13%)
  between operations  0.81 us (1%)
    ppermute x14, starting transfers between devices, exchange(): lax.ppermute(blocks[k], axis, [(i, (i + k) % count) for i in range(count)])  27.9 us
    pallas_call x6, Pallas kernels, call(): pl.pallas_call(kernel, out_shape=outs, in_specs=[SMEM if x.dtype == jnp.i...  19.1 us
    ppermute x14, waiting for transfers between devices, exchange(): lax.ppermute(blocks[k], axis, [(i, (i + k) % count) for i in range(count)])  6.81 us
    ppermute x3, starting transfers between devices, shares(): lax.ppermute(value, axis, [(i, i ^ flip) for i in range(4)])  5.51 us
  transfers between devices with their start and end apart: 17, of which 8 were waited for; matrix products, arithmetic and copies ran while one was open for 0% of the time, Pallas kernels for 18%

profile of v4, /device:TPU:0, one launch (start us, length us, event | category | flops | bytes accessed | tf_op | source)
XLA Modules:
  0.0 61.2 jit_solution(4829596029753316298)
XLA Ops:
  0.6 0.0 copy-start
  0.6 0.0 copy-start.5
  0.7 0.0 copy-start.6
  0.7 0.0 copy-start.7
  0.7 0.0 copy-start.8
  0.7 0.0 copy-start.9
  0.7 2.7 %prepare.1 = (bf16[256,256]{1,0:T(8,128)(2,1)}, bf16[256,256]{1,0:T(8,128)(2,1)}, bf16[256,256]{1,0:T(8,128)(2,1)}, bf16[256,256]{1,0:T(8,128)(2,1)}, bf16[256,2...) custom-call(s32[1]{0:T(128)} %bitcast.me_ref.refs_0_, ...), custom_call_target="tpu_custom_call" | custom-call | flops 1000000000 | bytes 2621444 | tf_op jit(solution)/shard_map/prepare/pallas_call | solution.py:306
  3.4 0.5 collective-permute-start
  3.9 2.6 %collective-permute-start.1 = (bf16[256,256]{1,0:T(8,128)(2,1)}, bf16[256,256]{1,0:T(8,128)(2,1)S(1)}, u32[]{:S(2)}, u32[]{:S(2)}) collective-permute-start(bf16[256,256]{1,0:T(8,128)(2,1)} %get-tuple-element.38), channel_id=1, source_target_pairs={{0,2},{1,3},{2,4},{3,5},{4,6},{5,7},{6,0},{7,1},{8,10},{9,11},{10,... | collective-permute-start | bytes 393224 | tf_op jit(solution)/shard_map/ppermute | solution.py:326
  6.6 2.5 %collective-permute-start.2 = (bf16[256,256]{1,0:T(8,128)(2,1)}, bf16[256,256]{1,0:T(8,128)(2,1)S(1)}, u32[]{:S(2)}, u32[]{:S(2)}) collective-permute-start(bf16[256,256]{1,0:T(8,128)(2,1)} %get-tuple-element.39), channel_id=1, source_target_pairs={{0,3},{1,4},{2,5},{3,6},{4,7},{5,0},{6,1},{7,2},{8,11},{9,12},{10,... | collective-permute-start | bytes 393224 | tf_op jit(solution)/shard_map/ppermute | solution.py:326
  9.1 1.2 %collective-permute-start.3 = (bf16[256,256]{1,0:T(8,128)(2,1)}, bf16[256,256]{1,0:T(8,128)(2,1)S(1)}, u32[]{:S(2)}, u32[]{:S(2)}) collective-permute-start(bf16[256,256]{1,0:T(8,128)(2,1)} %get-tuple-element.40), channel_id=1, source_target_pairs={{0,4},{1,5},{2,6},{3,7},{4,0},{5,1},{6,2},{7,3},{8,12},{9,13},{10,... | collective-permute-start | bytes 393224 | tf_op jit(solution)/shard_map/ppermute | solution.py:326
  10.3 1.2 %collective-permute-start.4 = (bf16[256,256]{1,0:T(8,128)(2,1)}, bf16[256,256]{1,0:T(8,128)(2,1)S(1)}, u32[]{:S(2)}, u32[]{:S(2)}) collective-permute-start(bf16[256,256]{1,0:T(8,128)(2,1)} %get-tuple-element.41), channel_id=1, source_target_pairs={{0,5},{1,6},{2,7},{3,0},{4,1},{5,2},{6,3},{7,4},{8,13},{9,14},{10,... | collective-permute-start | bytes 393224 | tf_op jit(solution)/shard_map/ppermute | solution.py:326
  11.5 0.0 copy-done
  11.5 0.0 collective-permute-done.refs_2_
  11.6 2.4 %collective-permute-start.5 = (bf16[256,256]{1,0:T(8,128)(2,1)}, bf16[256,256]{1,0:T(8,128)(2,1)S(1)}, u32[]{:S(2)}, u32[]{:S(2)}) collective-permute-start(bf16[256,256]{1,0:T(8,128)(2,1)} %get-tuple-element.42), channel_id=1, source_target_pairs={{0,6},{1,7},{2,0},{3,1},{4,2},{5,3},{6,4},{7,5},{8,14},{9,15},{10,... | collective-permute-start | bytes 393224 | tf_op jit(solution)/shard_map/ppermute | solution.py:326
  14.0 0.0 collective-permute-done.1.refs_3_
  14.0 2.2 %collective-permute-start.6 = (bf16[256,256]{1,0:T(8,128)(2,1)}, bf16[256,256]{1,0:T(8,128)(2,1)S(1)}, u32[]{:S(2)}, u32[]{:S(2)}) collective-permute-start(bf16[256,256]{1,0:T(8,128)(2,1)} %get-tuple-element.43), channel_id=1, source_target_pairs={{0,7},{1,0},{2,1},{3,2},{4,3},{5,4},{6,5},{7,6},{8,15},{9,8},{10,9... | collective-permute-start | bytes 393224 | tf_op jit(solution)/shard_map/ppermute | solution.py:326
  16.2 0.0 copy-start.10
  16.2 5.7 %filters.1 = (f32[512,256]{1,0:T(8,128)S(1)}, f32[512,1024]{1,0:T(8,128)S(1)}, f32[512,1024]{1,0:T(8,128)S(1)}) custom-call(bf16[128,256]{1,0:T(8,128)(2,1)S(1)} %constant_dynamic-slice_fusion.taps, f32[16,1024]{1,0:T(8,128)S(1)} %copy-done.3, bf16[16,256]{1,0:T(8,128)(2,1)S(1)} %copy-done.9, f32[1,256]{1,0:T(1,128)S(1)} %bitcast.13, ...), custom_call_target="tpu_custom_call" | custom-call | flops 5000000000 | bytes 5907456 | tf_op jit(solution)/shard_map/filters/pallas_call | solution.py:306
  21.9 1.4 %collective-permute-done.2.refs_4_ = bf16[256,256]{1,0:T(8,128)(2,1)S(1)} collective-permute-done((bf16[256,256]{1,0:T(8,128)(2,1)}, bf16[256,256]{1,0:T(8,128)(2,1)S(1)}, u32[]{:S(2)}, u32[]{:S(2)}) %collective-permute-start.2) | collective-permute-done | bytes 131104 | tf_op jit(solution)/shard_map/ppermute | solution.py:326
  23.4 0.2 collective-permute-done.3.refs_5_
  23.6 0.0 collective-permute-done.4.refs_6_
  23.6 0.0 collective-permute-done.5.refs_7_
  23.6 0.7 %collective-permute-done.6.refs_8_ = bf16[256,256]{1,0:T(8,128)(2,1)S(1)} collective-permute-done((bf16[256,256]{1,0:T(8,128)(2,1)}, bf16[256,256]{1,0:T(8,128)(2,1)S(1)}, u32[]{:S(2)}, u32[]{:S(2)}) %collective-permute-start.6) | collective-permute-done | bytes 131104 | tf_op jit(solution)/shard_map/ppermute | solution.py:326
  24.2 4.6 %conv.1 = (bf16[256,256]{1,0:T(8,128)(2,1)S(1)}, bf16[256,256]{1,0:T(8,128)(2,1)S(1)}, bf16[256,256]{1,0:T(8,128)(2,1)S(1)}, bf16[256,256]{1,0:T(8,128)(2,1)S(1)...) custom-call(s32[1]{0:T(128)} %bitcast.me_ref.refs_0_, ...), custom_call_target="tpu_custom_call" | custom-call | flops 8000000000 | bytes 9437188 | tf_op jit(solution)/shard_map/conv/pallas_call | solution.py:306
  28.8 2.0 %collective-permute-start.7 = (bf16[256,256]{1,0:T(8,128)(2,1)S(1)}, bf16[256,256]{1,0:T(8,128)(2,1)S(1)}, u32[]{:S(2)}, u32[]{:S(2)}) collective-permute-start(bf16[256,256]{1,0:T(8,128)(2,1)S(1)} %get-tuple-element.46), channel_id=1, source_target_pairs={{0,1},{1,2},{2,3},{3,4},{4,5},{5,6},{6,7},{7,0},{8,9},{9,10},{10,1... | collective-permute-start | bytes 393224 | tf_op jit(solution)/shard_map/ppermute | solution.py:326
  30.9 7.4 %collective-permute-start.8 = (bf16[256,256]{1,0:T(8,128)(2,1)S(1)}, bf16[256,256]{1,0:T(8,128)(2,1)S(1)}, u32[]{:S(2)}, u32[]{:S(2)}) collective-permute-start(bf16[256,256]{1,0:T(8,128)(2,1)S(1)} %get-tuple-element.47), channel_id=1, source_target_pairs={{0,7},{1,0},{2,1},{3,2},{4,3},{5,4},{6,5},{7,6},{8,15},{9,8},{10,9... | collective-permute-start | bytes 393224 | tf_op jit(solution)/shard_map/ppermute | solution.py:326
  38.3 0.0 collective-permute-start.9
  38.3 0.0 collective-permute-start.10
  38.3 2.6 %collective-permute-start.11 = (bf16[256,256]{1,0:T(8,128)(2,1)S(1)}, bf16[256,256]{1,0:T(8,128)(2,1)S(1)}, u32[]{:S(2)}, u32[]{:S(2)}) collective-permute-start(bf16[256,256]{1,0:T(8,128)(2,1)S(1)} %get-tuple-element.53), channel_id=1, source_target_pairs={{0,5},{1,6},{2,7},{3,0},{4,1},{5,2},{6,3},{7,4},{8,13},{9,14},{10,... | collective-permute-start | bytes 393224 | tf_op jit(solution)/shard_map/ppermute | solution.py:326
  40.9 0.7 %collective-permute-done.7.refs_2_ = bf16[256,256]{1,0:T(8,128)(2,1)S(1)} collective-permute-done((bf16[256,256]{1,0:T(8,128)(2,1)S(1)}, bf16[256,256]{1,0:T(8,128)(2,1)S(1)}, u32[]{:S(2)}, u32[]{:S(2)}) %collective-permute-start.7) | collective-permute-done | bytes 131104 | tf_op jit(solution)/shard_map/ppermute | solution.py:326
  41.6 0.2 collective-permute-start.12
  41.8 0.1 collective-permute-done.8.refs_4_
  41.9 2.9 %collective-permute-start.13 = (bf16[256,256]{1,0:T(8,128)(2,1)S(1)}, bf16[256,256]{1,0:T(8,128)(2,1)S(1)}, u32[]{:S(2)}, u32[]{:S(2)}) collective-permute-start(bf16[256,256]{1,0:T(8,128)(2,1)S(1)} %get-tuple-element.55), channel_id=1, source_target_pairs={{0,6},{1,7},{2,0},{3,1},{4,2},{5,3},{6,4},{7,5},{8,14},{9,15},{10,... | collective-permute-start | bytes 393224 | tf_op jit(solution)/shard_map/ppermute | solution.py:326
  44.8 3.9 %grads.1 = f32[200,256]{1,0:T(8,128)S(1)} custom-call(f32[512,1024]{1,0:T(8,128)S(1)} %get-tuple-element.59.grad_spec, f32[512,1024]{1,0:T(8,128)S(1)} %get-tuple-element.60.series_spec, f32[512,256]{1,0:T(8,128)S(1)} %get-tuple-element.61.taps_spec, f32[512,1024]{1,0:T(8,128)S(1)} %get-tuple-element.62.long_spec, bf16[16,256]{1,0:T(8,128)(2,1)S(1)} %copy-done.9, ...), custom_call_target="tpu_custom_call" | custom-call | flops 5000000000 | bytes 8077312 | tf_op jit(solution)/shard_map/grads/pallas_call | solution.py:306
  48.8 0.0 collective-permute-done.9.refs_3_
  48.8 2.5 %collective-permute-start.16 = (bf16[200,256]{1,0:T(8,128)(2,1)S(1)}, bf16[200,256]{1,0:T(8,128)(2,1)S(1)}, u32[]{:S(2)}, u32[]{:S(2)}) collective-permute-start(bf16[200,256]{1,0:T(8,128)(2,1)S(1)} %convert_element_type.3.first), channel_id=1, source_target_pairs={{0,24},{8,16},{16,8},{24,0},{1,25},{9,17},{17,9},{25,1},{2,26},{10... | collective-permute-start | bytes 307208 | tf_op jit(solution)/shard_map/ppermute | solution.py:347
  51.3 3.0 %collective-permute-done.10.refs_5_ = bf16[256,256]{1,0:T(8,128)(2,1)S(1)} collective-permute-done((bf16[256,256]{1,0:T(8,128)(2,1)S(1)}, bf16[256,256]{1,0:T(8,128)(2,1)S(1)}, u32[]{:S(2)}, u32[]{:S(2)}) %collective-permute-start.10) | collective-permute-done | bytes 131104 | tf_op jit(solution)/shard_map/ppermute | solution.py:326
  54.3 1.5 %collective-permute-start.15 = (bf16[200,256]{1,0:T(8,128)(2,1)S(1)}, bf16[200,256]{1,0:T(8,128)(2,1)S(1)}, u32[]{:S(2)}, u32[]{:S(2)}) collective-permute-start(bf16[200,256]{1,0:T(8,128)(2,1)S(1)} %convert_element_type.3.first), channel_id=1, source_target_pairs={{0,16},{8,24},{16,0},{24,8},{1,17},{9,25},{17,1},{25,9},{2,18},{10... | collective-permute-start | bytes 307208 | tf_op jit(solution)/shard_map/ppermute | solution.py:347
  55.8 0.0 collective-permute-done.11.refs_6_
  55.8 1.5 %collective-permute-start.14 = (bf16[200,256]{1,0:T(8,128)(2,1)S(1)}, bf16[200,256]{1,0:T(8,128)(2,1)S(1)}, u32[]{:S(2)}, u32[]{:S(2)}) collective-permute-start(bf16[200,256]{1,0:T(8,128)(2,1)S(1)} %convert_element_type.3.first), channel_id=1, source_target_pairs={{0,8},{8,0},{16,24},{24,16},{1,9},{9,1},{17,25},{25,17},{2,10},{10... | collective-permute-start | bytes 307208 | tf_op jit(solution)/shard_map/ppermute | solution.py:347
  57.3 0.8 %collective-permute-done.12.refs_7_ = bf16[256,256]{1,0:T(8,128)(2,1)S(1)} collective-permute-done((bf16[256,256]{1,0:T(8,128)(2,1)S(1)}, bf16[256,256]{1,0:T(8,128)(2,1)S(1)}, u32[]{:S(2)}, u32[]{:S(2)}) %collective-permute-start.12) | collective-permute-done | bytes 131104 | tf_op jit(solution)/shard_map/ppermute | solution.py:326
  58.0 0.0 collective-permute-done.13.refs_8_
  58.0 1.4 %gate.1 = (bf16[128,2048]{1,0:T(8,128)(2,1)}, bf16[128,2048]{1,0:T(8,128)(2,1)}, bf16[128,2048]{1,0:T(8,128)(2,1)}) custom-call(s32[1]{0:T(128)} %bitcast.me_ref.refs_0_, bf16[256,256]{1,0:T(8,128)(2,1)S(1)} %get-tuple-element.45.refs_1_, bf16[256,256]{1,0:T(8,128)(2,1)S(1)} %collective-permute-done.7.refs_2_, ...), custom_call_target="tpu_custom_call" | custom-call | flops 1000000000 | bytes 3670020 | tf_op jit(solution)/shard_map/gate/pallas_call | solution.py:306
  59.5 0.0 collective-permute-done.16.fourth
  59.5 0.0 collective-permute-done.15.third
  59.5 0.9 %collective-permute-done.14.second = bf16[200,256]{1,0:T(8,128)(2,1)S(1)} collective-permute-done((bf16[200,256]{1,0:T(8,128)(2,1)S(1)}, bf16[200,256]{1,0:T(8,128)(2,1)S(1)}, u32[]{:S(2)}, u32[]{:S(2)}) %collective-permute-start.14) | collective-permute-done | bytes 102432 | tf_op jit(solution)/shard_map/ppermute | solution.py:347
  60.4 0.7 %finish.1 = (f32[16,1024]{1,0:T(8,128)}, f32[128,256]{1,0:T(8,128)}, f32[1,256]{1,0:T(1,128)}) custom-call(bf16[200,256]{1,0:T(8,128)(2,1)S(1)} %convert_element_type.3.first, bf16[200,256]{1,0:T(8,128)(2,1)S(1)} %collective-permute-done.14.second, bf16[200,256]{1,0:T(8,128)(2,1)S(1)} %collective-permute-done.15.third, ...), custom_call_target="tpu_custom_call" | custom-call | flops 1000000000 | bytes 607232 | tf_op jit(solution)/shard_map/finish/pallas_call | solution.py:306
  (16 shorter events, 0.1 us)
Async XLA Ops:
  0.6 10.9 %copy-start = (bf16[128,2048]{1,0:T(8,128)(2,1)S(1)}, bf16[128,2048]{1,0:T(8,128)(2,1)}, u32[]{:S(2)}) copy-start(bf16[128,2048]{1,0:T(8,128)(2,1)} %param.15) | copy-start | bytes 1572868
  0.6 15.5 %copy-start.5 = (bf16[256,512]{1,0:T(8,128)(2,1)S(1)}, bf16[256,512]{1,0:T(8,128)(2,1)}, u32[]{:S(2)}) copy-start(bf16[256,512]{1,0:T(8,128)(2,1)} %constant.23.clone.inv_low.refs_12_) | copy-start | bytes 786436
  0.7 15.5 %copy-start.6 = (bf16[256,512]{1,0:T(8,128)(2,1)S(1)}, bf16[256,512]{1,0:T(8,128)(2,1)}, u32[]{:S(2)}) copy-start(bf16[256,512]{1,0:T(8,128)(2,1)} %constant.22.clone.inv_high.refs_11_) | copy-start | bytes 786436
  0.7 15.5 %copy-start.7 = (bf16[512,256]{1,0:T(8,128)(2,1)S(1)}, bf16[512,256]{1,0:T(8,128)(2,1)}, u32[]{:S(2)}) copy-start(bf16[512,256]{1,0:T(8,128)(2,1)} %constant.21.clone.fwd_low.refs_10_) | copy-start | bytes 786436
  0.7 15.5 %copy-start.8 = (bf16[512,256]{1,0:T(8,128)(2,1)S(1)}, bf16[512,256]{1,0:T(8,128)(2,1)}, u32[]{:S(2)}) copy-start(bf16[512,256]{1,0:T(8,128)(2,1)} %constant.20.clone.fwd_high.refs_9_) | copy-start | bytes 786436
  0.7 15.5 %copy-start.9 = (bf16[16,256]{1,0:T(8,128)(2,1)S(1)}, bf16[16,256]{1,0:T(8,128)(2,1)}, u32[]{:S(2)}) copy-start(bf16[16,256]{1,0:T(8,128)(2,1)} %constant.24.clone.member) | copy-start | bytes 24580
  0.7 15.5 %copy-start.4 = (f32[256]{0:T(256)S(1)}, f32[256]{0:T(256)}, u32[]{:S(2)}) copy-start(f32[256]{0:T(256)} %param.16) | copy-start | bytes 3076
  0.7 15.5 %copy-start.3 = (f32[16,1024]{1,0:T(8,128)S(1)}, f32[16,1024]{1,0:T(8,128)}, u32[]{:S(2)}) copy-start(f32[16,1024]{1,0:T(8,128)} %long_filter.1) | copy-start | bytes 196612
  3.4 8.1 %collective-permute-start = (bf16[256,256]{1,0:T(8,128)(2,1)}, bf16[256,256]{1,0:T(8,128)(2,1)S(1)}, u32[]{:S(2)}, u32[]{:S(2)}) collective-permute-start(bf16[256,256]{1,0:T(8,128)(2,1)} %get-tuple-element.37), channel_id=1, source_target_pairs={{0,1},{1,2},{2,3},{3,4},{4,5},{5,6},{6,7},{7,0},{8,9},{9,10},{10,1... | collective-permute-start | bytes 393224 | tf_op jit(solution)/shard_map/ppermute | solution.py:326
  3.9 10.0 %collective-permute-start.1 = (bf16[256,256]{1,0:T(8,128)(2,1)}, bf16[256,256]{1,0:T(8,128)(2,1)S(1)}, u32[]{:S(2)}, u32[]{:S(2)}) collective-permute-start(bf16[256,256]{1,0:T(8,128)(2,1)} %get-tuple-element.38), channel_id=1, source_target_pairs={{0,2},{1,3},{2,4},{3,5},{4,6},{5,7},{6,0},{7,1},{8,10},{9,11},{10,... | collective-permute-start | bytes 393224 | tf_op jit(solution)/shard_map/ppermute | solution.py:326
  6.6 16.8 %collective-permute-start.2 = (bf16[256,256]{1,0:T(8,128)(2,1)}, bf16[256,256]{1,0:T(8,128)(2,1)S(1)}, u32[]{:S(2)}, u32[]{:S(2)}) collective-permute-start(bf16[256,256]{1,0:T(8,128)(2,1)} %get-tuple-element.39), channel_id=1, source_target_pairs={{0,3},{1,4},{2,5},{3,6},{4,7},{5,0},{6,1},{7,2},{8,11},{9,12},{10,... | collective-permute-start | bytes 393224 | tf_op jit(solution)/shard_map/ppermute | solution.py:326
  9.1 14.5 %collective-permute-start.3 = (bf16[256,256]{1,0:T(8,128)(2,1)}, bf16[256,256]{1,0:T(8,128)(2,1)S(1)}, u32[]{:S(2)}, u32[]{:S(2)}) collective-permute-start(bf16[256,256]{1,0:T(8,128)(2,1)} %get-tuple-element.40), channel_id=1, source_target_pairs={{0,4},{1,5},{2,6},{3,7},{4,0},{5,1},{6,2},{7,3},{8,12},{9,13},{10,... | collective-permute-start | bytes 393224 | tf_op jit(solution)/shard_map/ppermute | solution.py:326
  10.3 13.2 %collective-permute-start.4 = (bf16[256,256]{1,0:T(8,128)(2,1)}, bf16[256,256]{1,0:T(8,128)(2,1)S(1)}, u32[]{:S(2)}, u32[]{:S(2)}) collective-permute-start(bf16[256,256]{1,0:T(8,128)(2,1)} %get-tuple-element.41), channel_id=1, source_target_pairs={{0,5},{1,6},{2,7},{3,0},{4,1},{5,2},{6,3},{7,4},{8,13},{9,14},{10,... | collective-permute-start | bytes 393224 | tf_op jit(solution)/shard_map/ppermute | solution.py:326
  11.6 12.0 %collective-permute-start.5 = (bf16[256,256]{1,0:T(8,128)(2,1)}, bf16[256,256]{1,0:T(8,128)(2,1)S(1)}, u32[]{:S(2)}, u32[]{:S(2)}) collective-permute-start(bf16[256,256]{1,0:T(8,128)(2,1)} %get-tuple-element.42), channel_id=1, source_target_pairs={{0,6},{1,7},{2,0},{3,1},{4,2},{5,3},{6,4},{7,5},{8,14},{9,15},{10,... | collective-permute-start | bytes 393224 | tf_op jit(solution)/shard_map/ppermute | solution.py:326
  14.0 10.3 %collective-permute-start.6 = (bf16[256,256]{1,0:T(8,128)(2,1)}, bf16[256,256]{1,0:T(8,128)(2,1)S(1)}, u32[]{:S(2)}, u32[]{:S(2)}) collective-permute-start(bf16[256,256]{1,0:T(8,128)(2,1)} %get-tuple-element.43), channel_id=1, source_target_pairs={{0,7},{1,0},{2,1},{3,2},{4,3},{5,4},{6,5},{7,6},{8,15},{9,8},{10,9... | collective-permute-start | bytes 393224 | tf_op jit(solution)/shard_map/ppermute | solution.py:326
  16.2 8.0 %copy-start.10 = (bf16[256,256]{1,0:T(8,128)(2,1)S(1)}, bf16[256,256]{1,0:T(8,128)(2,1)}, u32[]{:S(2)}) copy-start(bf16[256,256]{1,0:T(8,128)(2,1)} %get-tuple-element.36.refs_1_) | copy-start | bytes 393220
  28.8 12.8 %collective-permute-start.7 = (bf16[256,256]{1,0:T(8,128)(2,1)S(1)}, bf16[256,256]{1,0:T(8,128)(2,1)S(1)}, u32[]{:S(2)}, u32[]{:S(2)}) collective-permute-start(bf16[256,256]{1,0:T(8,128)(2,1)S(1)} %get-tuple-element.46), channel_id=1, source_target_pairs={{0,1},{1,2},{2,3},{3,4},{4,5},{5,6},{6,7},{7,0},{8,9},{9,10},{10,1... | collective-permute-start | bytes 393224 | tf_op jit(solution)/shard_map/ppermute | solution.py:326
  30.9 11.0 %collective-permute-start.8 = (bf16[256,256]{1,0:T(8,128)(2,1)S(1)}, bf16[256,256]{1,0:T(8,128)(2,1)S(1)}, u32[]{:S(2)}, u32[]{:S(2)}) collective-permute-start(bf16[256,256]{1,0:T(8,128)(2,1)S(1)} %get-tuple-element.47), channel_id=1, source_target_pairs={{0,7},{1,0},{2,1},{3,2},{4,3},{5,4},{6,5},{7,6},{8,15},{9,8},{10,9... | collective-permute-start | bytes 393224 | tf_op jit(solution)/shard_map/ppermute | solution.py:326
  38.3 10.5 %collective-permute-start.9 = (bf16[256,256]{1,0:T(8,128)(2,1)S(1)}, bf16[256,256]{1,0:T(8,128)(2,1)S(1)}, u32[]{:S(2)}, u32[]{:S(2)}) collective-permute-start(bf16[256,256]{1,0:T(8,128)(2,1)S(1)} %get-tuple-element.50), channel_id=1, source_target_pairs={{0,2},{1,3},{2,4},{3,5},{4,6},{5,7},{6,0},{7,1},{8,10},{9,11},{10,... | collective-permute-start | bytes 393224 | tf_op jit(solution)/shard_map/ppermute | solution.py:326
  38.3 16.0 %collective-permute-start.10 = (bf16[256,256]{1,0:T(8,128)(2,1)S(1)}, bf16[256,256]{1,0:T(8,128)(2,1)S(1)}, u32[]{:S(2)}, u32[]{:S(2)}) collective-permute-start(bf16[256,256]{1,0:T(8,128)(2,1)S(1)} %get-tuple-element.52), channel_id=1, source_target_pairs={{0,3},{1,4},{2,5},{3,6},{4,7},{5,0},{6,1},{7,2},{8,11},{9,12},{10,... | collective-permute-start | bytes 393224 | tf_op jit(solution)/shard_map/ppermute | solution.py:326
  38.3 17.5 %collective-permute-start.11 = (bf16[256,256]{1,0:T(8,128)(2,1)S(1)}, bf16[256,256]{1,0:T(8,128)(2,1)S(1)}, u32[]{:S(2)}, u32[]{:S(2)}) collective-permute-start(bf16[256,256]{1,0:T(8,128)(2,1)S(1)} %get-tuple-element.53), channel_id=1, source_target_pairs={{0,5},{1,6},{2,7},{3,0},{4,1},{5,2},{6,3},{7,4},{8,13},{9,14},{10,... | collective-permute-start | bytes 393224 | tf_op jit(solution)/shard_map/ppermute | solution.py:326
  41.6 16.4 %collective-permute-start.12 = (bf16[256,256]{1,0:T(8,128)(2,1)S(1)}, bf16[256,256]{1,0:T(8,128)(2,1)S(1)}, u32[]{:S(2)}, u32[]{:S(2)}) collective-permute-start(bf16[256,256]{1,0:T(8,128)(2,1)S(1)} %get-tuple-element.54), channel_id=1, source_target_pairs={{0,4},{1,5},{2,6},{3,7},{4,0},{5,1},{6,2},{7,3},{8,12},{9,13},{10,... | collective-permute-start | bytes 393224 | tf_op jit(solution)/shard_map/ppermute | solution.py:326
  41.9 16.1 %collective-permute-start.13 = (bf16[256,256]{1,0:T(8,128)(2,1)S(1)}, bf16[256,256]{1,0:T(8,128)(2,1)S(1)}, u32[]{:S(2)}, u32[]{:S(2)}) collective-permute-start(bf16[256,256]{1,0:T(8,128)(2,1)S(1)} %get-tuple-element.55), channel_id=1, source_target_pairs={{0,6},{1,7},{2,0},{3,1},{4,2},{5,3},{6,4},{7,5},{8,14},{9,15},{10,... | collective-permute-start | bytes 393224 | tf_op jit(solution)/shard_map/ppermute | solution.py:326
  44.8 13.2 %copy-start.1 = (bf16[1,128,2048]{2,1,0:T(8,128)(2,1)S(1)}, bf16[1,128,2048]{2,1,0:T(8,128)(2,1)}, u32[]{:S(2)}) copy-start(bf16[1,128,2048]{2,1,0:T(8,128)(2,1)} %param.12) | copy-start | bytes 1572868
  44.8 13.2 %copy-start.2 = (bf16[1,128,2048]{2,1,0:T(8,128)(2,1)S(1)}, bf16[1,128,2048]{2,1,0:T(8,128)(2,1)}, u32[]{:S(2)}) copy-start(bf16[1,128,2048]{2,1,0:T(8,128)(2,1)} %param.13) | copy-start | bytes 1572868
  48.8 10.7 %collective-permute-start.16 = (bf16[200,256]{1,0:T(8,128)(2,1)S(1)}, bf16[200,256]{1,0:T(8,128)(2,1)S(1)}, u32[]{:S(2)}, u32[]{:S(2)}) collective-permute-start(bf16[200,256]{1,0:T(8,128)(2,1)S(1)} %convert_element_type.3.first), channel_id=1, source_target_pairs={{0,24},{8,16},{16,8},{24,0},{1,25},{9,17},{17,9},{25,1},{2,26},{10... | collective-permute-start | bytes 307208 | tf_op jit(solution)/shard_map/ppermute | solution.py:347
  54.3 5.2 %collective-permute-start.15 = (bf16[200,256]{1,0:T(8,128)(2,1)S(1)}, bf16[200,256]{1,0:T(8,128)(2,1)S(1)}, u32[]{:S(2)}, u32[]{:S(2)}) collective-permute-start(bf16[200,256]{1,0:T(8,128)(2,1)S(1)} %convert_element_type.3.first), channel_id=1, source_target_pairs={{0,16},{8,24},{16,0},{24,8},{1,17},{9,25},{17,1},{25,9},{2,18},{10... | collective-permute-start | bytes 307208 | tf_op jit(solution)/shard_map/ppermute | solution.py:347
  55.8 4.7 %collective-permute-start.14 = (bf16[200,256]{1,0:T(8,128)(2,1)S(1)}, bf16[200,256]{1,0:T(8,128)(2,1)S(1)}, u32[]{:S(2)}, u32[]{:S(2)}) collective-permute-start(bf16[200,256]{1,0:T(8,128)(2,1)S(1)} %convert_element_type.3.first), channel_id=1, source_target_pairs={{0,8},{8,0},{16,24},{24,16},{1,9},{9,1},{17,25},{25,17},{2,10},{10... | collective-permute-start | bytes 307208 | tf_op jit(solution)/shard_map/ppermute | solution.py:347

commit v5 on v4

--- a/solution.py
+++ b/solution.py
@@ -77,19 +77,20 @@
     return pl.ds(row, rows), pl.ds(column, width)
 
 
-def gather_blocks(me_ref, order, blocks, which, whole):
+def gather_blocks(me_ref, order, blocks, which, whole, block):
     (rows, width), count = blocks[0].shape, len(blocks)
     rows //= 2
     for shift, ref in zip(order, blocks):
-        at = place_of(me_ref, -shift, count, rows, width, whole.shape[0])
-        whole[at] = ref[which * rows : (which + 1) * rows, :]
-
-
-def scatter_blocks(me_ref, whole, which, blocks):
+        row, column = place_of(me_ref, -shift, count, rows, width, block)
+        part = ref[which * rows : (which + 1) * rows, :]
+        whole[row, column] = part
+
+
+def scatter_blocks(me_ref, whole, which, blocks, block):
     (rows, width), count = blocks[0].shape, len(blocks)
     rows //= 2
     for shift, ref in enumerate(blocks):
-        ref[which * rows : (which + 1) * rows, :] = whole[place_of(me_ref, shift, count, rows, width, whole.shape[0])]
+        ref[which * rows : (which + 1) * rows, :] = whole[place_of(me_ref, shift, count, rows, width, block)]
 
 
 def filters_kernel(
@@ -138,16 +139,16 @@
 def conv_kernel(order, *refs):
     count = len(order)
     me_ref, blocks, refs = refs[0], refs[1 : 1 + count], refs[1 + count :]
-    fwd_high, fwd_low, inv_high, inv_low, both_spec = refs[:5]
-    outs, (series_spec, grad_spec, whole, high) = refs[5 : 5 + count], refs[5 + count :]
-    size, block = fwd_high.shape
+    forward, inward, both_spec = refs[:3]
+    outs, (series_spec, grad_spec, whole, product_spec) = refs[3 : 3 + count], refs[3 + count :]
+    block = inward.shape[0]
     width = blocks[0].shape[1]
     parts = series_spec.shape[1] // width
 
     for which, spec in enumerate((series_spec, grad_spec)):
         backward = which == 1
-        gather_blocks(me_ref, order, blocks, which, whole)
-        spec[...] = mm(fwd_high[...], whole[...]) + mm(fwd_low[...], whole[...])
+        gather_blocks(me_ref, order, blocks, which, whole, block)
+        spec[...] = mm(forward[...], whole[...])
 
         def product(re, im):
             for i in range(parts):
@@ -162,12 +163,12 @@
                     else:
                         sum_re = sum_re + (c_re * x_re - c_im * x_im)
                         sum_im = sum_im + (c_re * x_im + c_im * x_re)
-                high[re, lanes(i, width)] = sum_re.astype(BF16)
-                high[im, lanes(i, width)] = sum_im.astype(BF16)
+                product_spec[re, lanes(i, width)] = sum_re.astype(BF16)
+                product_spec[im, lanes(i, width)] = sum_im.astype(BF16)
 
         chunks(block, product)
-        whole[...] = (mm(inv_high[...], high[...]) + mm(inv_low[...], high[...])).astype(BF16)
-        scatter_blocks(me_ref, whole, which, outs)
+        whole[...] = mm(inward[...], product_spec[...]).astype(BF16)
+        scatter_blocks(me_ref, whole, which, outs, block)
 
 
 def grads_kernel(
@@ -374,6 +375,7 @@
     spectrum_out = jax.ShapeDtypeStruct(spectrum, F32)
     budget = 10 * 4 * math.prod(spectrum)
     tables = [jnp.asarray(t) for t in dft_tables(block)]
+    forward, inward = tables[0], tables[2]
     channel = np.arange(padded)[None, :]
     of_group = (channel // (width // groups) == np.arange(groups)[:, None]) & (channel < width)
     member = jnp.asarray(of_group.astype(ml_dtypes.bfloat16))
@@ -407,9 +409,12 @@
 
     *outs, series_spec, grad_spec = call(
         functools.partial(conv_kernel, out_order),
-        [where, *[received[k] for k in out_order], *tables, both_spec],
+        [where, *[received[k] for k in out_order], forward, inward, both_spec],
         [jax.ShapeDtypeStruct((2 * rows, padded), BF16)] * count + [spectrum_out] * 2,
-        [((block, parts * padded), BF16), (spectrum, BF16)],
+        [
+            ((block, parts * padded), BF16),
+            (spectrum, BF16),
+        ],
         budget,
         8,
         "conv",

time: 62.1 us -> 61.1 us (0.984)
  Pallas kernels: 19.1 us -> 18.1 us
    pallas_call x6, Pallas kernels: 19.1 us -> 18.1 us  [call(): pl.pallas_call(kernel, out_shape=outs, in_specs=[SMEM if x.dtype == jnp.i...]
where the time goes in v5:
time: 61.1 us; the launch traced here: 60.2 us
  starting transfers between devices  33.4 us (55%)
  Pallas kernels  18.1 us (30%)
  waiting for transfers between devices  7.8 us (13%)
  between operations  0.81 us (1%)
    ppermute x14, starting transfers between devices, exchange(): lax.ppermute(blocks[k], axis, [(i, (i + k) % count) for i in range(count)])  27.9 us
    pallas_call x6, Pallas kernels, call(): pl.pallas_call(kernel, out_shape=outs, in_specs=[SMEM if x.dtype == jnp.i...  18.1 us
    ppermute x14, waiting for transfers between devices, exchange(): lax.ppermute(blocks[k], axis, [(i, (i + k) % count) for i in range(count)])  6.86 us
    ppermute x3, starting transfers between devices, shares(): lax.ppermute(value, axis, [(i, i ^ flip) for i in range(4)])  5.5 us
  transfers between devices with their start and end apart: 17, of which 8 were waited for; matrix products, arithmetic and copies ran while one was open for 0% of the time, Pallas kernels for 18%

profile of v5, /device:TPU:0, one launch (start us, length us, event | category | flops | bytes accessed | tf_op | source)
XLA Modules:
  0.0 60.2 jit_solution(519760310203490451)
XLA Ops:
  0.6 0.0 copy-start
  0.6 0.0 copy-start.5
  0.7 0.0 copy-start.6
  0.7 0.0 copy-start.9
  0.7 0.0 copy-start.7
  0.7 0.0 copy-start.8
  0.7 2.7 %prepare.1 = (bf16[256,256]{1,0:T(8,128)(2,1)}, bf16[256,256]{1,0:T(8,128)(2,1)}, bf16[256,256]{1,0:T(8,128)(2,1)}, bf16[256,256]{1,0:T(8,128)(2,1)}, bf16[256,2...) custom-call(s32[1]{0:T(128)} %bitcast.me_ref.refs_0_, ...), custom_call_target="tpu_custom_call" | custom-call | flops 1000000000 | bytes 2621444 | tf_op jit(solution)/shard_map/prepare/pallas_call | solution.py:307
  3.4 0.5 collective-permute-start
  3.9 2.6 %collective-permute-start.1 = (bf16[256,256]{1,0:T(8,128)(2,1)}, bf16[256,256]{1,0:T(8,128)(2,1)S(1)}, u32[]{:S(2)}, u32[]{:S(2)}) collective-permute-start(bf16[256,256]{1,0:T(8,128)(2,1)} %get-tuple-element.38), channel_id=1, source_target_pairs={{0,2},{1,3},{2,4},{3,5},{4,6},{5,7},{6,0},{7,1},{8,10},{9,11},{10,... | collective-permute-start | bytes 393224 | tf_op jit(solution)/shard_map/ppermute | solution.py:327
  6.6 2.5 %collective-permute-start.2 = (bf16[256,256]{1,0:T(8,128)(2,1)}, bf16[256,256]{1,0:T(8,128)(2,1)S(1)}, u32[]{:S(2)}, u32[]{:S(2)}) collective-permute-start(bf16[256,256]{1,0:T(8,128)(2,1)} %get-tuple-element.39), channel_id=1, source_target_pairs={{0,3},{1,4},{2,5},{3,6},{4,7},{5,0},{6,1},{7,2},{8,11},{9,12},{10,... | collective-permute-start | bytes 393224 | tf_op jit(solution)/shard_map/ppermute | solution.py:327
  9.1 1.2 %collective-permute-start.3 = (bf16[256,256]{1,0:T(8,128)(2,1)}, bf16[256,256]{1,0:T(8,128)(2,1)S(1)}, u32[]{:S(2)}, u32[]{:S(2)}) collective-permute-start(bf16[256,256]{1,0:T(8,128)(2,1)} %get-tuple-element.40), channel_id=1, source_target_pairs={{0,4},{1,5},{2,6},{3,7},{4,0},{5,1},{6,2},{7,3},{8,12},{9,13},{10,... | collective-permute-start | bytes 393224 | tf_op jit(solution)/shard_map/ppermute | solution.py:327
  10.3 1.2 %collective-permute-start.4 = (bf16[256,256]{1,0:T(8,128)(2,1)}, bf16[256,256]{1,0:T(8,128)(2,1)S(1)}, u32[]{:S(2)}, u32[]{:S(2)}) collective-permute-start(bf16[256,256]{1,0:T(8,128)(2,1)} %get-tuple-element.41), channel_id=1, source_target_pairs={{0,5},{1,6},{2,7},{3,0},{4,1},{5,2},{6,3},{7,4},{8,13},{9,14},{10,... | collective-permute-start | bytes 393224 | tf_op jit(solution)/shard_map/ppermute | solution.py:327
  11.5 0.0 copy-done
  11.5 0.0 collective-permute-done.refs_2_
  11.6 2.4 %collective-permute-start.5 = (bf16[256,256]{1,0:T(8,128)(2,1)}, bf16[256,256]{1,0:T(8,128)(2,1)S(1)}, u32[]{:S(2)}, u32[]{:S(2)}) collective-permute-start(bf16[256,256]{1,0:T(8,128)(2,1)} %get-tuple-element.42), channel_id=1, source_target_pairs={{0,6},{1,7},{2,0},{3,1},{4,2},{5,3},{6,4},{7,5},{8,14},{9,15},{10,... | collective-permute-start | bytes 393224 | tf_op jit(solution)/shard_map/ppermute | solution.py:327
  14.0 0.0 collective-permute-done.1.refs_3_
  14.0 2.2 %collective-permute-start.6 = (bf16[256,256]{1,0:T(8,128)(2,1)}, bf16[256,256]{1,0:T(8,128)(2,1)S(1)}, u32[]{:S(2)}, u32[]{:S(2)}) collective-permute-start(bf16[256,256]{1,0:T(8,128)(2,1)} %get-tuple-element.43), channel_id=1, source_target_pairs={{0,7},{1,0},{2,1},{3,2},{4,3},{5,4},{6,5},{7,6},{8,15},{9,8},{10,9... | collective-permute-start | bytes 393224 | tf_op jit(solution)/shard_map/ppermute | solution.py:327
  16.2 0.0 copy-start.10
  16.2 5.7 %filters.1 = (f32[512,256]{1,0:T(8,128)S(1)}, f32[512,1024]{1,0:T(8,128)S(1)}, f32[512,1024]{1,0:T(8,128)S(1)}) custom-call(bf16[128,256]{1,0:T(8,128)(2,1)S(1)} %constant_dynamic-slice_fusion.taps, f32[16,1024]{1,0:T(8,128)S(1)} %copy-done.3, bf16[16,256]{1,0:T(8,128)(2,1)S(1)} %copy-done.9, f32[1,256]{1,0:T(1,128)S(1)} %bitcast.13, ...), custom_call_target="tpu_custom_call" | custom-call | flops 5000000000 | bytes 5907456 | tf_op jit(solution)/shard_map/filters/pallas_call | solution.py:307
  21.9 1.5 %collective-permute-done.2.refs_4_ = bf16[256,256]{1,0:T(8,128)(2,1)S(1)} collective-permute-done((bf16[256,256]{1,0:T(8,128)(2,1)}, bf16[256,256]{1,0:T(8,128)(2,1)S(1)}, u32[]{:S(2)}, u32[]{:S(2)}) %collective-permute-start.2) | collective-permute-done | bytes 131104 | tf_op jit(solution)/shard_map/ppermute | solution.py:327
  23.4 0.2 collective-permute-done.3.refs_5_
  23.6 0.0 collective-permute-done.4.refs_6_
  23.6 0.0 collective-permute-done.5.refs_7_
  23.6 0.7 %collective-permute-done.6.refs_8_ = bf16[256,256]{1,0:T(8,128)(2,1)S(1)} collective-permute-done((bf16[256,256]{1,0:T(8,128)(2,1)}, bf16[256,256]{1,0:T(8,128)(2,1)S(1)}, u32[]{:S(2)}, u32[]{:S(2)}) %collective-permute-start.6) | collective-permute-done | bytes 131104 | tf_op jit(solution)/shard_map/ppermute | solution.py:327
  24.2 3.6 %conv.1 = (bf16[256,256]{1,0:T(8,128)(2,1)S(1)}, bf16[256,256]{1,0:T(8,128)(2,1)S(1)}, bf16[256,256]{1,0:T(8,128)(2,1)S(1)}, bf16[256,256]{1,0:T(8,128)(2,1)S(1)...) custom-call(s32[1]{0:T(128)} %bitcast.me_ref.refs_0_, ...), custom_call_target="tpu_custom_call" | custom-call | flops 8000000000 | bytes 8912900 | tf_op jit(solution)/shard_map/conv/pallas_call | solution.py:307
  27.9 2.0 %collective-permute-start.7 = (bf16[256,256]{1,0:T(8,128)(2,1)S(1)}, bf16[256,256]{1,0:T(8,128)(2,1)S(1)}, u32[]{:S(2)}, u32[]{:S(2)}) collective-permute-start(bf16[256,256]{1,0:T(8,128)(2,1)S(1)} %get-tuple-element.46), channel_id=1, source_target_pairs={{0,1},{1,2},{2,3},{3,4},{4,5},{5,6},{6,7},{7,0},{8,9},{9,10},{10,1... | collective-permute-start | bytes 393224 | tf_op jit(solution)/shard_map/ppermute | solution.py:327
  29.9 7.4 %collective-permute-start.8 = (bf16[256,256]{1,0:T(8,128)(2,1)S(1)}, bf16[256,256]{1,0:T(8,128)(2,1)S(1)}, u32[]{:S(2)}, u32[]{:S(2)}) collective-permute-start(bf16[256,256]{1,0:T(8,128)(2,1)S(1)} %get-tuple-element.47), channel_id=1, source_target_pairs={{0,7},{1,0},{2,1},{3,2},{4,3},{5,4},{6,5},{7,6},{8,15},{9,8},{10,9... | collective-permute-start | bytes 393224 | tf_op jit(solution)/shard_map/ppermute | solution.py:327
  37.3 0.0 collective-permute-start.9
  37.3 0.0 collective-permute-start.10
  37.3 2.6 %collective-permute-start.11 = (bf16[256,256]{1,0:T(8,128)(2,1)S(1)}, bf16[256,256]{1,0:T(8,128)(2,1)S(1)}, u32[]{:S(2)}, u32[]{:S(2)}) collective-permute-start(bf16[256,256]{1,0:T(8,128)(2,1)S(1)} %get-tuple-element.53), channel_id=1, source_target_pairs={{0,5},{1,6},{2,7},{3,0},{4,1},{5,2},{6,3},{7,4},{8,13},{9,14},{10,... | collective-permute-start | bytes 393224 | tf_op jit(solution)/shard_map/ppermute | solution.py:327
  40.0 0.7 %collective-permute-done.7.refs_2_ = bf16[256,256]{1,0:T(8,128)(2,1)S(1)} collective-permute-done((bf16[256,256]{1,0:T(8,128)(2,1)S(1)}, bf16[256,256]{1,0:T(8,128)(2,1)S(1)}, u32[]{:S(2)}, u32[]{:S(2)}) %collective-permute-start.7) | collective-permute-done | bytes 131104 | tf_op jit(solution)/shard_map/ppermute | solution.py:327
  40.7 0.2 collective-permute-start.12
  40.9 0.1 collective-permute-done.8.refs_4_
  40.9 2.9 %collective-permute-start.13 = (bf16[256,256]{1,0:T(8,128)(2,1)S(1)}, bf16[256,256]{1,0:T(8,128)(2,1)S(1)}, u32[]{:S(2)}, u32[]{:S(2)}) collective-permute-start(bf16[256,256]{1,0:T(8,128)(2,1)S(1)} %get-tuple-element.55), channel_id=1, source_target_pairs={{0,6},{1,7},{2,0},{3,1},{4,2},{5,3},{6,4},{7,5},{8,14},{9,15},{10,... | collective-permute-start | bytes 393224 | tf_op jit(solution)/shard_map/ppermute | solution.py:327
  43.9 3.9 %grads.1 = f32[200,256]{1,0:T(8,128)S(1)} custom-call(f32[512,1024]{1,0:T(8,128)S(1)} %get-tuple-element.59.grad_spec, f32[512,1024]{1,0:T(8,128)S(1)} %get-tuple-element.60.series_spec, f32[512,256]{1,0:T(8,128)S(1)} %get-tuple-element.61.taps_spec, f32[512,1024]{1,0:T(8,128)S(1)} %get-tuple-element.62.long_spec, bf16[16,256]{1,0:T(8,128)(2,1)S(1)} %copy-done.9, ...), custom_call_target="tpu_custom_call" | custom-call | flops 5000000000 | bytes 8077312 | tf_op jit(solution)/shard_map/grads/pallas_call | solution.py:307
  47.8 0.0 collective-permute-done.9.refs_3_
  47.8 2.5 %collective-permute-start.16 = (bf16[200,256]{1,0:T(8,128)(2,1)S(1)}, bf16[200,256]{1,0:T(8,128)(2,1)S(1)}, u32[]{:S(2)}, u32[]{:S(2)}) collective-permute-start(bf16[200,256]{1,0:T(8,128)(2,1)S(1)} %convert_element_type.3.first), channel_id=1, source_target_pairs={{0,24},{8,16},{16,8},{24,0},{1,25},{9,17},{17,9},{25,1},{2,26},{10... | collective-permute-start | bytes 307208 | tf_op jit(solution)/shard_map/ppermute | solution.py:348
  50.3 3.0 %collective-permute-done.10.refs_5_ = bf16[256,256]{1,0:T(8,128)(2,1)S(1)} collective-permute-done((bf16[256,256]{1,0:T(8,128)(2,1)S(1)}, bf16[256,256]{1,0:T(8,128)(2,1)S(1)}, u32[]{:S(2)}, u32[]{:S(2)}) %collective-permute-start.10) | collective-permute-done | bytes 131104 | tf_op jit(solution)/shard_map/ppermute | solution.py:327
  53.3 1.5 %collective-permute-start.15 = (bf16[200,256]{1,0:T(8,128)(2,1)S(1)}, bf16[200,256]{1,0:T(8,128)(2,1)S(1)}, u32[]{:S(2)}, u32[]{:S(2)}) collective-permute-start(bf16[200,256]{1,0:T(8,128)(2,1)S(1)} %convert_element_type.3.first), channel_id=1, source_target_pairs={{0,16},{8,24},{16,0},{24,8},{1,17},{9,25},{17,1},{25,9},{2,18},{10... | collective-permute-start | bytes 307208 | tf_op jit(solution)/shard_map/ppermute | solution.py:348
  54.8 0.0 collective-permute-done.11.refs_6_
  54.8 1.5 %collective-permute-start.14 = (bf16[200,256]{1,0:T(8,128)(2,1)S(1)}, bf16[200,256]{1,0:T(8,128)(2,1)S(1)}, u32[]{:S(2)}, u32[]{:S(2)}) collective-permute-start(bf16[200,256]{1,0:T(8,128)(2,1)S(1)} %convert_element_type.3.first), channel_id=1, source_target_pairs={{0,8},{8,0},{16,24},{24,16},{1,9},{9,1},{17,25},{25,17},{2,10},{10... | collective-permute-start | bytes 307208 | tf_op jit(solution)/shard_map/ppermute | solution.py:348
  56.3 0.8 %collective-permute-done.12.refs_7_ = bf16[256,256]{1,0:T(8,128)(2,1)S(1)} collective-permute-done((bf16[256,256]{1,0:T(8,128)(2,1)S(1)}, bf16[256,256]{1,0:T(8,128)(2,1)S(1)}, u32[]{:S(2)}, u32[]{:S(2)}) %collective-permute-start.12) | collective-permute-done | bytes 131104 | tf_op jit(solution)/shard_map/ppermute | solution.py:327
  57.1 0.0 collective-permute-done.13.refs_8_
  57.1 1.4 %gate.1 = (bf16[128,2048]{1,0:T(8,128)(2,1)}, bf16[128,2048]{1,0:T(8,128)(2,1)}, bf16[128,2048]{1,0:T(8,128)(2,1)}) custom-call(s32[1]{0:T(128)} %bitcast.me_ref.refs_0_, bf16[256,256]{1,0:T(8,128)(2,1)S(1)} %get-tuple-element.45.refs_1_, bf16[256,256]{1,0:T(8,128)(2,1)S(1)} %collective-permute-done.7.refs_2_, ...), custom_call_target="tpu_custom_call" | custom-call | flops 1000000000 | bytes 3670020 | tf_op jit(solution)/shard_map/gate/pallas_call | solution.py:307
  58.5 0.0 collective-permute-done.16.fourth
  58.5 0.0 collective-permute-done.15.third
  58.5 0.9 %collective-permute-done.14.second = bf16[200,256]{1,0:T(8,128)(2,1)S(1)} collective-permute-done((bf16[200,256]{1,0:T(8,128)(2,1)S(1)}, bf16[200,256]{1,0:T(8,128)(2,1)S(1)}, u32[]{:S(2)}, u32[]{:S(2)}) %collective-permute-start.14) | collective-permute-done | bytes 102432 | tf_op jit(solution)/shard_map/ppermute | solution.py:348
  59.5 0.7 %finish.1 = (f32[16,1024]{1,0:T(8,128)}, f32[128,256]{1,0:T(8,128)}, f32[1,256]{1,0:T(1,128)}) custom-call(bf16[200,256]{1,0:T(8,128)(2,1)S(1)} %convert_element_type.3.first, bf16[200,256]{1,0:T(8,128)(2,1)S(1)} %collective-permute-done.14.second, bf16[200,256]{1,0:T(8,128)(2,1)S(1)} %collective-permute-done.15.third, ...), custom_call_target="tpu_custom_call" | custom-call | flops 1000000000 | bytes 607232 | tf_op jit(solution)/shard_map/finish/pallas_call | solution.py:307
  (16 shorter events, 0.1 us)
Async XLA Ops:
  0.6 10.9 %copy-start = (bf16[128,2048]{1,0:T(8,128)(2,1)S(1)}, bf16[128,2048]{1,0:T(8,128)(2,1)}, u32[]{:S(2)}) copy-start(bf16[128,2048]{1,0:T(8,128)(2,1)} %param.15) | copy-start | bytes 1572868
  0.6 15.5 %copy-start.5 = (bf16[256,512]{1,0:T(8,128)(2,1)S(1)}, bf16[256,512]{1,0:T(8,128)(2,1)}, u32[]{:S(2)}) copy-start(bf16[256,512]{1,0:T(8,128)(2,1)} %constant.22.clone.inv_high.refs_10_) | copy-start | bytes 786436
  0.7 15.5 %copy-start.6 = (bf16[512,256]{1,0:T(8,128)(2,1)S(1)}, bf16[512,256]{1,0:T(8,128)(2,1)}, u32[]{:S(2)}) copy-start(bf16[512,256]{1,0:T(8,128)(2,1)} %constant.20.clone.fwd_high.refs_9_) | copy-start | bytes 786436
  0.7 15.5 %copy-start.9 = (bf16[16,256]{1,0:T(8,128)(2,1)S(1)}, bf16[16,256]{1,0:T(8,128)(2,1)}, u32[]{:S(2)}) copy-start(bf16[16,256]{1,0:T(8,128)(2,1)} %constant.24.clone.member) | copy-start | bytes 24580
  0.7 15.5 %copy-start.7 = (bf16[256,512]{1,0:T(8,128)(2,1)S(1)}, bf16[256,512]{1,0:T(8,128)(2,1)}, u32[]{:S(2)}) copy-start(bf16[256,512]{1,0:T(8,128)(2,1)} %constant.23.clone.inv_low) | copy-start | bytes 786436
  0.7 15.5 %copy-start.8 = (bf16[512,256]{1,0:T(8,128)(2,1)S(1)}, bf16[512,256]{1,0:T(8,128)(2,1)}, u32[]{:S(2)}) copy-start(bf16[512,256]{1,0:T(8,128)(2,1)} %constant.21.clone.fwd_low) | copy-start | bytes 786436
  0.7 15.5 %copy-start.4 = (f32[256]{0:T(256)S(1)}, f32[256]{0:T(256)}, u32[]{:S(2)}) copy-start(f32[256]{0:T(256)} %param.16) | copy-start | bytes 3076
  0.7 15.5 %copy-start.3 = (f32[16,1024]{1,0:T(8,128)S(1)}, f32[16,1024]{1,0:T(8,128)}, u32[]{:S(2)}) copy-start(f32[16,1024]{1,0:T(8,128)} %long_filter.1) | copy-start | bytes 196612
  3.4 8.1 %collective-permute-start = (bf16[256,256]{1,0:T(8,128)(2,1)}, bf16[256,256]{1,0:T(8,128)(2,1)S(1)}, u32[]{:S(2)}, u32[]{:S(2)}) collective-permute-start(bf16[256,256]{1,0:T(8,128)(2,1)} %get-tuple-element.37), channel_id=1, source_target_pairs={{0,1},{1,2},{2,3},{3,4},{4,5},{5,6},{6,7},{7,0},{8,9},{9,10},{10,1... | collective-permute-start | bytes 393224 | tf_op jit(solution)/shard_map/ppermute | solution.py:327
  3.9 10.0 %collective-permute-start.1 = (bf16[256,256]{1,0:T(8,128)(2,1)}, bf16[256,256]{1,0:T(8,128)(2,1)S(1)}, u32[]{:S(2)}, u32[]{:S(2)}) collective-permute-start(bf16[256,256]{1,0:T(8,128)(2,1)} %get-tuple-element.38), channel_id=1, source_target_pairs={{0,2},{1,3},{2,4},{3,5},{4,6},{5,7},{6,0},{7,1},{8,10},{9,11},{10,... | collective-permute-start | bytes 393224 | tf_op jit(solution)/shard_map/ppermute | solution.py:327
  6.6 16.8 %collective-permute-start.2 = (bf16[256,256]{1,0:T(8,128)(2,1)}, bf16[256,256]{1,0:T(8,128)(2,1)S(1)}, u32[]{:S(2)}, u32[]{:S(2)}) collective-permute-start(bf16[256,256]{1,0:T(8,128)(2,1)} %get-tuple-element.39), channel_id=1, source_target_pairs={{0,3},{1,4},{2,5},{3,6},{4,7},{5,0},{6,1},{7,2},{8,11},{9,12},{10,... | collective-permute-start | bytes 393224 | tf_op jit(solution)/shard_map/ppermute | solution.py:327
  9.1 14.5 %collective-permute-start.3 = (bf16[256,256]{1,0:T(8,128)(2,1)}, bf16[256,256]{1,0:T(8,128)(2,1)S(1)}, u32[]{:S(2)}, u32[]{:S(2)}) collective-permute-start(bf16[256,256]{1,0:T(8,128)(2,1)} %get-tuple-element.40), channel_id=1, source_target_pairs={{0,4},{1,5},{2,6},{3,7},{4,0},{5,1},{6,2},{7,3},{8,12},{9,13},{10,... | collective-permute-start | bytes 393224 | tf_op jit(solution)/shard_map/ppermute | solution.py:327
  10.3 13.2 %collective-permute-start.4 = (bf16[256,256]{1,0:T(8,128)(2,1)}, bf16[256,256]{1,0:T(8,128)(2,1)S(1)}, u32[]{:S(2)}, u32[]{:S(2)}) collective-permute-start(bf16[256,256]{1,0:T(8,128)(2,1)} %get-tuple-element.41), channel_id=1, source_target_pairs={{0,5},{1,6},{2,7},{3,0},{4,1},{5,2},{6,3},{7,4},{8,13},{9,14},{10,... | collective-permute-start | bytes 393224 | tf_op jit(solution)/shard_map/ppermute | solution.py:327
  11.6 12.0 %collective-permute-start.5 = (bf16[256,256]{1,0:T(8,128)(2,1)}, bf16[256,256]{1,0:T(8,128)(2,1)S(1)}, u32[]{:S(2)}, u32[]{:S(2)}) collective-permute-start(bf16[256,256]{1,0:T(8,128)(2,1)} %get-tuple-element.42), channel_id=1, source_target_pairs={{0,6},{1,7},{2,0},{3,1},{4,2},{5,3},{6,4},{7,5},{8,14},{9,15},{10,... | collective-permute-start | bytes 393224 | tf_op jit(solution)/shard_map/ppermute | solution.py:327
  14.0 10.3 %collective-permute-start.6 = (bf16[256,256]{1,0:T(8,128)(2,1)}, bf16[256,256]{1,0:T(8,128)(2,1)S(1)}, u32[]{:S(2)}, u32[]{:S(2)}) collective-permute-start(bf16[256,256]{1,0:T(8,128)(2,1)} %get-tuple-element.43), channel_id=1, source_target_pairs={{0,7},{1,0},{2,1},{3,2},{4,3},{5,4},{6,5},{7,6},{8,15},{9,8},{10,9... | collective-permute-start | bytes 393224 | tf_op jit(solution)/shard_map/ppermute | solution.py:327
  16.2 8.0 %copy-start.10 = (bf16[256,256]{1,0:T(8,128)(2,1)S(1)}, bf16[256,256]{1,0:T(8,128)(2,1)}, u32[]{:S(2)}) copy-start(bf16[256,256]{1,0:T(8,128)(2,1)} %get-tuple-element.36.refs_1_) | copy-start | bytes 393220
  27.9 12.8 %collective-permute-start.7 = (bf16[256,256]{1,0:T(8,128)(2,1)S(1)}, bf16[256,256]{1,0:T(8,128)(2,1)S(1)}, u32[]{:S(2)}, u32[]{:S(2)}) collective-permute-start(bf16[256,256]{1,0:T(8,128)(2,1)S(1)} %get-tuple-element.46), channel_id=1, source_target_pairs={{0,1},{1,2},{2,3},{3,4},{4,5},{5,6},{6,7},{7,0},{8,9},{9,10},{10,1... | collective-permute-start | bytes 393224 | tf_op jit(solution)/shard_map/ppermute | solution.py:327
  29.9 11.0 %collective-permute-start.8 = (bf16[256,256]{1,0:T(8,128)(2,1)S(1)}, bf16[256,256]{1,0:T(8,128)(2,1)S(1)}, u32[]{:S(2)}, u32[]{:S(2)}) collective-permute-start(bf16[256,256]{1,0:T(8,128)(2,1)S(1)} %get-tuple-element.47), channel_id=1, source_target_pairs={{0,7},{1,0},{2,1},{3,2},{4,3},{5,4},{6,5},{7,6},{8,15},{9,8},{10,9... | collective-permute-start | bytes 393224 | tf_op jit(solution)/shard_map/ppermute | solution.py:327
  37.3 10.5 %collective-permute-start.9 = (bf16[256,256]{1,0:T(8,128)(2,1)S(1)}, bf16[256,256]{1,0:T(8,128)(2,1)S(1)}, u32[]{:S(2)}, u32[]{:S(2)}) collective-permute-start(bf16[256,256]{1,0:T(8,128)(2,1)S(1)} %get-tuple-element.50), channel_id=1, source_target_pairs={{0,2},{1,3},{2,4},{3,5},{4,6},{5,7},{6,0},{7,1},{8,10},{9,11},{10,... | collective-permute-start | bytes 393224 | tf_op jit(solution)/shard_map/ppermute | solution.py:327
  37.3 16.0 %collective-permute-start.10 = (bf16[256,256]{1,0:T(8,128)(2,1)S(1)}, bf16[256,256]{1,0:T(8,128)(2,1)S(1)}, u32[]{:S(2)}, u32[]{:S(2)}) collective-permute-start(bf16[256,256]{1,0:T(8,128)(2,1)S(1)} %get-tuple-element.52), channel_id=1, source_target_pairs={{0,3},{1,4},{2,5},{3,6},{4,7},{5,0},{6,1},{7,2},{8,11},{9,12},{10,... | collective-permute-start | bytes 393224 | tf_op jit(solution)/shard_map/ppermute | solution.py:327
  37.3 17.5 %collective-permute-start.11 = (bf16[256,256]{1,0:T(8,128)(2,1)S(1)}, bf16[256,256]{1,0:T(8,128)(2,1)S(1)}, u32[]{:S(2)}, u32[]{:S(2)}) collective-permute-start(bf16[256,256]{1,0:T(8,128)(2,1)S(1)} %get-tuple-element.53), channel_id=1, source_target_pairs={{0,5},{1,6},{2,7},{3,0},{4,1},{5,2},{6,3},{7,4},{8,13},{9,14},{10,... | collective-permute-start | bytes 393224 | tf_op jit(solution)/shard_map/ppermute | solution.py:327
  40.7 16.4 %collective-permute-start.12 = (bf16[256,256]{1,0:T(8,128)(2,1)S(1)}, bf16[256,256]{1,0:T(8,128)(2,1)S(1)}, u32[]{:S(2)}, u32[]{:S(2)}) collective-permute-start(bf16[256,256]{1,0:T(8,128)(2,1)S(1)} %get-tuple-element.54), channel_id=1, source_target_pairs={{0,4},{1,5},{2,6},{3,7},{4,0},{5,1},{6,2},{7,3},{8,12},{9,13},{10,... | collective-permute-start | bytes 393224 | tf_op jit(solution)/shard_map/ppermute | solution.py:327
  40.9 16.1 %collective-permute-start.13 = (bf16[256,256]{1,0:T(8,128)(2,1)S(1)}, bf16[256,256]{1,0:T(8,128)(2,1)S(1)}, u32[]{:S(2)}, u32[]{:S(2)}) collective-permute-start(bf16[256,256]{1,0:T(8,128)(2,1)S(1)} %get-tuple-element.55), channel_id=1, source_target_pairs={{0,6},{1,7},{2,0},{3,1},{4,2},{5,3},{6,4},{7,5},{8,14},{9,15},{10,... | collective-permute-start | bytes 393224 | tf_op jit(solution)/shard_map/ppermute | solution.py:327
  43.9 13.2 %copy-start.1 = (bf16[1,128,2048]{2,1,0:T(8,128)(2,1)S(1)}, bf16[1,128,2048]{2,1,0:T(8,128)(2,1)}, u32[]{:S(2)}) copy-start(bf16[1,128,2048]{2,1,0:T(8,128)(2,1)} %param.12) | copy-start | bytes 1572868
  43.9 13.2 %copy-start.2 = (bf16[1,128,2048]{2,1,0:T(8,128)(2,1)S(1)}, bf16[1,128,2048]{2,1,0:T(8,128)(2,1)}, u32[]{:S(2)}) copy-start(bf16[1,128,2048]{2,1,0:T(8,128)(2,1)} %param.13) | copy-start | bytes 1572868
  47.8 10.7 %collective-permute-start.16 = (bf16[200,256]{1,0:T(8,128)(2,1)S(1)}, bf16[200,256]{1,0:T(8,128)(2,1)S(1)}, u32[]{:S(2)}, u32[]{:S(2)}) collective-permute-start(bf16[200,256]{1,0:T(8,128)(2,1)S(1)} %convert_element_type.3.first), channel_id=1, source_target_pairs={{0,24},{8,16},{16,8},{24,0},{1,25},{9,17},{17,9},{25,1},{2,26},{10... | collective-permute-start | bytes 307208 | tf_op jit(solution)/shard_map/ppermute | solution.py:348
  53.3 5.2 %collective-permute-start.15 = (bf16[200,256]{1,0:T(8,128)(2,1)S(1)}, bf16[200,256]{1,0:T(8,128)(2,1)S(1)}, u32[]{:S(2)}, u32[]{:S(2)}) collective-permute-start(bf16[200,256]{1,0:T(8,128)(2,1)S(1)} %convert_element_type.3.first), channel_id=1, source_target_pairs={{0,16},{8,24},{16,0},{24,8},{1,17},{9,25},{17,1},{25,9},{2,18},{10... | collective-permute-start | bytes 307208 | tf_op jit(solution)/shard_map/ppermute | solution.py:348
  54.8 4.7 %collective-permute-start.14 = (bf16[200,256]{1,0:T(8,128)(2,1)S(1)}, bf16[200,256]{1,0:T(8,128)(2,1)S(1)}, u32[]{:S(2)}, u32[]{:S(2)}) collective-permute-start(bf16[200,256]{1,0:T(8,128)(2,1)S(1)} %convert_element_type.3.first), channel_id=1, source_target_pairs={{0,8},{8,0},{16,24},{24,16},{1,9},{9,1},{17,25},{25,17},{2,10},{10... | collective-permute-start | bytes 307208 | tf_op jit(solution)/shard_map/ppermute | solution.py:348

commit v6 on v5

--- a/solution.py
+++ b/solution.py
@@ -201,7 +201,7 @@
 
     chunks(block, correlate)
     folded = high[:, : parts * width]
-    lags = (mm(inv_high[...], folded) + mm(inv_low[...], folded)).astype(BF16)
+    lags = mm(inv_high[...], folded).astype(BF16)
     lag_spec[...] = mm(fwd_high[...], lags) + mm(fwd_low[...], lags)
     total[...] = jnp.zeros_like(total)
 

time: 61.1 us -> 61.1 us (level)
  no operation moved by 1% of the time
where the time goes in v6:
time: 61.1 us; the launch traced here: 60.2 us
  starting transfers between devices  33.4 us (55%)
  Pallas kernels  17.8 us (29%)
  waiting for transfers between devices  8.07 us (13%)
  between operations  0.81 us (1%)
    ppermute x14, starting transfers between devices, exchange(): lax.ppermute(blocks[k], axis, [(i, (i + k) % count) for i in range(count)])  27.9 us
    pallas_call x6, Pallas kernels, call(): pl.pallas_call(kernel, out_shape=outs, in_specs=[SMEM if x.dtype == jnp.i...  17.8 us
    ppermute x14, waiting for transfers between devices, exchange(): lax.ppermute(blocks[k], axis, [(i, (i + k) % count) for i in range(count)])  7.13 us
    ppermute x3, starting transfers between devices, shares(): lax.ppermute(value, axis, [(i, i ^ flip) for i in range(4)])  5.5 us
  transfers between devices with their start and end apart: 17, of which 8 were waited for; matrix products, arithmetic and copies ran while one was open for 0% of the time, Pallas kernels for 18%

profile of v6, /device:TPU:0, one launch (start us, length us, event | category | flops | bytes accessed | tf_op | source)
XLA Modules:
  0.0 60.2 jit_solution(17355878478021246363)
XLA Ops:
  0.6 0.0 copy-start
  0.6 0.0 copy-start.5
  0.7 0.0 copy-start.6
  0.7 0.0 copy-start.9
  0.7 0.0 copy-start.7
  0.7 0.0 copy-start.8
  0.7 2.7 %prepare.1 = (bf16[256,256]{1,0:T(8,128)(2,1)}, bf16[256,256]{1,0:T(8,128)(2,1)}, bf16[256,256]{1,0:T(8,128)(2,1)}, bf16[256,256]{1,0:T(8,128)(2,1)}, bf16[256,2...) custom-call(s32[1]{0:T(128)} %bitcast.me_ref.refs_0_, ...), custom_call_target="tpu_custom_call" | custom-call | flops 1000000000 | bytes 2621444 | tf_op jit(solution)/shard_map/prepare/pallas_call | solution.py:307
  3.4 0.5 collective-permute-start
  3.9 2.6 %collective-permute-start.1 = (bf16[256,256]{1,0:T(8,128)(2,1)}, bf16[256,256]{1,0:T(8,128)(2,1)S(1)}, u32[]{:S(2)}, u32[]{:S(2)}) collective-permute-start(bf16[256,256]{1,0:T(8,128)(2,1)} %get-tuple-element.38), channel_id=1, source_target_pairs={{0,2},{1,3},{2,4},{3,5},{4,6},{5,7},{6,0},{7,1},{8,10},{9,11},{10,... | collective-permute-start | bytes 393224 | tf_op jit(solution)/shard_map/ppermute | solution.py:327
  6.6 2.5 %collective-permute-start.2 = (bf16[256,256]{1,0:T(8,128)(2,1)}, bf16[256,256]{1,0:T(8,128)(2,1)S(1)}, u32[]{:S(2)}, u32[]{:S(2)}) collective-permute-start(bf16[256,256]{1,0:T(8,128)(2,1)} %get-tuple-element.39), channel_id=1, source_target_pairs={{0,3},{1,4},{2,5},{3,6},{4,7},{5,0},{6,1},{7,2},{8,11},{9,12},{10,... | collective-permute-start | bytes 393224 | tf_op jit(solution)/shard_map/ppermute | solution.py:327
  9.1 1.2 %collective-permute-start.3 = (bf16[256,256]{1,0:T(8,128)(2,1)}, bf16[256,256]{1,0:T(8,128)(2,1)S(1)}, u32[]{:S(2)}, u32[]{:S(2)}) collective-permute-start(bf16[256,256]{1,0:T(8,128)(2,1)} %get-tuple-element.40), channel_id=1, source_target_pairs={{0,4},{1,5},{2,6},{3,7},{4,0},{5,1},{6,2},{7,3},{8,12},{9,13},{10,... | collective-permute-start | bytes 393224 | tf_op jit(solution)/shard_map/ppermute | solution.py:327
  10.3 1.2 %collective-permute-start.4 = (bf16[256,256]{1,0:T(8,128)(2,1)}, bf16[256,256]{1,0:T(8,128)(2,1)S(1)}, u32[]{:S(2)}, u32[]{:S(2)}) collective-permute-start(bf16[256,256]{1,0:T(8,128)(2,1)} %get-tuple-element.41), channel_id=1, source_target_pairs={{0,5},{1,6},{2,7},{3,0},{4,1},{5,2},{6,3},{7,4},{8,13},{9,14},{10,... | collective-permute-start | bytes 393224 | tf_op jit(solution)/shard_map/ppermute | solution.py:327
  11.5 0.0 copy-done
  11.5 0.0 collective-permute-done.refs_2_
  11.6 2.4 %collective-permute-start.5 = (bf16[256,256]{1,0:T(8,128)(2,1)}, bf16[256,256]{1,0:T(8,128)(2,1)S(1)}, u32[]{:S(2)}, u32[]{:S(2)}) collective-permute-start(bf16[256,256]{1,0:T(8,128)(2,1)} %get-tuple-element.42), channel_id=1, source_target_pairs={{0,6},{1,7},{2,0},{3,1},{4,2},{5,3},{6,4},{7,5},{8,14},{9,15},{10,... | collective-permute-start | bytes 393224 | tf_op jit(solution)/shard_map/ppermute | solution.py:327
  14.0 0.0 collective-permute-done.1.refs_3_
  14.0 2.2 %collective-permute-start.6 = (bf16[256,256]{1,0:T(8,128)(2,1)}, bf16[256,256]{1,0:T(8,128)(2,1)S(1)}, u32[]{:S(2)}, u32[]{:S(2)}) collective-permute-start(bf16[256,256]{1,0:T(8,128)(2,1)} %get-tuple-element.43), channel_id=1, source_target_pairs={{0,7},{1,0},{2,1},{3,2},{4,3},{5,4},{6,5},{7,6},{8,15},{9,8},{10,9... | collective-permute-start | bytes 393224 | tf_op jit(solution)/shard_map/ppermute | solution.py:327
  16.2 0.0 copy-start.10
  16.2 5.7 %filters.1 = (f32[512,256]{1,0:T(8,128)S(1)}, f32[512,1024]{1,0:T(8,128)S(1)}, f32[512,1024]{1,0:T(8,128)S(1)}) custom-call(bf16[128,256]{1,0:T(8,128)(2,1)S(1)} %constant_dynamic-slice_fusion.taps, f32[16,1024]{1,0:T(8,128)S(1)} %copy-done.3, bf16[16,256]{1,0:T(8,128)(2,1)S(1)} %copy-done.9, f32[1,256]{1,0:T(1,128)S(1)} %bitcast.13, ...), custom_call_target="tpu_custom_call" | custom-call | flops 5000000000 | bytes 5907456 | tf_op jit(solution)/shard_map/filters/pallas_call | solution.py:307
  21.9 1.5 %collective-permute-done.2.refs_4_ = bf16[256,256]{1,0:T(8,128)(2,1)S(1)} collective-permute-done((bf16[256,256]{1,0:T(8,128)(2,1)}, bf16[256,256]{1,0:T(8,128)(2,1)S(1)}, u32[]{:S(2)}, u32[]{:S(2)}) %collective-permute-start.2) | collective-permute-done | bytes 131104 | tf_op jit(solution)/shard_map/ppermute | solution.py:327
  23.4 0.2 collective-permute-done.3.refs_5_
  23.6 0.0 collective-permute-done.4.refs_6_
  23.6 0.0 collective-permute-done.5.refs_7_
  23.6 0.7 %collective-permute-done.6.refs_8_ = bf16[256,256]{1,0:T(8,128)(2,1)S(1)} collective-permute-done((bf16[256,256]{1,0:T(8,128)(2,1)}, bf16[256,256]{1,0:T(8,128)(2,1)S(1)}, u32[]{:S(2)}, u32[]{:S(2)}) %collective-permute-start.6) | collective-permute-done | bytes 131104 | tf_op jit(solution)/shard_map/ppermute | solution.py:327
  24.2 3.6 %conv.1 = (bf16[256,256]{1,0:T(8,128)(2,1)S(1)}, bf16[256,256]{1,0:T(8,128)(2,1)S(1)}, bf16[256,256]{1,0:T(8,128)(2,1)S(1)}, bf16[256,256]{1,0:T(8,128)(2,1)S(1)...) custom-call(s32[1]{0:T(128)} %bitcast.me_ref.refs_0_, ...), custom_call_target="tpu_custom_call" | custom-call | flops 8000000000 | bytes 8912900 | tf_op jit(solution)/shard_map/conv/pallas_call | solution.py:307
  27.9 2.0 %collective-permute-start.7 = (bf16[256,256]{1,0:T(8,128)(2,1)S(1)}, bf16[256,256]{1,0:T(8,128)(2,1)S(1)}, u32[]{:S(2)}, u32[]{:S(2)}) collective-permute-start(bf16[256,256]{1,0:T(8,128)(2,1)S(1)} %get-tuple-element.46), channel_id=1, source_target_pairs={{0,1},{1,2},{2,3},{3,4},{4,5},{5,6},{6,7},{7,0},{8,9},{9,10},{10,1... | collective-permute-start | bytes 393224 | tf_op jit(solution)/shard_map/ppermute | solution.py:327
  29.9 7.4 %collective-permute-start.8 = (bf16[256,256]{1,0:T(8,128)(2,1)S(1)}, bf16[256,256]{1,0:T(8,128)(2,1)S(1)}, u32[]{:S(2)}, u32[]{:S(2)}) collective-permute-start(bf16[256,256]{1,0:T(8,128)(2,1)S(1)} %get-tuple-element.47), channel_id=1, source_target_pairs={{0,7},{1,0},{2,1},{3,2},{4,3},{5,4},{6,5},{7,6},{8,15},{9,8},{10,9... | collective-permute-start | bytes 393224 | tf_op jit(solution)/shard_map/ppermute | solution.py:327
  37.3 0.0 collective-permute-start.9
  37.3 0.0 collective-permute-start.10
  37.3 2.6 %collective-permute-start.11 = (bf16[256,256]{1,0:T(8,128)(2,1)S(1)}, bf16[256,256]{1,0:T(8,128)(2,1)S(1)}, u32[]{:S(2)}, u32[]{:S(2)}) collective-permute-start(bf16[256,256]{1,0:T(8,128)(2,1)S(1)} %get-tuple-element.53), channel_id=1, source_target_pairs={{0,5},{1,6},{2,7},{3,0},{4,1},{5,2},{6,3},{7,4},{8,13},{9,14},{10,... | collective-permute-start | bytes 393224 | tf_op jit(solution)/shard_map/ppermute | solution.py:327
  40.0 0.7 %collective-permute-done.7.refs_2_ = bf16[256,256]{1,0:T(8,128)(2,1)S(1)} collective-permute-done((bf16[256,256]{1,0:T(8,128)(2,1)S(1)}, bf16[256,256]{1,0:T(8,128)(2,1)S(1)}, u32[]{:S(2)}, u32[]{:S(2)}) %collective-permute-start.7) | collective-permute-done | bytes 131104 | tf_op jit(solution)/shard_map/ppermute | solution.py:327
  40.7 0.2 collective-permute-start.12
  40.9 0.1 collective-permute-done.8.refs_4_
  40.9 2.9 %collective-permute-start.13 = (bf16[256,256]{1,0:T(8,128)(2,1)S(1)}, bf16[256,256]{1,0:T(8,128)(2,1)S(1)}, u32[]{:S(2)}, u32[]{:S(2)}) collective-permute-start(bf16[256,256]{1,0:T(8,128)(2,1)S(1)} %get-tuple-element.55), channel_id=1, source_target_pairs={{0,6},{1,7},{2,0},{3,1},{4,2},{5,3},{6,4},{7,5},{8,14},{9,15},{10,... | collective-permute-start | bytes 393224 | tf_op jit(solution)/shard_map/ppermute | solution.py:327
  43.9 3.6 %grads.1 = f32[200,256]{1,0:T(8,128)S(1)} custom-call(f32[512,1024]{1,0:T(8,128)S(1)} %get-tuple-element.59.grad_spec, f32[512,1024]{1,0:T(8,128)S(1)} %get-tuple-element.60.series_spec, f32[512,256]{1,0:T(8,128)S(1)} %get-tuple-element.61.taps_spec, f32[512,1024]{1,0:T(8,128)S(1)} %get-tuple-element.62.long_spec, bf16[16,256]{1,0:T(8,128)(2,1)S(1)} %copy-done.9, ...), custom_call_target="tpu_custom_call" | custom-call | flops 5000000000 | bytes 8077312 | tf_op jit(solution)/shard_map/grads/pallas_call | solution.py:307
  47.5 0.0 collective-permute-done.9.refs_3_
  47.5 2.5 %collective-permute-start.16 = (bf16[200,256]{1,0:T(8,128)(2,1)S(1)}, bf16[200,256]{1,0:T(8,128)(2,1)S(1)}, u32[]{:S(2)}, u32[]{:S(2)}) collective-permute-start(bf16[200,256]{1,0:T(8,128)(2,1)S(1)} %convert_element_type.3.first), channel_id=1, source_target_pairs={{0,24},{8,16},{16,8},{24,0},{1,25},{9,17},{17,9},{25,1},{2,26},{10... | collective-permute-start | bytes 307208 | tf_op jit(solution)/shard_map/ppermute | solution.py:348
  50.0 3.2 %collective-permute-done.10.refs_5_ = bf16[256,256]{1,0:T(8,128)(2,1)S(1)} collective-permute-done((bf16[256,256]{1,0:T(8,128)(2,1)S(1)}, bf16[256,256]{1,0:T(8,128)(2,1)S(1)}, u32[]{:S(2)}, u32[]{:S(2)}) %collective-permute-start.10) | collective-permute-done | bytes 131104 | tf_op jit(solution)/shard_map/ppermute | solution.py:327
  53.3 1.5 %collective-permute-start.15 = (bf16[200,256]{1,0:T(8,128)(2,1)S(1)}, bf16[200,256]{1,0:T(8,128)(2,1)S(1)}, u32[]{:S(2)}, u32[]{:S(2)}) collective-permute-start(bf16[200,256]{1,0:T(8,128)(2,1)S(1)} %convert_element_type.3.first), channel_id=1, source_target_pairs={{0,16},{8,24},{16,0},{24,8},{1,17},{9,25},{17,1},{25,9},{2,18},{10... | collective-permute-start | bytes 307208 | tf_op jit(solution)/shard_map/ppermute | solution.py:348
  54.8 0.0 collective-permute-done.11.refs_6_
  54.8 1.5 %collective-permute-start.14 = (bf16[200,256]{1,0:T(8,128)(2,1)S(1)}, bf16[200,256]{1,0:T(8,128)(2,1)S(1)}, u32[]{:S(2)}, u32[]{:S(2)}) collective-permute-start(bf16[200,256]{1,0:T(8,128)(2,1)S(1)} %convert_element_type.3.first), channel_id=1, source_target_pairs={{0,8},{8,0},{16,24},{24,16},{1,9},{9,1},{17,25},{25,17},{2,10},{10... | collective-permute-start | bytes 307208 | tf_op jit(solution)/shard_map/ppermute | solution.py:348
  56.3 0.8 %collective-permute-done.12.refs_7_ = bf16[256,256]{1,0:T(8,128)(2,1)S(1)} collective-permute-done((bf16[256,256]{1,0:T(8,128)(2,1)S(1)}, bf16[256,256]{1,0:T(8,128)(2,1)S(1)}, u32[]{:S(2)}, u32[]{:S(2)}) %collective-permute-start.12) | collective-permute-done | bytes 131104 | tf_op jit(solution)/shard_map/ppermute | solution.py:327
  57.1 0.0 collective-permute-done.13.refs_8_
  57.1 1.4 %gate.1 = (bf16[128,2048]{1,0:T(8,128)(2,1)}, bf16[128,2048]{1,0:T(8,128)(2,1)}, bf16[128,2048]{1,0:T(8,128)(2,1)}) custom-call(s32[1]{0:T(128)} %bitcast.me_ref.refs_0_, bf16[256,256]{1,0:T(8,128)(2,1)S(1)} %get-tuple-element.45.refs_1_, bf16[256,256]{1,0:T(8,128)(2,1)S(1)} %collective-permute-done.7.refs_2_, ...), custom_call_target="tpu_custom_call" | custom-call | flops 1000000000 | bytes 3670020 | tf_op jit(solution)/shard_map/gate/pallas_call | solution.py:307
  58.5 0.0 collective-permute-done.16.fourth
  58.5 0.0 collective-permute-done.15.third
  58.5 0.9 %collective-permute-done.14.second = bf16[200,256]{1,0:T(8,128)(2,1)S(1)} collective-permute-done((bf16[200,256]{1,0:T(8,128)(2,1)S(1)}, bf16[200,256]{1,0:T(8,128)(2,1)S(1)}, u32[]{:S(2)}, u32[]{:S(2)}) %collective-permute-start.14) | collective-permute-done | bytes 102432 | tf_op jit(solution)/shard_map/ppermute | solution.py:348
  59.5 0.7 %finish.1 = (f32[16,1024]{1,0:T(8,128)}, f32[128,256]{1,0:T(8,128)}, f32[1,256]{1,0:T(1,128)}) custom-call(bf16[200,256]{1,0:T(8,128)(2,1)S(1)} %convert_element_type.3.first, bf16[200,256]{1,0:T(8,128)(2,1)S(1)} %collective-permute-done.14.second, bf16[200,256]{1,0:T(8,128)(2,1)S(1)} %collective-permute-done.15.third, ...), custom_call_target="tpu_custom_call" | custom-call | flops 1000000000 | bytes 607232 | tf_op jit(solution)/shard_map/finish/pallas_call | solution.py:307
  (16 shorter events, 0.1 us)
Async XLA Ops:
  0.6 10.9 %copy-start = (bf16[128,2048]{1,0:T(8,128)(2,1)S(1)}, bf16[128,2048]{1,0:T(8,128)(2,1)}, u32[]{:S(2)}) copy-start(bf16[128,2048]{1,0:T(8,128)(2,1)} %param.15) | copy-start | bytes 1572868
  0.6 15.5 %copy-start.5 = (bf16[256,512]{1,0:T(8,128)(2,1)S(1)}, bf16[256,512]{1,0:T(8,128)(2,1)}, u32[]{:S(2)}) copy-start(bf16[256,512]{1,0:T(8,128)(2,1)} %constant.22.clone.inv_high.refs_10_) | copy-start | bytes 786436
  0.7 15.5 %copy-start.6 = (bf16[512,256]{1,0:T(8,128)(2,1)S(1)}, bf16[512,256]{1,0:T(8,128)(2,1)}, u32[]{:S(2)}) copy-start(bf16[512,256]{1,0:T(8,128)(2,1)} %constant.20.clone.fwd_high.refs_9_) | copy-start | bytes 786436
  0.7 15.5 %copy-start.9 = (bf16[16,256]{1,0:T(8,128)(2,1)S(1)}, bf16[16,256]{1,0:T(8,128)(2,1)}, u32[]{:S(2)}) copy-start(bf16[16,256]{1,0:T(8,128)(2,1)} %constant.24.clone.member) | copy-start | bytes 24580
  0.7 15.5 %copy-start.7 = (bf16[256,512]{1,0:T(8,128)(2,1)S(1)}, bf16[256,512]{1,0:T(8,128)(2,1)}, u32[]{:S(2)}) copy-start(bf16[256,512]{1,0:T(8,128)(2,1)} %constant.23.clone.inv_low) | copy-start | bytes 786436
  0.7 15.5 %copy-start.8 = (bf16[512,256]{1,0:T(8,128)(2,1)S(1)}, bf16[512,256]{1,0:T(8,128)(2,1)}, u32[]{:S(2)}) copy-start(bf16[512,256]{1,0:T(8,128)(2,1)} %constant.21.clone.fwd_low) | copy-start | bytes 786436
  0.7 15.5 %copy-start.4 = (f32[256]{0:T(256)S(1)}, f32[256]{0:T(256)}, u32[]{:S(2)}) copy-start(f32[256]{0:T(256)} %param.16) | copy-start | bytes 3076
  0.7 15.5 %copy-start.3 = (f32[16,1024]{1,0:T(8,128)S(1)}, f32[16,1024]{1,0:T(8,128)}, u32[]{:S(2)}) copy-start(f32[16,1024]{1,0:T(8,128)} %long_filter.1) | copy-start | bytes 196612
  3.4 8.1 %collective-permute-start = (bf16[256,256]{1,0:T(8,128)(2,1)}, bf16[256,256]{1,0:T(8,128)(2,1)S(1)}, u32[]{:S(2)}, u32[]{:S(2)}) collective-permute-start(bf16[256,256]{1,0:T(8,128)(2,1)} %get-tuple-element.37), channel_id=1, source_target_pairs={{0,1},{1,2},{2,3},{3,4},{4,5},{5,6},{6,7},{7,0},{8,9},{9,10},{10,1... | collective-permute-start | bytes 393224 | tf_op jit(solution)/shard_map/ppermute | solution.py:327
  3.9 10.0 %collective-permute-start.1 = (bf16[256,256]{1,0:T(8,128)(2,1)}, bf16[256,256]{1,0:T(8,128)(2,1)S(1)}, u32[]{:S(2)}, u32[]{:S(2)}) collective-permute-start(bf16[256,256]{1,0:T(8,128)(2,1)} %get-tuple-element.38), channel_id=1, source_target_pairs={{0,2},{1,3},{2,4},{3,5},{4,6},{5,7},{6,0},{7,1},{8,10},{9,11},{10,... | collective-permute-start | bytes 393224 | tf_op jit(solution)/shard_map/ppermute | solution.py:327
  6.6 16.8 %collective-permute-start.2 = (bf16[256,256]{1,0:T(8,128)(2,1)}, bf16[256,256]{1,0:T(8,128)(2,1)S(1)}, u32[]{:S(2)}, u32[]{:S(2)}) collective-permute-start(bf16[256,256]{1,0:T(8,128)(2,1)} %get-tuple-element.39), channel_id=1, source_target_pairs={{0,3},{1,4},{2,5},{3,6},{4,7},{5,0},{6,1},{7,2},{8,11},{9,12},{10,... | collective-permute-start | bytes 393224 | tf_op jit(solution)/shard_map/ppermute | solution.py:327
  9.1 14.5 %collective-permute-start.3 = (bf16[256,256]{1,0:T(8,128)(2,1)}, bf16[256,256]{1,0:T(8,128)(2,1)S(1)}, u32[]{:S(2)}, u32[]{:S(2)}) collective-permute-start(bf16[256,256]{1,0:T(8,128)(2,1)} %get-tuple-element.40), channel_id=1, source_target_pairs={{0,4},{1,5},{2,6},{3,7},{4,0},{5,1},{6,2},{7,3},{8,12},{9,13},{10,... | collective-permute-start | bytes 393224 | tf_op jit(solution)/shard_map/ppermute | solution.py:327
  10.3 13.2 %collective-permute-start.4 = (bf16[256,256]{1,0:T(8,128)(2,1)}, bf16[256,256]{1,0:T(8,128)(2,1)S(1)}, u32[]{:S(2)}, u32[]{:S(2)}) collective-permute-start(bf16[256,256]{1,0:T(8,128)(2,1)} %get-tuple-element.41), channel_id=1, source_target_pairs={{0,5},{1,6},{2,7},{3,0},{4,1},{5,2},{6,3},{7,4},{8,13},{9,14},{10,... | collective-permute-start | bytes 393224 | tf_op jit(solution)/shard_map/ppermute | solution.py:327
  11.6 12.0 %collective-permute-start.5 = (bf16[256,256]{1,0:T(8,128)(2,1)}, bf16[256,256]{1,0:T(8,128)(2,1)S(1)}, u32[]{:S(2)}, u32[]{:S(2)}) collective-permute-start(bf16[256,256]{1,0:T(8,128)(2,1)} %get-tuple-element.42), channel_id=1, source_target_pairs={{0,6},{1,7},{2,0},{3,1},{4,2},{5,3},{6,4},{7,5},{8,14},{9,15},{10,... | collective-permute-start | bytes 393224 | tf_op jit(solution)/shard_map/ppermute | solution.py:327
  14.0 10.3 %collective-permute-start.6 = (bf16[256,256]{1,0:T(8,128)(2,1)}, bf16[256,256]{1,0:T(8,128)(2,1)S(1)}, u32[]{:S(2)}, u32[]{:S(2)}) collective-permute-start(bf16[256,256]{1,0:T(8,128)(2,1)} %get-tuple-element.43), channel_id=1, source_target_pairs={{0,7},{1,0},{2,1},{3,2},{4,3},{5,4},{6,5},{7,6},{8,15},{9,8},{10,9... | collective-permute-start | bytes 393224 | tf_op jit(solution)/shard_map/ppermute | solution.py:327
  16.2 8.0 %copy-start.10 = (bf16[256,256]{1,0:T(8,128)(2,1)S(1)}, bf16[256,256]{1,0:T(8,128)(2,1)}, u32[]{:S(2)}) copy-start(bf16[256,256]{1,0:T(8,128)(2,1)} %get-tuple-element.36.refs_1_) | copy-start | bytes 393220
  27.9 12.8 %collective-permute-start.7 = (bf16[256,256]{1,0:T(8,128)(2,1)S(1)}, bf16[256,256]{1,0:T(8,128)(2,1)S(1)}, u32[]{:S(2)}, u32[]{:S(2)}) collective-permute-start(bf16[256,256]{1,0:T(8,128)(2,1)S(1)} %get-tuple-element.46), channel_id=1, source_target_pairs={{0,1},{1,2},{2,3},{3,4},{4,5},{5,6},{6,7},{7,0},{8,9},{9,10},{10,1... | collective-permute-start | bytes 393224 | tf_op jit(solution)/shard_map/ppermute | solution.py:327
  29.9 11.0 %collective-permute-start.8 = (bf16[256,256]{1,0:T(8,128)(2,1)S(1)}, bf16[256,256]{1,0:T(8,128)(2,1)S(1)}, u32[]{:S(2)}, u32[]{:S(2)}) collective-permute-start(bf16[256,256]{1,0:T(8,128)(2,1)S(1)} %get-tuple-element.47), channel_id=1, source_target_pairs={{0,7},{1,0},{2,1},{3,2},{4,3},{5,4},{6,5},{7,6},{8,15},{9,8},{10,9... | collective-permute-start | bytes 393224 | tf_op jit(solution)/shard_map/ppermute | solution.py:327
  37.3 10.2 %collective-permute-start.9 = (bf16[256,256]{1,0:T(8,128)(2,1)S(1)}, bf16[256,256]{1,0:T(8,128)(2,1)S(1)}, u32[]{:S(2)}, u32[]{:S(2)}) collective-permute-start(bf16[256,256]{1,0:T(8,128)(2,1)S(1)} %get-tuple-element.50), channel_id=1, source_target_pairs={{0,2},{1,3},{2,4},{3,5},{4,6},{5,7},{6,0},{7,1},{8,10},{9,11},{10,... | collective-permute-start | bytes 393224 | tf_op jit(solution)/shard_map/ppermute | solution.py:327
  37.3 16.0 %collective-permute-start.10 = (bf16[256,256]{1,0:T(8,128)(2,1)S(1)}, bf16[256,256]{1,0:T(8,128)(2,1)S(1)}, u32[]{:S(2)}, u32[]{:S(2)}) collective-permute-start(bf16[256,256]{1,0:T(8,128)(2,1)S(1)} %get-tuple-element.52), channel_id=1, source_target_pairs={{0,3},{1,4},{2,5},{3,6},{4,7},{5,0},{6,1},{7,2},{8,11},{9,12},{10,... | collective-permute-start | bytes 393224 | tf_op jit(solution)/shard_map/ppermute | solution.py:327
  37.3 17.5 %collective-permute-start.11 = (bf16[256,256]{1,0:T(8,128)(2,1)S(1)}, bf16[256,256]{1,0:T(8,128)(2,1)S(1)}, u32[]{:S(2)}, u32[]{:S(2)}) collective-permute-start(bf16[256,256]{1,0:T(8,128)(2,1)S(1)} %get-tuple-element.53), channel_id=1, source_target_pairs={{0,5},{1,6},{2,7},{3,0},{4,1},{5,2},{6,3},{7,4},{8,13},{9,14},{10,... | collective-permute-start | bytes 393224 | tf_op jit(solution)/shard_map/ppermute | solution.py:327
  40.7 16.4 %collective-permute-start.12 = (bf16[256,256]{1,0:T(8,128)(2,1)S(1)}, bf16[256,256]{1,0:T(8,128)(2,1)S(1)}, u32[]{:S(2)}, u32[]{:S(2)}) collective-permute-start(bf16[256,256]{1,0:T(8,128)(2,1)S(1)} %get-tuple-element.54), channel_id=1, source_target_pairs={{0,4},{1,5},{2,6},{3,7},{4,0},{5,1},{6,2},{7,3},{8,12},{9,13},{10,... | collective-permute-start | bytes 393224 | tf_op jit(solution)/shard_map/ppermute | solution.py:327
  40.9 16.1 %collective-permute-start.13 = (bf16[256,256]{1,0:T(8,128)(2,1)S(1)}, bf16[256,256]{1,0:T(8,128)(2,1)S(1)}, u32[]{:S(2)}, u32[]{:S(2)}) collective-permute-start(bf16[256,256]{1,0:T(8,128)(2,1)S(1)} %get-tuple-element.55), channel_id=1, source_target_pairs={{0,6},{1,7},{2,0},{3,1},{4,2},{5,3},{6,4},{7,5},{8,14},{9,15},{10,... | collective-permute-start | bytes 393224 | tf_op jit(solution)/shard_map/ppermute | solution.py:327
  43.9 13.2 %copy-start.1 = (bf16[1,128,2048]{2,1,0:T(8,128)(2,1)S(1)}, bf16[1,128,2048]{2,1,0:T(8,128)(2,1)}, u32[]{:S(2)}) copy-start(bf16[1,128,2048]{2,1,0:T(8,128)(2,1)} %param.12) | copy-start | bytes 1572868
  43.9 13.2 %copy-start.2 = (bf16[1,128,2048]{2,1,0:T(8,128)(2,1)S(1)}, bf16[1,128,2048]{2,1,0:T(8,128)(2,1)}, u32[]{:S(2)}) copy-start(bf16[1,128,2048]{2,1,0:T(8,128)(2,1)} %param.13) | copy-start | bytes 1572868
  47.5 11.0 %collective-permute-start.16 = (bf16[200,256]{1,0:T(8,128)(2,1)S(1)}, bf16[200,256]{1,0:T(8,128)(2,1)S(1)}, u32[]{:S(2)}, u32[]{:S(2)}) collective-permute-start(bf16[200,256]{1,0:T(8,128)(2,1)S(1)} %convert_element_type.3.first), channel_id=1, source_target_pairs={{0,24},{8,16},{16,8},{24,0},{1,25},{9,17},{17,9},{25,1},{2,26},{10... | collective-permute-start | bytes 307208 | tf_op jit(solution)/shard_map/ppermute | solution.py:348
  53.3 5.2 %collective-permute-start.15 = (bf16[200,256]{1,0:T(8,128)(2,1)S(1)}, bf16[200,256]{1,0:T(8,128)(2,1)S(1)}, u32[]{:S(2)}, u32[]{:S(2)}) collective-permute-start(bf16[200,256]{1,0:T(8,128)(2,1)S(1)} %convert_element_type.3.first), channel_id=1, source_target_pairs={{0,16},{8,24},{16,0},{24,8},{1,17},{9,25},{17,1},{25,9},{2,18},{10... | collective-permute-start | bytes 307208 | tf_op jit(solution)/shard_map/ppermute | solution.py:348
  54.8 4.7 %collective-permute-start.14 = (bf16[200,256]{1,0:T(8,128)(2,1)S(1)}, bf16[200,256]{1,0:T(8,128)(2,1)S(1)}, u32[]{:S(2)}, u32[]{:S(2)}) collective-permute-start(bf16[200,256]{1,0:T(8,128)(2,1)S(1)} %convert_element_type.3.first), channel_id=1, source_target_pairs={{0,8},{8,0},{16,24},{24,16},{1,9},{9,1},{17,25},{25,17},{2,10},{10... | collective-permute-start | bytes 307208 | tf_op jit(solution)/shard_map/ppermute | solution.py:348
